TPU v7x, 128 devices: a whole 4x4x4 slice. The times are simulated.
128 devices in a mesh: hst: 4 (over y), chip: 32 (over x, z, core).
Axes of the slice: x: 4, y: 4, z: 4, core: 2. Of those that a mesh axis runs over, the one named last changes fastest.
Arguments:
- resident_row_blocks: bfloat16 [6144, 128, 128], P(('hst', 'chip')), may hold values from -3 to 3
- orphan_blocks: bfloat16 [4096, 128, 128], P(('hst', 'chip')), may hold values from -3 to 3
- home_offsets: int32 [6144, 128, 8], P(('hst', 'chip')), may hold values from 0 to 127
- home_lengths: int32 [6144, 128], P(('hst', 'chip')), may hold values from 1 to 8
- home_samples: int32 [6144, 128], P(('hst', 'chip')), may hold values from 0 to 511
- orphan_offsets: int32 [4096, 128, 8], P(('hst', 'chip')), may hold values from 0 to 127
- orphan_lengths: int32 [4096, 128], P(('hst', 'chip')), may hold values from 1 to 8
- orphan_samples: int32 [4096, 128], P(('hst', 'chip')), may hold values from 0 to 511
- orphan_owner: int32 [4096, 1], P(('hst', 'chip')), may hold values from 0 to 31; in each aligned block of 32 rows (0 to 31, 32 to 63, ...) at most 2 rows name the same one
- dense_inputs: bfloat16 [65536, 13], P(('hst', 'chip')), may hold values from -6 to 6
- labels: int32 [65536], P(('hst', 'chip')), may hold values 0 or 1
- bottom_first: bfloat16 [13, 512], replicated, may hold values from -1.75 to 1.75
- bias_first: float32 [512], replicated, may hold values from -1.5 to 1.5
- bottom_second: bfloat16 [512, 256], replicated, may hold values from -0.375 to 0.375
- bias_second: float32 [256], replicated, may hold values from -1.5 to 1.5
- bottom_third: bfloat16 [256, 128], replicated, may hold values from -0.5 to 0.5
- bias_third: float32 [128], replicated, may hold values from -1.5 to 1.5
- top_hidden: bfloat16 [479, 1024], replicated, may hold values from -0.125 to 0.125
- bias_hidden: float32 [1024], replicated, may hold values from -1.5 to 1.5
- top_logit: bfloat16 [1024, 1], replicated, may hold values from -0.25 to 0.25
- bias_logit: float32 [1], replicated, may hold values from -3 to 3
Outputs:
- rehomed: bfloat16 [8192, 128, 128], P(('hst', 'chip'))
- logits: float32 [65536], P(('hst', 'chip'))
- loss: float32 [], replicated
Inputs may be any that keep to these rules, and one draw needn't show every extreme that they name: `orphan_owner`: among the 32 orphans of one device at most 2 have the same new owner; some holder and owner reach 2.
All inputs are finite; a program needn't handle non-finite values. No bound on the sum of `labels` on one device may be relied on, other than what follows from the above.
Results may differ from a plain program's by a relative error of at most 0.0079.
Values may be sent and summed in bfloat16 or wider, within the bound.
No kernel may reach another device: no remote copies, remote signals or barrier semaphores. Data moves between devices by JAX's collectives and lax.ppermute only.
A program may use at most 128 MiB of HBM per device.

v0:
```python
import functools

import jax
import jax.numpy as jnp
import numpy as np
from jax import lax
from jax.sharding import Mesh
from jax.sharding import PartitionSpec as P

F = 26
CHIP = ("chip_0", "chip_1", "chip_2")
HST_CHIP = ("hst", "chip_0", "chip_1", "chip_2")


def over_axes(value, axes):
    return functools.reduce(lax.psum, axes, value)


def pool_blocks(blocks, offsets, lengths):
    rows = jnp.arange(blocks.shape[1], dtype=jnp.int32)
    counts = jnp.zeros((blocks.shape[0], offsets.shape[1], blocks.shape[1]), jnp.float32)
    for place in range(offsets.shape[2]):
        hit = (offsets[:, :, place, None] == rows[None, None, :]) & (place < lengths)[:, :, None]
        counts = counts + hit.astype(jnp.float32)
    return jnp.einsum(
        "bqr,bre->bqe", counts.astype(jnp.bfloat16), blocks, preferred_element_type=jnp.float32
    ).astype(jnp.bfloat16)


def per_device(
    resident_row_blocks,
    orphan_blocks,
    home_offsets,
    home_lengths,
    home_samples,
    orphan_offsets,
    orphan_lengths,
    orphan_samples,
    orphan_owner,
    dense_inputs,
    labels,
    bottom_first,
    bias_first,
    bottom_second,
    bias_second,
    bottom_third,
    bias_third,
    top_hidden,
    bias_hidden,
    top_logit,
    bias_logit,
):
    hosts = lax.axis_size("hst")
    chips = lax.axis_size(CHIP)
    devices = hosts * chips
    mine = lax.axis_index(HST_CHIP)
    home_count = resident_row_blocks.shape[0]
    stranded_block_count = orphan_blocks.shape[0]
    batch_rows = dense_inputs.shape[0]
    width = resident_row_blocks.shape[2]
    slots = (2 * stranded_block_count + chips - 1) // chips
    receive = chips * slots
    owners = orphan_owner[:, 0]
    index = jnp.arange(stranded_block_count, dtype=jnp.int32)
    earlier = index[None, :] < index[:, None]
    rank = jnp.sum(((owners[:, None] == owners[None, :]) & earlier).astype(jnp.int32), axis=1)
    flat = owners * slots + rank
    match = flat[None, :] == jnp.arange(receive, dtype=jnp.int32)[:, None]
    source = jnp.sum(match.astype(jnp.int32) * index[None, :], axis=1)
    filled = jnp.any(match, axis=1)
    outgoing = jnp.where(filled[:, None, None], orphan_blocks[source], jnp.zeros((), jnp.bfloat16))
    rehomed = lax.all_to_all(outgoing, CHIP, split_axis=0, concat_axis=0, tiled=True)
    home_ids = mine * home_count + jnp.arange(home_count, dtype=jnp.int32)
    orphan_ids = devices * home_count + mine * stranded_block_count + index
    blocks = jnp.concatenate([resident_row_blocks, orphan_blocks], axis=0)
    offsets = jnp.concatenate([home_offsets, orphan_offsets], axis=0)
    lengths = jnp.concatenate([home_lengths, orphan_lengths], axis=0)
    samples = jnp.concatenate([home_samples, orphan_samples], axis=0)
    block_ids = jnp.concatenate([home_ids, orphan_ids], axis=0)
    first = jax.nn.relu(
        jnp.dot(dense_inputs, bottom_first, preferred_element_type=jnp.float32) + bias_first
    ).astype(jnp.bfloat16)
    second = jax.nn.relu(
        jnp.dot(first, bottom_second, preferred_element_type=jnp.float32) + bias_second
    ).astype(jnp.bfloat16)
    bottom = jax.nn.relu(
        jnp.dot(second, bottom_third, preferred_element_type=jnp.float32) + bias_third
    )
    piece = pool_blocks(blocks, offsets, lengths)
    targets = samples * F + (block_ids % F)[:, None]
    arrived_pieces = lax.all_to_all(piece, HST_CHIP, split_axis=1, concat_axis=0, tiled=True)
    arrived_targets = lax.all_to_all(targets, HST_CHIP, split_axis=1, concat_axis=0, tiled=True)
    pooled = jax.ops.segment_sum(
        arrived_pieces.reshape(-1, width).astype(jnp.float32),
        arrived_targets.reshape(-1),
        num_segments=batch_rows * F,
    )
    pooled = pooled.reshape(batch_rows, F, width)
    stacked_vectors = jnp.concatenate([bottom[:, None, :], pooled], axis=1).astype(jnp.bfloat16)
    pairwise_products = jnp.einsum(
        "asu,adu->asd", stacked_vectors, stacked_vectors, preferred_element_type=jnp.float32
    )
    lower_i, lower_j = np.tril_indices(F + 1, -1)
    pairs = pairwise_products[:, lower_i, lower_j]
    feature_vectors = jnp.concatenate([bottom, pairs], axis=1).astype(jnp.bfloat16)
    hidden = jax.nn.relu(
        jnp.dot(feature_vectors, top_hidden, preferred_element_type=jnp.float32) + bias_hidden
    ).astype(jnp.bfloat16)
    logits = jnp.dot(hidden, top_logit, preferred_element_type=jnp.float32)[:, 0] + bias_logit[0]
    local_loss = jnp.sum(jax.nn.softplus(logits) - labels.astype(jnp.float32) * logits)
    loss = over_axes(local_loss, HST_CHIP)
    return (rehomed, logits, loss)


def solution(mesh):
    finer = Mesh(
        mesh.devices.reshape(mesh.shape["hst"], 4, 4, 2), ("hst", "chip_0", "chip_1", "chip_2")
    )
    placed = (
        P(HST_CHIP, None, None),
        P(HST_CHIP, None, None),
        P(HST_CHIP, None, None),
        P(HST_CHIP, None),
        P(HST_CHIP, None),
        P(HST_CHIP, None, None),
        P(HST_CHIP, None),
        P(HST_CHIP, None),
        P(HST_CHIP, None),
        P(HST_CHIP, None),
        P(HST_CHIP),
        P(),
        P(),
        P(),
        P(),
        P(),
        P(),
        P(),
        P(),
        P(),
        P(),
    )
    return jax.shard_map(
        per_device,
        mesh=finer,
        in_specs=placed,
        out_specs=(P(HST_CHIP, None, None), P(HST_CHIP), P()),
        check_vma=False,
    )
```

profile of v0, /device:TPU:0, one launch (start us, length us, event | category | flops | bytes accessed | tf_op | source)
XLA Modules:
  0.0 238.0 jit_solution(8213412658634780871)
XLA Ops:
  3.3 11.1 %all-to-all-start.1 = ((s32[80,128,1]{0,2,1:T(1,128)}), s32[80,128,1]{0,2,1:T(1,128)S(1)}, u32[]{:S(2)}, u32[]{:S(2)}) async-start(s32[80,128,1]{0,2,1:T(1,128)} %fusion.56), calls=%async_computation.1 | async-start | bytes 131072 | tf_op jit(solution)/shard_map/all_to_all | solution.py:92
  14.5 0.9 constant_dynamic-update-slice_fusion.1
  15.4 0.9 constant_dynamic-update-slice_fusion
  18.1 30.5 %fusion.34 = bf16[80,128,128]{2,1,0:T(8,128)(2,1)S(1)} fusion(bf16[32,128,128]{2,1,0:T(8,128)(2,1)} %param.26, bf16[48,128,128]{2,1,0:T(8,128)(2,1)} %param.25, s32[80,128]{1,0:T(8,128)S(1)} %bitcast.44, s32[80,128]{1,0:T(8,128)S(1)} %bitcast.45, s32[80,128]{1,0:T(8,128)S(1)} %bitcast.46, s32[80,128]{1,0:T(8,128)S(1)} %bitcast.47, ...), kind=kOutput, calls=%fused_computation.49 | convolution fusion | flops 380108800 | bytes 5652480 | tf_op jit(solution)/shard_map/bqr,bre->bqe/dot_general | solution.py:25
  48.6 3.2 %copy.39 = bf16[80,128,128]{2,0,1:T(8,128)(2,1)} copy(bf16[80,128,128]{2,1,0:T(8,128)(2,1)S(1)} %fusion.34) | data formatting | bytes 5242880 | tf_op jit(solution)/shard_map/convert_element_type | solution.py:27
  51.8 10.2 %all-to-all-start.2 = ((bf16[80,128,128]{2,0,1:T(8,128)(2,1)}), bf16[80,128,128]{2,0,1:T(8,128)(2,1)}, u32[]{:S(2)}, u32[]{:S(2)}) async-start(bf16[80,128,128]{2,0,1:T(8,128)(2,1)} %copy.39), calls=%async_computation.2 | async-start | bytes 5242880 | tf_op jit(solution)/shard_map/all_to_all | solution.py:91
  62.4 2.2 gather_fusion
  64.8 1.5 broadcast_select_fusion
  66.3 31.4 %all-to-all-done.2 = bf16[80,128,128]{2,0,1:T(8,128)(2,1)} async-done(((bf16[80,128,128]{2,0,1:T(8,128)(2,1)}), bf16[80,128,128]{2,0,1:T(8,128)(2,1)}, u32[]{:S(2)}, u32[]{:S(2)}) %all-to-all-start.2) | async-done | bytes 2621472 | tf_op jit(solution)/shard_map/all_to_all | solution.py:91
  97.7 4.8 %all-to-all-start = ((bf16[64,128,128]{2,1,0:T(8,128)(2,1)}), bf16[64,128,128]{2,1,0:T(8,128)(2,1)}, u32[]{:S(2)}, u32[]{:S(2)}) async-start(bf16[64,128,128]{2,1,0:T(8,128)(2,1)} %broadcast_select_fusion), calls=%async_computation | async-start | bytes 4194304 | tf_op jit(solution)/shard_map/all_to_all | solution.py:72
  104.4 4.5 %bitcast_convert_fusion = f32[80,128,1,128]{3,0,1,2:T(8,128)} fusion(bf16[80,128,128]{2,0,1:T(8,128)(2,1)} %all-to-all-done.2), kind=kLoop, calls=%fused_computation.30 | loop fusion | flops 1310720 | bytes 7864320 | tf_op jit(solution)/shard_map/convert_element_type | solution.py:94
  108.9 58.3 %scatter_custom_fusion = f32[13312,128]{1,0:T(8,128)} fusion(s32[10240]{0:T(1024)S(1)} %reshape.262, f32[10240,128]{1,0:T(8,128)} %bitcast.38, f32[]{:T(128)} %constant.28.clone.1), kind=kCustom, calls=%fused_computation.24 | custom fusion | flops 1310720 | bytes 6816256 | tf_op jit(solution)/shard_map/scatter-add | solution.py:93
  167.2 4.4 %convert.16 = bf16[13312,128]{1,0:T(8,128)(2,1)} convert(f32[13312,128]{1,0:T(8,128)} %scatter_custom_fusion) | non-fusion elementwise | flops 1703936 | bytes 10223616 | tf_op jit(solution)/shard_map/convert.7
  171.6 6.4 %reshape.242 = bf16[512,26,128]{2,1,0:T(8,128)(2,1)} reshape(bf16[13312,128]{1,0:T(8,128)(2,1)} %convert.16) | data formatting | bytes 6815744 | tf_op jit(solution)/shard_map/reshape | solution.py:98
  178.1 8.1 %fusion.8 = bf16[512,27,27]{2,1,0:T(8,128)(2,1)} fusion(bf16[512,26,128]{2,1,0:T(8,128)(2,1)} %reshape.242, bf16[512,1,128]{2,1,0:T(2,128)(2,1)S(1)} %copy.40), kind=kOutput, calls=%fused_computation.20 | convolution fusion | flops 102629376 | bytes 4285440 | tf_op jit(solution)/shard_map/asu,adu->asd/dot_general | solution.py:100
  186.2 6.0 %copy.41 = bf16[512,27,27]{0,2,1:T(8,128)(2,1)S(1)} copy(bf16[512,27,27]{2,1,0:T(8,128)(2,1)} %fusion.8) | data formatting | bytes 1492992 | tf_op jit(solution)/shard_map/asu,adu->asd/dot_general | solution.py:100
  192.2 5.5 %gather_fusion.1 = bf16[351,512]{1,0:T(8,128)(2,1)S(1)} fusion(bf16[512,27,27]{0,2,1:T(8,128)(2,1)S(1)} %copy.41, s32[351]{0:T(512)S(1)} %copy-done.1), kind=kCustom, calls=%fused_computation.1 | custom fusion | bytes 721656 | tf_op jit(solution)/shard_map/gather | solution.py:104
  197.7 0.9 fusion.37
  198.7 1.3 fusion.60
  199.9 9.4 %psum.28 = f32[]{:T(128)} all-reduce(f32[]{:T(128)} %get-tuple-element.3), channel_id=1, replica_groups=mesh['hst'=4,'chip_0'=4,'chip_1'=4,'chip_2'=2] {'hst'}, use_global_device_ids=true, to_apply=%region_5.6 | all-reduce | flops 1 | bytes 8 | tf_op jit(solution)/shard_map/psum | solution.py:16
  209.4 11.3 %psum.29 = f32[]{:T(128)} all-reduce(f32[]{:T(128)} %psum.28), channel_id=1, replica_groups=mesh['hst'=4,'chip_0'=4,'chip_1'=4,'chip_2'=2] {'chip_0'}, use_global_device_ids=true, to_apply=%region_6.7 | all-reduce | flops 1 | bytes 8 | tf_op jit(solution)/shard_map/psum | solution.py:16
  220.7 11.0 %psum.30 = f32[]{:T(128)} all-reduce(f32[]{:T(128)} %psum.29), channel_id=1, replica_groups=mesh['hst'=4,'chip_0'=4,'chip_1'=4,'chip_2'=2] {'chip_1'}, use_global_device_ids=true, to_apply=%region_7.8 | all-reduce | flops 1 | bytes 8 | tf_op jit(solution)/shard_map/psum | solution.py:16
  231.7 3.1 %psum.31 = f32[]{:T(128)} all-reduce(f32[]{:T(128)} %psum.30), channel_id=1, replica_groups=mesh['hst'=4,'chip_0'=4,'chip_1'=4,'chip_2'=2] {'chip_2'}, use_global_device_ids=true, to_apply=%region_8.9 | all-reduce | flops 1 | bytes 8 | tf_op jit(solution)/shard_map/psum | solution.py:16
  234.8 3.2 %copy.46 = bf16[64,128,128]{2,1,0:T(8,128)(2,1)} copy(bf16[64,128,128]{2,1,0:T(8,128)(2,1)} %all-to-all-done) | data formatting | bytes 4194304
  (49 shorter events, 6.0 us)
Async XLA Ops:
  0.6 197.1 %copy-start = (bf16[479,1024]{1,0:T(8,128)(2,1)S(1)}, bf16[479,1024]{1,0:T(8,128)(2,1)}, u32[]{:S(2)}) copy-start(bf16[479,1024]{1,0:T(8,128)(2,1)} %param.42) | copy-start | bytes 2942980
  3.3 48.5 %all-to-all-start.1 = ((s32[80,128,1]{0,2,1:T(1,128)}), s32[80,128,1]{0,2,1:T(1,128)S(1)}, u32[]{:S(2)}, u32[]{:S(2)}) async-start(s32[80,128,1]{0,2,1:T(1,128)} %fusion.56), calls=%async_computation.1 | async-start | bytes 131072 | tf_op jit(solution)/shard_map/all_to_all | solution.py:92
  48.6 13.5 %copy-start.12 = (s32[32,1]{0,1:T(1,128)S(1)}, s32[32,1]{0,1:T(1,128)}, u32[]{:S(2)}) copy-start(s32[32,1]{0,1:T(1,128)} %param.33) | copy-start | bytes 388
  51.8 45.9 %all-to-all-start.2 = ((bf16[80,128,128]{2,0,1:T(8,128)(2,1)}), bf16[80,128,128]{2,0,1:T(8,128)(2,1)}, u32[]{:S(2)}, u32[]{:S(2)}) async-start(bf16[80,128,128]{2,0,1:T(8,128)(2,1)} %copy.39), calls=%async_computation.2 | async-start | bytes 5242880 | tf_op jit(solution)/shard_map/all_to_all | solution.py:91
  64.7 37.8 %copy-start.5 = (bf16[512,256]{1,0:T(8,128)(2,1)S(1)}, bf16[512,256]{1,0:T(8,128)(2,1)}, u32[]{:S(2)}) copy-start(bf16[512,256]{1,0:T(8,128)(2,1)} %param.38) | copy-start | bytes 786436
  64.7 37.8 %copy-start.6 = (bf16[512,13]{0,1:T(8,128)(2,1)S(1)}, bf16[512,13]{0,1:T(8,128)(2,1)}, u32[]{:S(2)}) copy-start(bf16[512,13]{0,1:T(8,128)(2,1)} %param.34) | copy-start | bytes 39940
  64.7 37.8 %copy-start.7 = (bf16[13,512]{1,0:T(8,128)(2,1)S(1)}, bf16[13,512]{1,0:T(8,128)(2,1)}, u32[]{:S(2)}) copy-start(bf16[13,512]{1,0:T(8,128)(2,1)} %param.36) | copy-start | bytes 39940
  64.7 37.8 %copy-start.10 = (f32[512]{0:T(512)S(1)}, f32[512]{0:T(512)}, u32[]{:S(2)}) copy-start(f32[512]{0:T(512)} %param.37) | copy-start | bytes 6148
  64.7 37.8 %copy-start.11 = (f32[256]{0:T(256)S(1)}, f32[256]{0:T(256)}, u32[]{:S(2)}) copy-start(f32[256]{0:T(256)} %param.39) | copy-start | bytes 3076
  64.7 38.3 %copy-start.2 = (bf16[256,128]{1,0:T(8,128)(2,1)S(1)}, bf16[256,128]{1,0:T(8,128)(2,1)}, u32[]{:S(2)}) copy-start(bf16[256,128]{1,0:T(8,128)(2,1)} %param.40) | copy-start | bytes 196612
  64.7 38.3 %copy-start.4 = (f32[128]{0:T(128)S(1)}, f32[128]{0:T(128)}, u32[]{:S(2)}) copy-start(f32[128]{0:T(128)} %param.41) | copy-start | bytes 1540
  97.7 134.0 %all-to-all-start = ((bf16[64,128,128]{2,1,0:T(8,128)(2,1)}), bf16[64,128,128]{2,1,0:T(8,128)(2,1)}, u32[]{:S(2)}, u32[]{:S(2)}) async-start(bf16[64,128,128]{2,1,0:T(8,128)(2,1)} %broadcast_select_fusion), calls=%async_computation | async-start | bytes 4194304 | tf_op jit(solution)/shard_map/all_to_all | solution.py:72
  186.2 6.0 %copy-start.1 = (s32[351]{0:T(512)S(1)}, s32[351]{0:T(512)}, u32[]{:S(2)}) copy-start(s32[351]{0:T(512)} %constant.117) | copy-start | bytes 4216
  186.2 11.5 %copy-start.8 = (bf16[1024,1]{0,1:T(2,128)(2,1)S(1)}, bf16[1024,1]{0,1:T(2,128)(2,1)}, u32[]{:S(2)}) copy-start(bf16[1024,1]{0,1:T(2,128)(2,1)} %param.44) | copy-start | bytes 6148
  186.2 11.5 %copy-start.9 = (f32[1024]{0:T(1024)S(1)}, f32[1024]{0:T(1024)}, u32[]{:S(2)}) copy-start(f32[1024]{0:T(1024)} %param.43) | copy-start | bytes 12292
  192.2 6.4 %copy-start.3 = (s32[512]{0:T(512)S(1)}, s32[512]{0:T(512)}, u32[]{:S(2)}) copy-start(s32[512]{0:T(512)} %param.35) | copy-start | bytes 6148
where the time goes:
time: 240 us; the launch traced here: 238 us
  other arithmetic  71.4 us (30%)
  matrix products  40.3 us (17%)
  blocking collectives  34.9 us (15%)
  local copies, waits for them, and re-layouts  32.2 us (13%)
  waiting for transfers between devices  31.5 us (13%)
  starting transfers between devices  26.1 us (11%)
    scatter-add x1, other arithmetic, per_device(): jax.ops.segment_sum(arrived_pieces.reshape(-1, width).astype(jnp.float32)...  58.3 us
    psum x4, blocking collectives, over_axes(): return functools.reduce(lax.psum, axes, value)  34.9 us
    all_to_all x1, waiting for transfers between devices, per_device(): lax.all_to_all(piece, HST_CHIP, split_axis=1, concat_axis=0, tiled=True)  31.4 us
    dot_general x1, matrix products, pool_blocks(): jnp.einsum('bqr,bre->bqe', counts.astype(jnp.bfloat16), blocks, preferred...  30.5 us
    all_to_all x1, starting transfers between devices, per_device(): lax.all_to_all(targets, HST_CHIP, split_axis=1, concat_axis=0, tiled=True)  11.1 us
    all_to_all x1, starting transfers between devices, per_device(): lax.all_to_all(piece, HST_CHIP, split_axis=1, concat_axis=0, tiled=True)  10.2 us
    dot_general x1, matrix products, per_device(): jnp.einsum('asu,adu->asd', stacked_vectors, stacked_vectors, preferred_el...  8.15 us
    unnamed x31, local copies, waits for them, and re-layouts  6.64 us
  transfers between devices with their start and end apart: 3, of which 1 were waited for; matrix products, arithmetic and copies ran while one was open for 58% of the time, Pallas kernels for 0%

commit v1 on v0

v1 whole, which is shorter than its diff:
```python
import functools

import jax
import jax.numpy as jnp
import numpy as np
from jax import lax
from jax.experimental import pallas as pl
from jax.experimental.pallas import tpu as pltpu
from jax.sharding import PartitionSpec as P

ALL = ("hst", "chip")
PERIOD = 13
HOME, ORPHAN = 48, 32
FIXED = 6
SLOTS = 84
ROWS = 88
F = 26
BATCH = 512
NONE = 1023
QW = 896
BF, F32 = jnp.bfloat16, jnp.float32
VMEM = pl.BlockSpec(memory_space=pltpu.VMEM)
SMEM = pl.BlockSpec(memory_space=pltpu.SMEM)


def slot_tables():
    table = np.full((PERIOD, 128), -1, np.int32)
    label = np.full((PERIOD, 3), -1, np.int32)
    for r in range(PERIOD):
        for g in range(PERIOD):
            k = (g - 11 * r) % PERIOD
            o = (g - 4 - 3 * r) % PERIOD
            for e in range(2):
                table[r, FIXED * g + e] = 2 * k + e
                if k + PERIOD < HOME // 2:
                    table[r, FIXED * g + 2 + e] = 2 * (k + PERIOD) + e
                table[r, FIXED * g + 4 + e] = 2 * o + e
        rest = [(PERIOD + i, (4 + 3 * r + i) % PERIOD) for i in range(3)]
        free = [0, 1, 2]
        for k, g in sorted(rest, key=lambda item: item[1] == 0):
            at = g % 3 if g % 3 in free else free[0]
            free.remove(at)
            label[r, at] = g
            for e in range(2):
                table[r, PERIOD * FIXED + 2 * at + e] = 2 * k + e
    for g in range(1, PERIOD):
        assert all(at == g % 3 for r in range(PERIOD) for at in range(3) if label[r, at] == g)
    return table, label


def feature_rows():
    rows = np.full((QW,), 479, np.int32)
    rows[:128] = np.arange(128)
    at = 128
    for a in range(4):
        for tile in range(1 if a < 2 else 2):
            for lane in range(128):
                turn = (lane - 7) % 128
                i, j = 8 * a + turn % 8, 16 * tile + turn // 8
                if j < i <= F:
                    rows[at + lane] = 128 + i * (i - 1) // 2 + j
            at += 128
    return rows


TABLE, LABEL = slot_tables()
FEATURE_ROWS = feature_rows()


def route_kernel(owner, orphans, out, count):
    slots = out.shape[0] // count.shape[0]

    def clear(c, _):
        count[c] = 0
        return 0

    lax.fori_loop(0, count.shape[0], clear, 0)
    out[...] = jnp.zeros_like(out)

    def place(i, _):
        o = owner[i]
        n = count[o]
        out[slots * o + n] = orphans[i]
        count[o] = n + 1
        return 0

    lax.fori_loop(0, orphans.shape[0], place, 0)


def route(orphan_owner, orphans, chips):
    return pl.pallas_call(
        route_kernel,
        out_shape=jax.ShapeDtypeStruct((2 * chips,) + orphans.shape[1:], BF),
        in_specs=[SMEM, VMEM],
        out_specs=VMEM,
        scratch_shapes=[pltpu.SMEM((chips,), jnp.int32)],
        compiler_params=pltpu.CompilerParams(vmem_limit_bytes=16 << 20),
        cost_estimate=pl.CostEstimate(flops=0, transcendentals=0, bytes_accessed=3 << 20),
    )(orphan_owner, orphans)


def pool_kernel(tab, home, orphan, home_off, home_len, home_sam, orphan_off, orphan_len, orphan_sam, out, wide, sam):
    rows = lax.broadcasted_iota(jnp.int32, (128, 128), 0).astype(F32).astype(BF)
    place = lax.broadcasted_iota(jnp.int32, (8, 128), 0)
    one, zero = jnp.ones((), BF), jnp.zeros((), BF)
    sam[...] = jnp.zeros_like(sam)

    def piece(slot, blocks, off, length, samples):
        at = tab[slot]
        b = jnp.maximum(at, 0)
        live = jnp.where(place < length[pl.ds(b, 1), :], off[b], -1).astype(F32).astype(BF)
        counts = jnp.zeros((128, 128), BF)
        for n in range(8):
            counts = counts + jnp.where(rows == live[n : n + 1, :], one, zero)
        sums = lax.dot_general(counts, blocks[b], (((0,), (0,)), ((), ())), preferred_element_type=F32)
        wide[pl.ds(slot, 128, stride=ROWS), :] = sums
        sam[pl.ds(slot, 1), :] = jnp.where(at >= 0, samples[pl.ds(b, 1), :], NONE)

    def group(g, _):
        for e in range(4):
            piece(FIXED * g + e, home, home_off, home_len, home_sam)
        for e in range(4, 6):
            piece(FIXED * g + e, orphan, orphan_off, orphan_len, orphan_sam)
        return 0

    lax.fori_loop(0, PERIOD, group, 0)

    def last(s, _):
        piece(PERIOD * FIXED + s, orphan, orphan_off, orphan_len, orphan_sam)
        return 0

    lax.fori_loop(0, 6, last, 0)
    index = sam[...]
    wide[pl.ds(SLOTS, 128, stride=ROWS), :] = (index >> 4).astype(F32).T
    wide[pl.ds(SLOTS + 1, 128, stride=ROWS), :] = (index & 15).astype(F32).T
    for s in range(SLOTS + 2, ROWS):
        wide[pl.ds(s, 128, stride=ROWS), :] = jnp.zeros((128, 128), F32)

    def narrow(q, _):
        out[pl.ds(4 * q, 4)] = wide[pl.ds(4 * q * ROWS, 4 * ROWS), :].reshape(4, ROWS, 128).astype(BF)
        return 0

    lax.fori_loop(0, 32, narrow, 0)


def pool(tab, *arrays):
    return pl.pallas_call(
        pool_kernel,
        out_shape=jax.ShapeDtypeStruct((128, ROWS, 128), BF),
        in_specs=[SMEM] + [VMEM] * 8,
        out_specs=VMEM,
        scratch_shapes=[pltpu.VMEM((128 * ROWS, 128), F32), pltpu.VMEM((128, 128), jnp.int32)],
        compiler_params=pltpu.CompilerParams(vmem_limit_bytes=24 << 20),
        cost_estimate=pl.CostEstimate(flops=84 * 128 * 128 * 256, transcendentals=0, bytes_accessed=6 << 20),
    )(tab, *arrays)


def tail_kernel(label, recv, bottom, weights, bias, last, last_bias, marks, logits, loss, wide, hi, lo, stack, turned, packed):
    zero = jnp.zeros((), BF)
    ones = lax.broadcasted_iota(jnp.int32, (16, 128), 0).astype(F32).astype(BF)

    def widen(p, _):
        wide[pl.ds(4 * p * ROWS, 4 * ROWS), :] = recv[pl.ds(4 * p, 4)].astype(F32).reshape(4 * ROWS, 128)
        return 0

    lax.fori_loop(0, 32, widen, 0)
    hi[...] = wide[pl.ds(SLOTS, 128, stride=ROWS), :].T
    lo[...] = wide[pl.ds(SLOTS + 1, 128, stride=ROWS), :].T

    def put(f, value):
        stack[f] = value
        for k in range(8):
            turned[pl.ds(f * BATCH + k, BATCH // 8, stride=8), :] = stack[f, pl.ds(7 - k, BATCH // 8, stride=8), :]

    put(0, bottom[...].astype(BF).astype(F32))
    turned[(F + 1) * BATCH :, :] = jnp.zeros(((31 - F) * BATCH, 128), F32)

    def hits(slot, keep=None):
        high = hi[pl.ds(slot, 1), :]
        if keep is not None:
            high = jnp.where(keep, high, 63.0)
        high = jnp.broadcast_to(high, (16, 128)).astype(BF)
        low = jnp.broadcast_to(lo[pl.ds(slot, 1), :], (16, 128)).astype(BF)
        low = jnp.where(low == ones, jnp.ones((), BF), zero)
        return jnp.concatenate([jnp.where(high == jnp.asarray(h, BF), low, zero) for h in range(32)], axis=0)

    def rows(slot):
        return wide[pl.ds(slot, 128, stride=ROWS), :].astype(BF)

    def pooled(g, places):
        for e in range(2):
            slots = [(FIXED * g + 2 * n + e, None) for n in range(3)]
            for at in places:
                keep = label[pl.ds(at, 1), :] == jnp.asarray(g, jnp.int32)
                slots.append((PERIOD * FIXED + 2 * at + e, keep))
            left = jnp.concatenate([hits(s, keep) for s, keep in slots], axis=1)
            right = jnp.concatenate([rows(s) for s, _ in slots], axis=0)
            total = jnp.dot(left, right, preferred_element_type=F32)
            put(1 + 2 * g + e, total.astype(BF).astype(F32))

    pooled(0, [0, 1, 2])

    def group(g, _):
        pooled(g, [lax.rem(g, 3)])
        return 0

    lax.fori_loop(1, PERIOD, group, 0)

    packed[:, :128] = bottom[...].astype(BF)
    own = lax.broadcasted_iota(jnp.int32, (8, 128), 1) % 8 == 7 - lax.broadcasted_iota(jnp.int32, (8, 128), 0)

    def interact(m, _):
        halves = []
        for half in range(2):
            left = stack[:, pl.ds(16 * m + 8 * half, 8), :].reshape(8 * (F + 1), 128).astype(BF)
            right = [turned[pl.ds(j * BATCH + 16 * m + 8 * half, 8), :] for j in range(32)]
            right = jnp.concatenate(right, axis=0).astype(BF)
            gram = lax.dot_general(left, right, (((1,), (1,)), ((), ())), preferred_element_type=F32)
            columns = []
            for a in range(4):
                for tile in range(1 if a < 2 else 2):
                    total = None
                    for c in range(8):
                        i = 8 * a + c
                        if i > F or 16 * tile >= i:
                            continue
                        part = jnp.where(own, gram[8 * i : 8 * i + 8, 128 * tile : 128 * tile + 128], 0.0)
                        part = pltpu.roll(part, c, 1, stride=1, stride_axis=0)
                        total = part if total is None else total + part
                    columns.append(total)
            halves.append(jnp.concatenate(columns, axis=1))
        packed[pl.ds(pl.multiple_of(16 * m, 16), 16), 128:] = jnp.concatenate(halves, axis=0).astype(BF)
        return 0

    lax.fori_loop(0, BATCH // 16, interact, 0)

    for m in range(4):
        at = pl.ds(128 * m, 128)
        hidden = jnp.dot(packed[at, :], weights[...], preferred_element_type=F32)
        hidden = jnp.maximum(hidden + bias[...], 0.0).astype(BF)
        out = lax.dot_general(last[...], hidden, (((1,), (1,)), ((), ())), preferred_element_type=F32)
        logits[:, at] = out[:1] + last_bias[0]
    x = logits[...]
    soft = jnp.maximum(x, 0.0) + jnp.log1p(jnp.exp(-jnp.abs(x)))
    term = jnp.sum(soft - marks[...].astype(F32) * x)
    loss[...] = jnp.full(loss.shape, term, F32)


def tail(label, recv, bottom, weights, bias, last, last_bias, marks):
    return pl.pallas_call(
        tail_kernel,
        out_shape=(jax.ShapeDtypeStruct((1, BATCH), F32), jax.ShapeDtypeStruct((128, 1, 128), F32)),
        in_specs=[VMEM] * 6 + [SMEM, VMEM],
        out_specs=(VMEM, VMEM),
        scratch_shapes=[
            pltpu.VMEM((128 * ROWS, 128), F32),
            pltpu.VMEM((128, 128), F32),
            pltpu.VMEM((128, 128), F32),
            pltpu.VMEM((F + 1, BATCH, 128), F32),
            pltpu.VMEM((32 * BATCH, 128), F32),
            pltpu.VMEM((BATCH, QW), BF),
        ],
        compiler_params=pltpu.CompilerParams(vmem_limit_bytes=40 << 20),
        cost_estimate=pl.CostEstimate(flops=6 << 30, transcendentals=0, bytes_accessed=5 << 20),
    )(label, recv, bottom, weights, bias, last, last_bias, marks)


def labels_by_holder():
    label = np.full((8, 128), -1, np.int32)
    label[:3] = LABEL[np.arange(128) % PERIOD].T
    return label


def exchange(value, axes):
    return lax.all_to_all(value, axes, split_axis=0, concat_axis=0, tiled=True)


def per_device(
    resident_row_blocks,
    orphan_blocks,
    home_offsets,
    home_lengths,
    home_samples,
    orphan_offsets,
    orphan_lengths,
    orphan_samples,
    orphan_owner,
    dense_inputs,
    labels,
    bottom_first,
    bias_first,
    bottom_second,
    bias_second,
    bottom_third,
    bias_third,
    top_hidden,
    bias_hidden,
    top_logit,
    bias_logit,
):
    chips = lax.axis_size("chip")
    mine = lax.axis_index(ALL)
    outgoing = route(orphan_owner[:, 0], orphan_blocks, chips)
    rehomed = exchange(outgoing, "chip")
    tab = lax.dynamic_index_in_dim(jnp.asarray(TABLE), mine % PERIOD, 0, keepdims=False)
    pieces = pool(
        tab,
        resident_row_blocks,
        orphan_blocks,
        home_offsets.transpose(0, 2, 1),
        home_lengths,
        home_samples,
        orphan_offsets.transpose(0, 2, 1),
        orphan_lengths,
        orphan_samples,
    )
    arrived = exchange(pieces, ALL)
    first = jax.nn.relu(
        jnp.dot(dense_inputs, bottom_first, preferred_element_type=F32) + bias_first
    ).astype(BF)
    second = jax.nn.relu(
        jnp.dot(first, bottom_second, preferred_element_type=F32) + bias_second
    ).astype(BF)
    bottom = jax.nn.relu(jnp.dot(second, bottom_third, preferred_element_type=F32) + bias_third)
    padded = jnp.concatenate([top_hidden, jnp.zeros((1, top_hidden.shape[1]), BF)], axis=0)
    weights = jnp.take(padded, jnp.asarray(FEATURE_ROWS), axis=0)
    last = jnp.broadcast_to(top_logit.reshape(1, -1), (8, top_logit.shape[0]))
    logits, term = tail(
        jnp.asarray(labels_by_holder()),
        arrived,
        bottom,
        weights,
        bias_hidden[None, :],
        last,
        bias_logit,
        labels[None, :],
    )
    loss = jnp.sum(exchange(term, ALL)[:, 0, 0])
    return rehomed, logits[0], loss


def solution(mesh):
    split = P(ALL)
    return jax.shard_map(
        per_device,
        mesh=mesh,
        in_specs=(split,) * 11 + (P(),) * 10,
        out_specs=(split, split, P()),
        check_vma=False,
    )
```

time: 240 us -> 122 us (0.51)
  other arithmetic: 71.4 us -> 0.76 us
  matrix products: 40.3 us -> 0.69 us
  Pallas kernels: 0 us -> 33.7 us
  blocking collectives: 34.9 us -> 16.1 us
  local copies, waits for them, and re-layouts: 32.2 us -> 15 us
  starting transfers between devices: 26.1 us -> 16.4 us
  waiting for transfers between devices: 31.5 us -> 37.1 us
    scatter-add x1 -> x0, other arithmetic: 58.3 us -> none  [per_device(): jax.ops.segment_sum(arrived_pieces.reshape(-1, width).astype(jnp.float32)...]
    dot_general x5 -> x2, matrix products: 40.3 us -> 0.69 us  [the longest x1 0.46 us: per_device(): jnp.dot(first, bottom_second, preferred_element_type=F32) + bias_second]
    psum x4 -> x0, blocking collectives: 34.9 us -> none  [over_axes(): return functools.reduce(lax.psum, axes, value)]
    pallas_call x0 -> x3, Pallas kernels: none -> 33.7 us  [the longest x1 22.3 us: tail(): pl.pallas_call(tail_kernel, out_shape=(jax.ShapeDtypeStruct((1, BATCH), F...]
    all_to_all x0 -> x1, blocking collectives: none -> 16.1 us  [exchange(): return lax.all_to_all(value, axes, split_axis=0, concat_axis=0, tiled=True)]
    all_to_all x3 -> x2, starting transfers between devices: 26.1 us -> 16.4 us  [exchange(): return lax.all_to_all(value, axes, split_axis=0, concat_axis=0, tiled=True)]
    reshape x1 -> x0, local copies, waits for them, and re-layouts: 6.45 us -> none  [per_device(): pooled = pooled.reshape(batch_rows, F, width)]
    dot_general x1 -> x0, local copies, waits for them, and re-layouts: 5.98 us -> none  [per_device(): jnp.einsum('asu,adu->asd', stacked_vectors, stacked_vectors, preferred_el...]
  transfers between devices with their start and end apart: 3 -> 2, of which waited for: 1 -> 2; matrix products, arithmetic and copies ran while one was open for 58% -> 4% of each run, Pallas kernels for 0% -> 21%
where the time goes in v1:
time: 122 us; the launch traced here: 121 us
  waiting for transfers between devices  37.1 us (30%)
  Pallas kernels  33.7 us (28%)
  starting transfers between devices  16.4 us (13%)
  blocking collectives  16.1 us (13%)
  local copies, waits for them, and re-layouts  15 us (12%)
  between operations  1.58 us (1%)
    all_to_all x2, waiting for transfers between devices, exchange(): return lax.all_to_all(value, axes, split_axis=0, concat_axis=0, tiled=True)  37.1 us
    pallas_call x1, Pallas kernels, tail(): pl.pallas_call(tail_kernel, out_shape=(jax.ShapeDtypeStruct((1, BATCH), F...  22.3 us
    all_to_all x2, starting transfers between devices, exchange(): return lax.all_to_all(value, axes, split_axis=0, concat_axis=0, tiled=True)  16.4 us
    all_to_all x1, blocking collectives, exchange(): return lax.all_to_all(value, axes, split_axis=0, concat_axis=0, tiled=True)  16.1 us
    unnamed x47, local copies, waits for them, and re-layouts  10.6 us
    pallas_call x1, Pallas kernels, pool(): pl.pallas_call(pool_kernel, out_shape=jax.ShapeDtypeStruct((128, ROWS, 12...  8.78 us
    gather x1, local copies, waits for them, and re-layouts, per_device(): weights = jnp.take(padded, jnp.asarray(FEATURE_ROWS), axis=0)  3.61 us
    pallas_call x1, Pallas kernels, route(): pl.pallas_call(route_kernel, out_shape=jax.ShapeDtypeStruct((2 * chips,)...  2.68 us
  transfers between devices with their start and end apart: 2, of which 2 were waited for; matrix products, arithmetic and copies ran while one was open for 4% of the time, Pallas kernels for 21%

profile of v1, /device:TPU:0, one launch (start us, length us, event | category | flops | bytes accessed | tf_op | source)
XLA Modules:
  0.0 121.3 jit_solution(5642360353488967898)
XLA Ops:
  0.6 0.0 copy-start
  0.7 0.7 dynamic-slice_bitcast_fusion.tab
  1.4 1.2 %copy-done.1 = bf16[32,128,128]{2,1,0:T(8,128)(2,1)S(1)} copy-done((bf16[32,128,128]{2,1,0:T(8,128)(2,1)S(1)}, bf16[32,128,128]{2,1,0:T(8,128)(2,1)}, u32[]{:S(2)}) %copy-start.1) | copy-done | bytes 1048600
  2.6 1.4 %copy-done.3 = bf16[48,128,128]{2,1,0:T(8,128)(2,1)S(1)} copy-done((bf16[48,128,128]{2,1,0:T(8,128)(2,1)S(1)}, bf16[48,128,128]{2,1,0:T(8,128)(2,1)}, u32[]{:S(2)}) %copy-start.3) | copy-done | bytes 1572888
  4.0 0.9 copy-done.4
  5.0 0.9 copy-done.5
  5.9 0.7 copy-done.6
  6.6 0.7 copy-done.7
  7.3 0.7 copy-done.8
  8.1 0.7 copy-done.9
  8.8 8.8 %shard_map.248 = bf16[128,88,128]{2,1,0:T(8,128)(2,1)} custom-call(s32[128]{0:T(128)S(1)} %dynamic-slice_bitcast_fusion.tab, bf16[48,128,128]{2,1,0:T(8,128)(2,1)S(1)} %copy-done.3, bf16[32,128,128]{2,1,0:T(8,128)(2,1)S(1)} %copy-done.1, s32[48,8,128]{2,1,0:T(8,128)S(1)} %bitcast.13, s32[48,128]{1,0:T(8,128)S(1)} %copy-done.6, s32[48,128]{1,0:T(8,128)S(1)} %copy-done.7, ...), custom_call_target="tpu_custom_call" | custom-call | flops 352321536 | bytes 6291456 | tf_op jit(solution)/shard_map/pallas_call | solution.py:147
  17.6 11.6 %all-to-all-start.1 = ((bf16[128,88,128]{2,1,0:T(8,128)(2,1)}), bf16[128,88,128]{2,1,0:T(8,128)(2,1)}, u32[]{:S(2)}, u32[]{:S(2)}) async-start(bf16[128,88,128]{2,1,0:T(8,128)(2,1)} %shard_map.248), calls=%async_computation.1 | async-start | bytes 5767168 | tf_op jit(solution)/shard_map/all_to_all | solution.py:275
  29.2 2.7 %shard_map.247 = bf16[64,128,128]{2,1,0:T(8,128)(2,1)} custom-call(s32[32]{0:T(128)S(1)} %bitcast.15, bf16[32,128,128]{2,1,0:T(8,128)(2,1)S(1)} %copy-done.2), custom_call_target="tpu_custom_call" | custom-call | bytes 3145728 | tf_op jit(solution)/shard_map/pallas_call | solution.py:91
  31.9 35.8 %all-to-all-done.1.recv = bf16[128,88,128]{2,1,0:T(8,128)(2,1)} async-done(((bf16[128,88,128]{2,1,0:T(8,128)(2,1)}), bf16[128,88,128]{2,1,0:T(8,128)(2,1)}, u32[]{:S(2)}, u32[]{:S(2)}) %all-to-all-start.1) | async-done | bytes 2883616 | tf_op jit(solution)/shard_map/all_to_all | solution.py:275
  67.7 4.8 %all-to-all-start = ((bf16[64,128,128]{2,1,0:T(8,128)(2,1)}), bf16[64,128,128]{2,1,0:T(8,128)(2,1)}, u32[]{:S(2)}, u32[]{:S(2)}) async-start(bf16[64,128,128]{2,1,0:T(8,128)(2,1)} %shard_map.247), calls=%async_computation | async-start | bytes 4194304 | tf_op jit(solution)/shard_map/all_to_all | solution.py:275
  73.1 0.1 concatenate.3
  73.3 3.6 %gather_fusion = bf16[896,1024]{1,0:T(8,128)(2,1)S(1)} fusion(bf16[480,1024]{1,0:T(8,128)(2,1)S(1)} %concatenate.3, s32[1024]{0:T(1024)S(1)} %pad_clamp_fusion), kind=kCustom, calls=%fused_computation | custom fusion | bytes 3673600 | tf_op jit(solution)/shard_map/jit(_take)/gather | solution.py:326
  77.0 0.5 fusion.5
  77.5 0.2 fusion.6.bottom
  77.8 22.3 %shard_map.249 = (f32[1,512]{1,0:T(1,128)}, f32[128,1,128]{2,1,0:T(1,128)S(1)}) custom-call(s32[8,128]{1,0:T(8,128)S(1)} %copy-done.13, bf16[128,88,128]{2,1,0:T(8,128)(2,1)} %all-to-all-done.1.recv, f32[512,128]{1,0:T(8,128)S(1)} %fusion.6.bottom, bf16[896,1024]{1,0:T(8,128)(2,1)S(1)} %gather_fusion, f32[1,1024]{1,0:T(1,128)S(1)} %bitcast.16, ...), custom_call_target="tpu_custom_call" | custom-call | flops 6442450944 | bytes 5242880 | tf_op jit(solution)/shard_map/pallas_call | solution.py:250
  100.1 1.3 %all-to-all-done = bf16[64,128,128]{2,1,0:T(8,128)(2,1)} async-done(((bf16[64,128,128]{2,1,0:T(8,128)(2,1)}), bf16[64,128,128]{2,1,0:T(8,128)(2,1)}, u32[]{:S(2)}, u32[]{:S(2)}) %all-to-all-start) | async-done | bytes 2097184 | tf_op jit(solution)/shard_map/all_to_all | solution.py:275
  101.3 16.1 %all_to_all.15 = f32[128,1,128]{2,1,0:T(1,128)S(1)} all-to-all(f32[128,1,128]{2,1,0:T(1,128)S(1)} %get-tuple-element.6), channel_id=1, replica_groups=mesh['hst'=4,'chip'=32] {'hst','chip'}, dimensions={0} | all-to-all | bytes 131072 | tf_op jit(solution)/shard_map/all_to_all | solution.py:275
  117.4 0.7 slice_reduce_fusion
  118.1 3.2 %copy.29 = bf16[64,128,128]{2,1,0:T(8,128)(2,1)} copy(bf16[64,128,128]{2,1,0:T(8,128)(2,1)} %all-to-all-done) | data formatting | bytes 4194304
  (40 shorter events, 0.1 us)
Async XLA Ops:
  0.6 76.4 %copy-start = (bf16[512,256]{1,0:T(8,128)(2,1)S(1)}, bf16[512,256]{1,0:T(8,128)(2,1)}, u32[]{:S(2)}) copy-start(bf16[512,256]{1,0:T(8,128)(2,1)} %param.37) | copy-start | bytes 786436
  1.4 1.2 %copy-start.1 = (bf16[32,128,128]{2,1,0:T(8,128)(2,1)S(1)}, bf16[32,128,128]{2,1,0:T(8,128)(2,1)}, u32[]{:S(2)}) copy-start(bf16[32,128,128]{2,1,0:T(8,128)(2,1)} %orphan.1) | copy-start | bytes 3145732
  2.6 1.4 %copy-start.3 = (bf16[48,128,128]{2,1,0:T(8,128)(2,1)S(1)}, bf16[48,128,128]{2,1,0:T(8,128)(2,1)}, u32[]{:S(2)}) copy-start(bf16[48,128,128]{2,1,0:T(8,128)(2,1)} %home.1) | copy-start | bytes 4718596
  4.0 0.9 copy-start.4
  5.0 0.9 copy-start.5
  5.9 0.7 copy-start.6
  6.6 0.7 copy-start.7
  7.3 0.7 copy-start.8
  17.6 11.6 %copy-start.2 = (bf16[32,128,128]{2,1,0:T(8,128)(2,1)S(1)}, bf16[32,128,128]{2,1,0:T(8,128)(2,1)}, u32[]{:S(2)}) copy-start(bf16[32,128,128]{2,1,0:T(8,128)(2,1)} %orphan.1) | copy-start | bytes 3145732
  17.6 11.6 %copy-start.10 = (s32[32,1]{0,1:T(1,128)S(1)}, s32[32,1]{0,1:T(1,128)}, u32[]{:S(2)}) copy-start(s32[32,1]{0,1:T(1,128)} %param.32) | copy-start | bytes 388
  17.6 50.1 %all-to-all-start.1 = ((bf16[128,88,128]{2,1,0:T(8,128)(2,1)}), bf16[128,88,128]{2,1,0:T(8,128)(2,1)}, u32[]{:S(2)}, u32[]{:S(2)}) async-start(bf16[128,88,128]{2,1,0:T(8,128)(2,1)} %shard_map.248), calls=%async_computation.1 | async-start | bytes 5767168 | tf_op jit(solution)/shard_map/all_to_all | solution.py:275
  31.9 41.2 %copy-start.14 = (bf16[479,1024]{1,0:T(8,128)(2,1)S(1)}, bf16[479,1024]{1,0:T(8,128)(2,1)}, u32[]{:S(2)}) copy-start(bf16[479,1024]{1,0:T(8,128)(2,1)} %param.41) | copy-start | bytes 2942980
  31.9 41.3 %copy-start.16 = (s32[896]{0:T(1024)S(1)}, s32[896]{0:T(1024)}, u32[]{:S(2)}) copy-start(s32[896]{0:T(1024)} %constant.78) | copy-start | bytes 10756
  67.7 33.7 %all-to-all-start = ((bf16[64,128,128]{2,1,0:T(8,128)(2,1)}), bf16[64,128,128]{2,1,0:T(8,128)(2,1)}, u32[]{:S(2)}, u32[]{:S(2)}) async-start(bf16[64,128,128]{2,1,0:T(8,128)(2,1)} %shard_map.247), calls=%async_computation | async-start | bytes 4194304 | tf_op jit(solution)/shard_map/all_to_all | solution.py:275
  73.2 3.7 %copy-start.17 = (bf16[1024,1]{0,1:T(2,128)(2,1)S(1)}, bf16[1024,1]{0,1:T(2,128)(2,1)}, u32[]{:S(2)}) copy-start(bf16[1024,1]{0,1:T(2,128)(2,1)} %param.43) | copy-start | bytes 6148
  73.2 3.8 %copy-start.19 = (bf16[512,13]{0,1:T(8,128)(2,1)S(1)}, bf16[512,13]{0,1:T(8,128)(2,1)}, u32[]{:S(2)}) copy-start(bf16[512,13]{0,1:T(8,128)(2,1)} %param.33) | copy-start | bytes 39940
  73.2 3.8 %copy-start.20 = (bf16[13,512]{1,0:T(8,128)(2,1)S(1)}, bf16[13,512]{1,0:T(8,128)(2,1)}, u32[]{:S(2)}) copy-start(bf16[13,512]{1,0:T(8,128)(2,1)} %param.35) | copy-start | bytes 39940
  73.3 3.8 %copy-start.21 = (f32[512]{0:T(512)S(1)}, f32[512]{0:T(512)}, u32[]{:S(2)}) copy-start(f32[512]{0:T(512)} %param.36) | copy-start | bytes 6148
  73.3 3.8 %copy-start.22 = (f32[256]{0:T(256)S(1)}, f32[256]{0:T(256)}, u32[]{:S(2)}) copy-start(f32[256]{0:T(256)} %param.38) | copy-start | bytes 3076
  73.3 4.2 %copy-start.15 = (bf16[256,128]{1,0:T(8,128)(2,1)S(1)}, bf16[256,128]{1,0:T(8,128)(2,1)}, u32[]{:S(2)}) copy-start(bf16[256,128]{1,0:T(8,128)(2,1)} %param.39) | copy-start | bytes 196612
  73.3 4.2 %copy-start.18 = (f32[128]{0:T(128)S(1)}, f32[128]{0:T(128)}, u32[]{:S(2)}) copy-start(f32[128]{0:T(128)} %param.40) | copy-start | bytes 1540
  76.9 0.9 copy-start.11
  76.9 0.8 copy-start.12
  77.0 0.8 copy-start.13
  (1 other events, 0.7 us)

commit v2 on v1

--- a/solution.py
+++ b/solution.py
@@ -99,60 +99,81 @@
     )(orphan_owner, orphans)
 
 
-def pool_kernel(tab, home, orphan, home_off, home_len, home_sam, orphan_off, orphan_len, orphan_sam, out, wide, sam):
+def pool_kernel(*refs):
+    given, out, (wide, sam), held, sem = refs[:8], refs[8], refs[9:11], refs[11:19], refs[19]
+    copies = [pltpu.make_async_copy(g, h, sem.at[n]) for n, (g, h) in enumerate(zip(given, held))]
+    for copy in copies:
+        copy.start()
+    home, orphan = (held[0],) + tuple(held[2:5]), (held[1],) + tuple(held[5:8])
+    me = lax.axis_index("hst") * lax.axis_size("chip") + lax.axis_index("chip")
     rows = lax.broadcasted_iota(jnp.int32, (128, 128), 0).astype(F32).astype(BF)
     place = lax.broadcasted_iota(jnp.int32, (8, 128), 0)
     one, zero = jnp.ones((), BF), jnp.zeros((), BF)
-    sam[...] = jnp.zeros_like(sam)
-
-    def piece(slot, blocks, off, length, samples):
-        at = tab[slot]
-        b = jnp.maximum(at, 0)
+    sam[...] = jnp.full(sam.shape, NONE, jnp.int32)
+    for s in range(SLOTS + 2, ROWS):
+        wide[pl.ds(s, 128, stride=ROWS), :] = jnp.zeros((128, 128), F32)
+    for copy in copies:
+        copy.wait()
+
+    def piece(slot, b, blocks, off, length, samples):
         live = jnp.where(place < length[pl.ds(b, 1), :], off[b], -1).astype(F32).astype(BF)
         counts = jnp.zeros((128, 128), BF)
         for n in range(8):
             counts = counts + jnp.where(rows == live[n : n + 1, :], one, zero)
         sums = lax.dot_general(counts, blocks[b], (((0,), (0,)), ((), ())), preferred_element_type=F32)
         wide[pl.ds(slot, 128, stride=ROWS), :] = sums
-        sam[pl.ds(slot, 1), :] = jnp.where(at >= 0, samples[pl.ds(b, 1), :], NONE)
-
-    def group(g, _):
-        for e in range(4):
-            piece(FIXED * g + e, home, home_off, home_len, home_sam)
-        for e in range(4, 6):
-            piece(FIXED * g + e, orphan, orphan_off, orphan_len, orphan_sam)
-        return 0
-
-    lax.fori_loop(0, PERIOD, group, 0)
-
-    def last(s, _):
-        piece(PERIOD * FIXED + s, orphan, orphan_off, orphan_len, orphan_sam)
-        return 0
-
-    lax.fori_loop(0, 6, last, 0)
+        sam[pl.ds(slot, 1), :] = samples[pl.ds(b, 1), :]
+
+    def pair(k, more):
+        g = FIXED * lax.rem(11 * me + k, PERIOD)
+        for e in range(2):
+            piece(g + e, 2 * k + e, *home)
+        for e in range(2):
+            if more:
+                piece(g + 2 + e, 2 * (k + PERIOD) + e, *home)
+            else:
+                wide[pl.ds(g + 2 + e, 128, stride=ROWS), :] = jnp.zeros((128, 128), F32)
+        g = FIXED * lax.rem(4 + 3 * me + k, PERIOD)
+        for e in range(2):
+            piece(g + 4 + e, 2 * k + e, *orphan)
+
+    def step(k, _):
+        pair(k, True)
+        return 0
+
+    both = HOME // 2 - PERIOD
+    lax.fori_loop(0, both, step, 0, unroll=2)
+    for k in range(both, PERIOD):
+        pair(k, False)
+    rest = [lax.rem(4 + 3 * me + i, PERIOD) for i in range(3)]
+    for i, g in enumerate(rest):
+        others = sum(lax.rem(h, 3) for h in rest if h is not g)
+        at = jnp.where(g == 0, 3 - others, lax.rem(g, 3))
+        for e in range(2):
+            piece(PERIOD * FIXED + 2 * at + e, 2 * (PERIOD + i) + e, *orphan)
     index = sam[...]
     wide[pl.ds(SLOTS, 128, stride=ROWS), :] = (index >> 4).astype(F32).T
     wide[pl.ds(SLOTS + 1, 128, stride=ROWS), :] = (index & 15).astype(F32).T
-    for s in range(SLOTS + 2, ROWS):
-        wide[pl.ds(s, 128, stride=ROWS), :] = jnp.zeros((128, 128), F32)
 
     def narrow(q, _):
         out[pl.ds(4 * q, 4)] = wide[pl.ds(4 * q * ROWS, 4 * ROWS), :].reshape(4, ROWS, 128).astype(BF)
         return 0
 
-    lax.fori_loop(0, 32, narrow, 0)
-
-
-def pool(tab, *arrays):
+    lax.fori_loop(0, 32, narrow, 0, unroll=2)
+
+
+def pool(*arrays):
     return pl.pallas_call(
         pool_kernel,
         out_shape=jax.ShapeDtypeStruct((128, ROWS, 128), BF),
-        in_specs=[SMEM] + [VMEM] * 8,
+        in_specs=[pl.BlockSpec(memory_space=pl.ANY)] * 8,
         out_specs=VMEM,
-        scratch_shapes=[pltpu.VMEM((128 * ROWS, 128), F32), pltpu.VMEM((128, 128), jnp.int32)],
+        scratch_shapes=[pltpu.VMEM((128 * ROWS, 128), F32), pltpu.VMEM((128, 128), jnp.int32)]
+        + [pltpu.VMEM(a.shape, a.dtype) for a in arrays]
+        + [pltpu.SemaphoreType.DMA((8,))],
         compiler_params=pltpu.CompilerParams(vmem_limit_bytes=24 << 20),
         cost_estimate=pl.CostEstimate(flops=84 * 128 * 128 * 256, transcendentals=0, bytes_accessed=6 << 20),
-    )(tab, *arrays)
+    )(*arrays)
 
 
 def tail_kernel(label, recv, bottom, weights, bias, last, last_bias, marks, logits, loss, wide, hi, lo, stack, turned, packed):
@@ -163,7 +184,7 @@
         wide[pl.ds(4 * p * ROWS, 4 * ROWS), :] = recv[pl.ds(4 * p, 4)].astype(F32).reshape(4 * ROWS, 128)
         return 0
 
-    lax.fori_loop(0, 32, widen, 0)
+    lax.fori_loop(0, 32, widen, 0, unroll=2)
     hi[...] = wide[pl.ds(SLOTS, 128, stride=ROWS), :].T
     lo[...] = wide[pl.ds(SLOTS + 1, 128, stride=ROWS), :].T
 
@@ -204,7 +225,7 @@
         pooled(g, [lax.rem(g, 3)])
         return 0
 
-    lax.fori_loop(1, PERIOD, group, 0)
+    lax.fori_loop(1, PERIOD, group, 0, unroll=4)
 
     packed[:, :128] = bottom[...].astype(BF)
     own = lax.broadcasted_iota(jnp.int32, (8, 128), 1) % 8 == 7 - lax.broadcasted_iota(jnp.int32, (8, 128), 0)
@@ -232,7 +253,7 @@
         packed[pl.ds(pl.multiple_of(16 * m, 16), 16), 128:] = jnp.concatenate(halves, axis=0).astype(BF)
         return 0
 
-    lax.fori_loop(0, BATCH // 16, interact, 0)
+    lax.fori_loop(0, BATCH // 16, interact, 0, unroll=4)
 
     for m in range(4):
         at = pl.ds(128 * m, 128)
@@ -249,7 +270,7 @@
 def tail(label, recv, bottom, weights, bias, last, last_bias, marks):
     return pl.pallas_call(
         tail_kernel,
-        out_shape=(jax.ShapeDtypeStruct((1, BATCH), F32), jax.ShapeDtypeStruct((128, 1, 128), F32)),
+        out_shape=(jax.ShapeDtypeStruct((1, BATCH), F32), jax.ShapeDtypeStruct((1, 128), F32)),
         in_specs=[VMEM] * 6 + [SMEM, VMEM],
         out_specs=(VMEM, VMEM),
         scratch_shapes=[
@@ -273,6 +294,14 @@
 
 def exchange(value, axes):
     return lax.all_to_all(value, axes, split_axis=0, concat_axis=0, tiled=True)
+
+
+def ring_sum(value, axis, size, step):
+    def shifted(k):
+        pairs = [(i, i - i // step % 4 * step + (i // step + k) % 4 * step) for i in range(size)]
+        return lax.ppermute(value, axis, pairs)
+
+    return (value + shifted(2)) + (shifted(1) + shifted(3))
 
 
 def per_device(
@@ -299,12 +328,8 @@
     bias_logit,
 ):
     chips = lax.axis_size("chip")
-    mine = lax.axis_index(ALL)
     outgoing = route(orphan_owner[:, 0], orphan_blocks, chips)
-    rehomed = exchange(outgoing, "chip")
-    tab = lax.dynamic_index_in_dim(jnp.asarray(TABLE), mine % PERIOD, 0, keepdims=False)
     pieces = pool(
-        tab,
         resident_row_blocks,
         orphan_blocks,
         home_offsets.transpose(0, 2, 1),
@@ -325,6 +350,8 @@
     padded = jnp.concatenate([top_hidden, jnp.zeros((1, top_hidden.shape[1]), BF)], axis=0)
     weights = jnp.take(padded, jnp.asarray(FEATURE_ROWS), axis=0)
     last = jnp.broadcast_to(top_logit.reshape(1, -1), (8, top_logit.shape[0]))
+    outgoing, weights, bottom, last = lax.optimization_barrier((outgoing, weights, bottom, last))
+    rehomed = exchange(outgoing, "chip")
     logits, term = tail(
         jnp.asarray(labels_by_holder()),
         arrived,
@@ -335,8 +362,11 @@
         bias_logit,
         labels[None, :],
     )
-    loss = jnp.sum(exchange(term, ALL)[:, 0, 0])
-    return rehomed, logits[0], loss
+    term = ring_sum(term, "hst", lax.axis_size("hst"), 1)
+    term = term + lax.ppermute(term, "chip", [(i, i ^ 1) for i in range(chips)])
+    term = ring_sum(term, "chip", chips, 2)
+    term = ring_sum(term, "chip", chips, 8)
+    return rehomed, logits[0], term[0, 0]
 
 
 def solution(mesh):

time: 122 us -> 113 us (0.926)
  starting transfers between devices: 16.4 us -> 33.2 us
  blocking collectives: 16.1 us -> 0 us
  Pallas kernels: 33.7 us -> 24.5 us
    ppermute x0 -> x10, starting transfers between devices: none -> 16.8 us  [the longest x9 16.7 us: shifted(): return lax.ppermute(value, axis, pairs)]
    all_to_all x1 -> x0, blocking collectives: 16.1 us -> none  [exchange(): return lax.all_to_all(value, axes, split_axis=0, concat_axis=0, tiled=True)]
    pallas_call x1, Pallas kernels: 22.3 us -> 15.4 us  [tail(): pl.pallas_call(tail_kernel, out_shape=(jax.ShapeDtypeStruct((1, BATCH), F...]
    all_to_all x2, waiting for transfers between devices: 37.1 us -> 31.1 us  [exchange(): return lax.all_to_all(value, axes, split_axis=0, concat_axis=0, tiled=True)]
    ppermute x0 -> x10, waiting for transfers between devices: none -> 5.66 us  [the longest x9 4.55 us: shifted(): return lax.ppermute(value, axis, pairs)]
    pallas_call x1, Pallas kernels: 8.78 us -> 6.37 us  [pool(): pl.pallas_call(pool_kernel, out_shape=jax.ShapeDtypeStruct((128, ROWS, 12...]
  transfers between devices with their start and end apart: 2 -> 12, of which waited for: 2 -> 6; matrix products, arithmetic and copies ran while one was open for 4% -> 4% of each run, Pallas kernels for 21% -> 16%
where the time goes in v2:
time: 113 us; the launch traced here: 112 us
  waiting for transfers between devices  36.8 us (33%)
  starting transfers between devices  33.2 us (29%)
  Pallas kernels  24.5 us (22%)
  local copies, waits for them, and re-layouts  14.3 us (13%)
  between operations  1.62 us (1%)
    all_to_all x2, waiting for transfers between devices, exchange(): return lax.all_to_all(value, axes, split_axis=0, concat_axis=0, tiled=True)  31.1 us
    ppermute x9, starting transfers between devices, shifted(): return lax.ppermute(value, axis, pairs)  16.7 us
    all_to_all x2, starting transfers between devices, exchange(): return lax.all_to_all(value, axes, split_axis=0, concat_axis=0, tiled=True)  16.4 us
    pallas_call x1, Pallas kernels, tail(): pl.pallas_call(tail_kernel, out_shape=(jax.ShapeDtypeStruct((1, BATCH), F...  15.4 us
    unnamed x47, local copies, waits for them, and re-layouts  10.7 us
    pallas_call x1, Pallas kernels, pool(): pl.pallas_call(pool_kernel, out_shape=jax.ShapeDtypeStruct((128, ROWS, 12...  6.37 us
    ppermute x9, waiting for transfers between devices, shifted(): return lax.ppermute(value, axis, pairs)  4.55 us
    gather x1, local copies, waits for them, and re-layouts, per_device(): weights = jnp.take(padded, jnp.asarray(FEATURE_ROWS), axis=0)  3.61 us
  transfers between devices with their start and end apart: 12, of which 6 were waited for; matrix products, arithmetic and copies ran while one was open for 4% of the time, Pallas kernels for 16%

profile of v2, /device:TPU:0, one launch (start us, length us, event | category | flops | bytes accessed | tf_op | source)
XLA Modules:
  0.0 111.6 jit_solution(10822177745103544697)
XLA Ops:
  0.7 1.3 %copy-done.1 = bf16[32,128,128]{2,1,0:T(8,128)(2,1)S(1)} copy-done((bf16[32,128,128]{2,1,0:T(8,128)(2,1)S(1)}, bf16[32,128,128]{2,1,0:T(8,128)(2,1)}, u32[]{:S(2)}) %copy-start.1) | copy-done | bytes 1048600
  1.9 1.4 %copy-done.3 = bf16[48,128,128]{2,1,0:T(8,128)(2,1)S(1)} copy-done((bf16[48,128,128]{2,1,0:T(8,128)(2,1)S(1)}, bf16[48,128,128]{2,1,0:T(8,128)(2,1)}, u32[]{:S(2)}) %copy-start.3) | copy-done | bytes 1572888
  3.3 0.9 copy-done.4
  4.3 0.9 copy-done.5
  5.2 0.7 copy-done.6
  5.9 0.7 copy-done.7
  8.1 6.4 %shard_map.239 = bf16[128,88,128]{2,1,0:T(8,128)(2,1)} custom-call(bf16[48,128,128]{2,1,0:T(8,128)(2,1)S(1)} %copy-done.3, bf16[32,128,128]{2,1,0:T(8,128)(2,1)S(1)} %copy-done.1, s32[48,8,128]{2,1,0:T(8,128)S(1)} %bitcast.13, s32[48,128]{1,0:T(8,128)S(1)} %copy-done.6, s32[48,128]{1,0:T(8,128)S(1)} %copy-done.7, s32[32,8,128]{2,1,0:T(8,128)S(1)} %bitcast.14, ...), custom_call_target="tpu_custom_call" | custom-call | flops 352321536 | bytes 6291456 | tf_op jit(solution)/shard_map/pallas_call | solution.py:166
  14.5 11.6 %all-to-all-start.1 = ((bf16[128,88,128]{2,1,0:T(8,128)(2,1)}), bf16[128,88,128]{2,1,0:T(8,128)(2,1)}, u32[]{:S(2)}, u32[]{:S(2)}) async-start(bf16[128,88,128]{2,1,0:T(8,128)(2,1)} %shard_map.239), calls=%async_computation.1 | async-start | bytes 5767168 | tf_op jit(solution)/shard_map/all_to_all | solution.py:296
  26.1 2.7 %shard_map.238 = bf16[64,128,128]{2,1,0:T(8,128)(2,1)} custom-call(s32[32]{0:T(128)S(1)} %bitcast.15, bf16[32,128,128]{2,1,0:T(8,128)(2,1)S(1)} %copy-done.2), custom_call_target="tpu_custom_call" | custom-call | bytes 3145728 | tf_op jit(solution)/shard_map/pallas_call | solution.py:91
  29.0 3.6 %gather_fusion = bf16[896,1024]{1,0:T(8,128)(2,1)S(1)} fusion(bf16[480,1024]{1,0:T(8,128)(2,1)S(1)} %concatenate.3, s32[1024]{0:T(1024)S(1)} %pad_clamp_fusion), kind=kCustom, calls=%fused_computation | custom fusion | bytes 3673600 | tf_op jit(solution)/shard_map/jit(_take)/gather | solution.py:351
  33.5 31.1 %all-to-all-done.1.recv = bf16[128,88,128]{2,1,0:T(8,128)(2,1)} async-done(((bf16[128,88,128]{2,1,0:T(8,128)(2,1)}), bf16[128,88,128]{2,1,0:T(8,128)(2,1)}, u32[]{:S(2)}, u32[]{:S(2)}) %all-to-all-start.1) | async-done | bytes 2883616 | tf_op jit(solution)/shard_map/all_to_all | solution.py:296
  64.6 4.8 %all-to-all-start = ((bf16[64,128,128]{2,1,0:T(8,128)(2,1)}), bf16[64,128,128]{2,1,0:T(8,128)(2,1)}, u32[]{:S(2)}, u32[]{:S(2)}) async-start(bf16[64,128,128]{2,1,0:T(8,128)(2,1)} %shard_map.238), calls=%async_computation | async-start | bytes 4194304 | tf_op jit(solution)/shard_map/all_to_all | solution.py:296
  70.0 15.4 %shard_map.240 = (f32[1,512]{1,0:T(1,128)}, f32[1,128]{1,0:T(1,128)S(1)}) custom-call(s32[8,128]{1,0:T(8,128)S(1)} %copy-done.13, bf16[128,88,128]{2,1,0:T(8,128)(2,1)} %all-to-all-done.1.recv, f32[512,128]{1,0:T(8,128)S(1)} %fusion.6.bottom, bf16[896,1024]{1,0:T(8,128)(2,1)S(1)} %gather_fusion, f32[1,1024]{1,0:T(1,128)S(1)} %bitcast.16, ...), custom_call_target="tpu_custom_call" | custom-call | flops 6442450944 | bytes 5242880 | tf_op jit(solution)/shard_map/pallas_call | solution.py:271
  86.2 1.2 %collective-permute-start.1 = (f32[1,128]{1,0:T(1,128)S(1)}, f32[1,128]{1,0:T(1,128)S(1)}, u32[]{:S(2)}, u32[]{:S(2)}) collective-permute-start(f32[1,128]{1,0:T(1,128)S(1)} %get-tuple-element.14), channel_id=1, source_target_pairs={{0,32},{32,64},{64,96},{96,0},{1,33},{33,65},{65,97},{97,1},{2,34}... | collective-permute-start | bytes 1544 | tf_op jit(solution)/shard_map/ppermute | solution.py:302
  87.4 2.0 %collective-permute-start.2 = (f32[1,128]{1,0:T(1,128)S(1)}, f32[1,128]{1,0:T(1,128)S(1)}, u32[]{:S(2)}, u32[]{:S(2)}) collective-permute-start(f32[1,128]{1,0:T(1,128)S(1)} %get-tuple-element.14), channel_id=1, source_target_pairs={{0,96},{32,0},{64,32},{96,64},{1,97},{33,1},{65,33},{97,65},{2,98}... | collective-permute-start | bytes 1544 | tf_op jit(solution)/shard_map/ppermute | solution.py:302
  89.4 1.1 %collective-permute-done = f32[1,128]{1,0:T(1,128)S(1)} collective-permute-done((f32[1,128]{1,0:T(1,128)S(1)}, f32[1,128]{1,0:T(1,128)S(1)}, u32[]{:S(2)}, u32[]{:S(2)}) %collective-permute-start) | collective-permute-done | bytes 544 | tf_op jit(solution)/shard_map/ppermute | solution.py:302
  91.0 1.1 collective-permute-done.3
  92.1 3.1 %collective-permute-start.4 = (f32[1,128]{1,0:T(1,128)S(1)}, f32[1,128]{1,0:T(1,128)S(1)}, u32[]{:S(2)}, u32[]{:S(2)}) collective-permute-start(f32[1,128]{1,0:T(1,128)S(1)} %add.75), channel_id=1, source_target_pairs={{0,4},{1,5},{2,6},{3,7},{4,0},{5,1},{6,2},{7,3},{8,12},{9,13},{10,... | collective-permute-start | bytes 1544 | tf_op jit(solution)/shard_map/ppermute | solution.py:302
  95.8 2.7 %collective-permute-start.6 = (f32[1,128]{1,0:T(1,128)S(1)}, f32[1,128]{1,0:T(1,128)S(1)}, u32[]{:S(2)}, u32[]{:S(2)}) collective-permute-start(f32[1,128]{1,0:T(1,128)S(1)} %add.75), channel_id=1, source_target_pairs={{0,6},{1,7},{2,0},{3,1},{4,2},{5,3},{6,4},{7,5},{8,14},{9,15},{10,... | collective-permute-start | bytes 1544 | tf_op jit(solution)/shard_map/ppermute | solution.py:302
  98.5 1.5 %collective-permute-done.5 = f32[1,128]{1,0:T(1,128)S(1)} collective-permute-done((f32[1,128]{1,0:T(1,128)S(1)}, f32[1,128]{1,0:T(1,128)S(1)}, u32[]{:S(2)}, u32[]{:S(2)}) %collective-permute-start.5) | collective-permute-done | bytes 544 | tf_op jit(solution)/shard_map/ppermute | solution.py:302
  100.0 3.2 %collective-permute-start.7 = (f32[1,128]{1,0:T(1,128)S(1)}, f32[1,128]{1,0:T(1,128)S(1)}, u32[]{:S(2)}, u32[]{:S(2)}) collective-permute-start(f32[1,128]{1,0:T(1,128)S(1)} %add_add_fusion.1), channel_id=1, source_target_pairs={{0,16},{1,17},{2,18},{3,19},{4,20},{5,21},{6,22},{7,23},{8,24},{9,... | collective-permute-start | bytes 1544 | tf_op jit(solution)/shard_map/ppermute | solution.py:302
  103.8 2.6 %collective-permute-start.9 = (f32[1,128]{1,0:T(1,128)S(1)}, f32[1,128]{1,0:T(1,128)S(1)}, u32[]{:S(2)}, u32[]{:S(2)}) collective-permute-start(f32[1,128]{1,0:T(1,128)S(1)} %add_add_fusion.1), channel_id=1, source_target_pairs={{0,24},{1,25},{2,26},{3,27},{4,28},{5,29},{6,30},{7,31},{8,0},{9,1... | collective-permute-start | bytes 1544 | tf_op jit(solution)/shard_map/ppermute | solution.py:302
  106.4 1.5 %collective-permute-done.8 = f32[1,128]{1,0:T(1,128)S(1)} collective-permute-done((f32[1,128]{1,0:T(1,128)S(1)}, f32[1,128]{1,0:T(1,128)S(1)}, u32[]{:S(2)}, u32[]{:S(2)}) %collective-permute-start.8) | collective-permute-done | bytes 544 | tf_op jit(solution)/shard_map/ppermute | solution.py:302
  108.5 3.2 %copy.28 = bf16[64,128,128]{2,1,0:T(8,128)(2,1)} copy(bf16[64,128,128]{2,1,0:T(8,128)(2,1)} %all-to-all-done) | data formatting | bytes 4194304
  (61 shorter events, 5.2 us)
Async XLA Ops:
  0.6 32.0 %copy-start = (bf16[512,256]{1,0:T(8,128)(2,1)S(1)}, bf16[512,256]{1,0:T(8,128)(2,1)}, u32[]{:S(2)}) copy-start(bf16[512,256]{1,0:T(8,128)(2,1)} %param.36) | copy-start | bytes 786436
  14.4 11.7 %copy-start.2 = (bf16[32,128,128]{2,1,0:T(8,128)(2,1)S(1)}, bf16[32,128,128]{2,1,0:T(8,128)(2,1)}, u32[]{:S(2)}) copy-start(bf16[32,128,128]{2,1,0:T(8,128)(2,1)} %refs_1_.1) | copy-start | bytes 3145732
  14.5 11.7 %copy-start.10 = (s32[32,1]{0,1:T(1,128)S(1)}, s32[32,1]{0,1:T(1,128)}, u32[]{:S(2)}) copy-start(s32[32,1]{0,1:T(1,128)} %param.31) | copy-start | bytes 388
  14.5 50.1 %all-to-all-start.1 = ((bf16[128,88,128]{2,1,0:T(8,128)(2,1)}), bf16[128,88,128]{2,1,0:T(8,128)(2,1)}, u32[]{:S(2)}, u32[]{:S(2)}) async-start(bf16[128,88,128]{2,1,0:T(8,128)(2,1)} %shard_map.239), calls=%async_computation.1 | async-start | bytes 5767168 | tf_op jit(solution)/shard_map/all_to_all | solution.py:296
  28.9 3.7 %copy-start.19 = (bf16[512,13]{0,1:T(8,128)(2,1)S(1)}, bf16[512,13]{0,1:T(8,128)(2,1)}, u32[]{:S(2)}) copy-start(bf16[512,13]{0,1:T(8,128)(2,1)} %param.32) | copy-start | bytes 39940
  28.9 3.7 %copy-start.20 = (bf16[13,512]{1,0:T(8,128)(2,1)S(1)}, bf16[13,512]{1,0:T(8,128)(2,1)}, u32[]{:S(2)}) copy-start(bf16[13,512]{1,0:T(8,128)(2,1)} %param.34) | copy-start | bytes 39940
  29.0 3.7 %copy-start.21 = (f32[512]{0:T(512)S(1)}, f32[512]{0:T(512)}, u32[]{:S(2)}) copy-start(f32[512]{0:T(512)} %param.35) | copy-start | bytes 6148
  29.0 3.7 %copy-start.22 = (f32[256]{0:T(256)S(1)}, f32[256]{0:T(256)}, u32[]{:S(2)}) copy-start(f32[256]{0:T(256)} %param.37) | copy-start | bytes 3076
  29.0 4.2 %copy-start.15 = (bf16[256,128]{1,0:T(8,128)(2,1)S(1)}, bf16[256,128]{1,0:T(8,128)(2,1)}, u32[]{:S(2)}) copy-start(bf16[256,128]{1,0:T(8,128)(2,1)} %param.38) | copy-start | bytes 196612
  29.0 4.2 %copy-start.18 = (f32[128]{0:T(128)S(1)}, f32[128]{0:T(128)}, u32[]{:S(2)}) copy-start(f32[128]{0:T(128)} %param.39) | copy-start | bytes 1540
  33.4 36.6 %copy-start.11 = (f32[1024]{0:T(1024)S(1)}, f32[1024]{0:T(1024)}, u32[]{:S(2)}) copy-start(f32[1024]{0:T(1024)} %param.41) | copy-start | bytes 12292
  33.5 36.6 %copy-start.12 = (s32[512]{0:T(512)S(1)}, s32[512]{0:T(512)}, u32[]{:S(2)}) copy-start(s32[512]{0:T(512)} %param.33) | copy-start | bytes 6148
  33.5 36.6 %copy-start.13 = (s32[8,128]{1,0:T(8,128)S(1)}, s32[8,128]{1,0:T(8,128)}, u32[]{:S(2)}) copy-start(s32[8,128]{1,0:T(8,128)} %constant.30.clone.label) | copy-start | bytes 12292
  64.6 41.8 %all-to-all-start = ((bf16[64,128,128]{2,1,0:T(8,128)(2,1)}), bf16[64,128,128]{2,1,0:T(8,128)(2,1)}, u32[]{:S(2)}, u32[]{:S(2)}) async-start(bf16[64,128,128]{2,1,0:T(8,128)(2,1)} %shard_map.238), calls=%async_computation | async-start | bytes 4194304 | tf_op jit(solution)/shard_map/all_to_all | solution.py:296
  85.5 5.0 %collective-permute-start = (f32[1,128]{1,0:T(1,128)S(1)}, f32[1,128]{1,0:T(1,128)S(1)}, u32[]{:S(2)}, u32[]{:S(2)}) collective-permute-start(f32[1,128]{1,0:T(1,128)S(1)} %get-tuple-element.14), channel_id=1, source_target_pairs={{0,64},{32,96},{64,0},{96,32},{1,65},{33,97},{65,1},{97,33},{2,66}... | collective-permute-start | bytes 1544 | tf_op jit(solution)/shard_map/ppermute | solution.py:302
  86.2 4.8 %collective-permute-start.1 = (f32[1,128]{1,0:T(1,128)S(1)}, f32[1,128]{1,0:T(1,128)S(1)}, u32[]{:S(2)}, u32[]{:S(2)}) collective-permute-start(f32[1,128]{1,0:T(1,128)S(1)} %get-tuple-element.14), channel_id=1, source_target_pairs={{0,32},{32,64},{64,96},{96,0},{1,33},{33,65},{65,97},{97,1},{2,34}... | collective-permute-start | bytes 1544 | tf_op jit(solution)/shard_map/ppermute | solution.py:302
  87.4 3.5 %collective-permute-start.2 = (f32[1,128]{1,0:T(1,128)S(1)}, f32[1,128]{1,0:T(1,128)S(1)}, u32[]{:S(2)}, u32[]{:S(2)}) collective-permute-start(f32[1,128]{1,0:T(1,128)S(1)} %get-tuple-element.14), channel_id=1, source_target_pairs={{0,96},{32,0},{64,32},{96,64},{1,97},{33,1},{65,33},{97,65},{2,98}... | collective-permute-start | bytes 1544 | tf_op jit(solution)/shard_map/ppermute | solution.py:302
  90.9 1.2 %collective-permute-start.3 = (f32[1,128]{1,0:T(1,128)S(1)}, f32[1,128]{1,0:T(1,128)S(1)}, u32[]{:S(2)}, u32[]{:S(2)}) collective-permute-start(f32[1,128]{1,0:T(1,128)S(1)} %add_add_fusion.2), channel_id=1, source_target_pairs={{0,1},{1,0},{2,3},{3,2},{4,5},{5,4},{6,7},{7,6},{8,9},{9,8},{10,11... | collective-permute-start | bytes 1544 | tf_op jit(solution)/shard_map/ppermute | solution.py:366
  92.1 6.4 %collective-permute-start.4 = (f32[1,128]{1,0:T(1,128)S(1)}, f32[1,128]{1,0:T(1,128)S(1)}, u32[]{:S(2)}, u32[]{:S(2)}) collective-permute-start(f32[1,128]{1,0:T(1,128)S(1)} %add.75), channel_id=1, source_target_pairs={{0,4},{1,5},{2,6},{3,7},{4,0},{5,1},{6,2},{7,3},{8,12},{9,13},{10,... | collective-permute-start | bytes 1544 | tf_op jit(solution)/shard_map/ppermute | solution.py:302
  95.2 4.8 %collective-permute-start.5 = (f32[1,128]{1,0:T(1,128)S(1)}, f32[1,128]{1,0:T(1,128)S(1)}, u32[]{:S(2)}, u32[]{:S(2)}) collective-permute-start(f32[1,128]{1,0:T(1,128)S(1)} %add.75), channel_id=1, source_target_pairs={{0,2},{1,3},{2,4},{3,5},{4,6},{5,7},{6,0},{7,1},{8,10},{9,11},{10,... | collective-permute-start | bytes 1544 | tf_op jit(solution)/shard_map/ppermute | solution.py:302
  95.8 4.2 %collective-permute-start.6 = (f32[1,128]{1,0:T(1,128)S(1)}, f32[1,128]{1,0:T(1,128)S(1)}, u32[]{:S(2)}, u32[]{:S(2)}) collective-permute-start(f32[1,128]{1,0:T(1,128)S(1)} %add.75), channel_id=1, source_target_pairs={{0,6},{1,7},{2,0},{3,1},{4,2},{5,3},{6,4},{7,5},{8,14},{9,15},{10,... | collective-permute-start | bytes 1544 | tf_op jit(solution)/shard_map/ppermute | solution.py:302
  100.0 6.4 %collective-permute-start.7 = (f32[1,128]{1,0:T(1,128)S(1)}, f32[1,128]{1,0:T(1,128)S(1)}, u32[]{:S(2)}, u32[]{:S(2)}) collective-permute-start(f32[1,128]{1,0:T(1,128)S(1)} %add_add_fusion.1), channel_id=1, source_target_pairs={{0,16},{1,17},{2,18},{3,19},{4,20},{5,21},{6,22},{7,23},{8,24},{9,... | collective-permute-start | bytes 1544 | tf_op jit(solution)/shard_map/ppermute | solution.py:302
  103.2 4.8 %collective-permute-start.8 = (f32[1,128]{1,0:T(1,128)S(1)}, f32[1,128]{1,0:T(1,128)S(1)}, u32[]{:S(2)}, u32[]{:S(2)}) collective-permute-start(f32[1,128]{1,0:T(1,128)S(1)} %add_add_fusion.1), channel_id=1, source_target_pairs={{0,8},{1,9},{2,10},{3,11},{4,12},{5,13},{6,14},{7,15},{8,16},{9,17... | collective-permute-start | bytes 1544 | tf_op jit(solution)/shard_map/ppermute | solution.py:302
  103.8 4.1 %collective-permute-start.9 = (f32[1,128]{1,0:T(1,128)S(1)}, f32[1,128]{1,0:T(1,128)S(1)}, u32[]{:S(2)}, u32[]{:S(2)}) collective-permute-start(f32[1,128]{1,0:T(1,128)S(1)} %add_add_fusion.1), channel_id=1, source_target_pairs={{0,24},{1,25},{2,26},{3,27},{4,28},{5,29},{6,30},{7,31},{8,0},{9,1... | collective-permute-start | bytes 1544 | tf_op jit(solution)/shard_map/ppermute | solution.py:302
  (11 other events, 16.6 us)

commit v3 on v2

--- a/solution.py
+++ b/solution.py
@@ -171,7 +171,7 @@
         scratch_shapes=[pltpu.VMEM((128 * ROWS, 128), F32), pltpu.VMEM((128, 128), jnp.int32)]
         + [pltpu.VMEM(a.shape, a.dtype) for a in arrays]
         + [pltpu.SemaphoreType.DMA((8,))],
-        compiler_params=pltpu.CompilerParams(vmem_limit_bytes=24 << 20),
+        compiler_params=pltpu.CompilerParams(vmem_limit_bytes=60 << 20),
         cost_estimate=pl.CostEstimate(flops=84 * 128 * 128 * 256, transcendentals=0, bytes_accessed=6 << 20),
     )(*arrays)
 
@@ -297,11 +297,34 @@
 
 
 def ring_sum(value, axis, size, step):
-    def shifted(k):
-        pairs = [(i, i - i // step % 4 * step + (i // step + k) % 4 * step) for i in range(size)]
-        return lax.ppermute(value, axis, pairs)
-
-    return (value + shifted(2)) + (shifted(1) + shifted(3))
+    for other in ((1, 0, 3, 2), (3, 2, 1, 0)):
+        pairs = [(i, i + (other[i // step % 4] - i // step % 4) * step) for i in range(size)]
+        value = value + lax.ppermute(value, axis, pairs)
+    return value
+
+
+def keep_kernel(given, out, sems):
+    part = given.shape[0] // sems.shape[0]
+    copies = []
+    for n in range(sems.shape[0]):
+        at = pl.ds(n * part, part)
+        copies.append(pltpu.make_async_copy(given.at[at], out.at[at], sems.at[n]))
+    for copy in copies:
+        copy.start()
+    for copy in copies:
+        copy.wait()
+
+
+def keep(value):
+    return pl.pallas_call(
+        keep_kernel,
+        out_shape=jax.ShapeDtypeStruct(value.shape, value.dtype),
+        in_specs=[pl.BlockSpec(memory_space=pl.ANY)],
+        out_specs=pl.BlockSpec(memory_space=pl.ANY),
+        scratch_shapes=[pltpu.SemaphoreType.DMA((8,))],
+        compiler_params=pltpu.CompilerParams(vmem_limit_bytes=60 << 20),
+        cost_estimate=pl.CostEstimate(flops=0, transcendentals=0, bytes_accessed=4 << 20),
+    )(value)
 
 
 def per_device(
@@ -365,6 +388,7 @@
     term = ring_sum(term, "hst", lax.axis_size("hst"), 1)
     term = term + lax.ppermute(term, "chip", [(i, i ^ 1) for i in range(chips)])
     term = ring_sum(term, "chip", chips, 2)
+    rehomed, term = lax.optimization_barrier((keep(rehomed), term))
     term = ring_sum(term, "chip", chips, 8)
     return rehomed, logits[0], term[0, 0]
 

time: 113 us -> 169 us (1.50)
  Pallas kernels: 24.5 us -> 90.3 us
  local copies, waits for them, and re-layouts: 14.3 us -> 3.78 us
  waiting for transfers between devices: 36.8 us -> 44.8 us
  starting transfers between devices: 33.2 us -> 26.8 us
    pallas_call x0 -> x1, Pallas kernels: none -> 64.7 us  [keep(): pl.pallas_call(keep_kernel, out_shape=jax.ShapeDtypeStruct(value.shape, v...]
    unnamed x47 -> x30, local copies, waits for them, and re-layouts: 10.7 us -> 0.1 us
    ppermute x9 -> x6, waiting for transfers between devices: 4.55 us -> 12.6 us  [ring_sum(): value = value + lax.ppermute(value, axis, pairs)]
    ppermute x9 -> x6, starting transfers between devices: 16.7 us -> 10.4 us  [ring_sum(): value = value + lax.ppermute(value, axis, pairs)]
  transfers between devices with their start and end apart: 12 -> 9, of which waited for: 6 -> 7; matrix products, arithmetic and copies ran while one was open for 4% -> 3% of each run, Pallas kernels for 16% -> 49%
where the time goes in v3:
time: 169 us
  Pallas kernels  90.3 us (53%)
  waiting for transfers between devices  44.8 us (27%)
  starting transfers between devices  26.8 us (16%)
  local copies, waits for them, and re-layouts  3.78 us (2%)
    pallas_call x1, Pallas kernels, keep(): pl.pallas_call(keep_kernel, out_shape=jax.ShapeDtypeStruct(value.shape, v...  64.7 us
    all_to_all x2, waiting for transfers between devices, exchange(): return lax.all_to_all(value, axes, split_axis=0, concat_axis=0, tiled=True)  31.1 us
    all_to_all x2, starting transfers between devices, exchange(): return lax.all_to_all(value, axes, split_axis=0, concat_axis=0, tiled=True)  16.4 us
    pallas_call x1, Pallas kernels, tail(): pl.pallas_call(tail_kernel, out_shape=(jax.ShapeDtypeStruct((1, BATCH), F...  15.4 us
    ppermute x6, waiting for transfers between devices, ring_sum(): value = value + lax.ppermute(value, axis, pairs)  12.6 us
    ppermute x6, starting transfers between devices, ring_sum(): value = value + lax.ppermute(value, axis, pairs)  10.4 us
    pallas_call x1, Pallas kernels, pool(): pl.pallas_call(pool_kernel, out_shape=jax.ShapeDtypeStruct((128, ROWS, 12...  7.45 us
    gather x1, local copies, waits for them, and re-layouts, per_device(): weights = jnp.take(padded, jnp.asarray(FEATURE_ROWS), axis=0)  3.61 us
  transfers between devices with their start and end apart: 9, of which 7 were waited for; matrix products, arithmetic and copies ran while one was open for 3% of the time, Pallas kernels for 49%

profile of v3, /device:TPU:0, one launch (start us, length us, event | category | flops | bytes accessed | tf_op | source)
XLA Modules:
  0.0 168.6 jit_solution(18091695560366336243)
XLA Ops:
  0.6 7.5 %shard_map.240 = bf16[128,88,128]{2,1,0:T(8,128)(2,1)} custom-call(bf16[48,128,128]{2,1,0:T(8,128)(2,1)} %refs_0_.1, bf16[32,128,128]{2,1,0:T(8,128)(2,1)} %refs_1_.1, s32[48,8,128]{2,1,0:T(8,128)} %bitcast.16, s32[48,128]{1,0:T(8,128)} %refs_3_.1, s32[48,128]{1,0:T(8,128)} %refs_4_.1, s32[32,8,128]{2,1,0:T(8,128)} %bitcast.17, s32[32,128]{1,0:T(8,128)} %refs_6_.1, ...), custom_call_target="tpu_custom_call" | custom-call | flops 352321536 | bytes 6291456 | tf_op jit(solution)/shard_map/pallas_call | solution.py:166
  8.1 11.6 %all-to-all-start.1 = ((bf16[128,88,128]{2,1,0:T(8,128)(2,1)}), bf16[128,88,128]{2,1,0:T(8,128)(2,1)}, u32[]{:S(2)}, u32[]{:S(2)}) async-start(bf16[128,88,128]{2,1,0:T(8,128)(2,1)} %shard_map.240), calls=%async_computation.1 | async-start | bytes 5767168 | tf_op jit(solution)/shard_map/all_to_all | solution.py:296
  19.8 2.7 %shard_map.238 = bf16[64,128,128]{2,1,0:T(8,128)(2,1)} custom-call(s32[32]{0:T(128)S(1)} %bitcast.13, bf16[32,128,128]{2,1,0:T(8,128)(2,1)S(1)} %copy-done.1), custom_call_target="tpu_custom_call" | custom-call | bytes 3145728 | tf_op jit(solution)/shard_map/pallas_call | solution.py:91
  22.5 0.1 concatenate.3
  22.7 3.6 %gather_fusion = bf16[896,1024]{1,0:T(8,128)(2,1)S(1)} fusion(bf16[480,1024]{1,0:T(8,128)(2,1)S(1)} %concatenate.3, s32[1024]{0:T(1024)S(1)} %pad_clamp_fusion), kind=kCustom, calls=%fused_computation | custom fusion | bytes 3673600 | tf_op jit(solution)/shard_map/jit(_take)/gather | solution.py:374
  26.4 0.5 fusion.5
  26.9 0.2 fusion.6.bottom
  27.1 31.1 %all-to-all-done.1.recv = bf16[128,88,128]{2,1,0:T(8,128)(2,1)} async-done(((bf16[128,88,128]{2,1,0:T(8,128)(2,1)}), bf16[128,88,128]{2,1,0:T(8,128)(2,1)}, u32[]{:S(2)}, u32[]{:S(2)}) %all-to-all-start.1) | async-done | bytes 2883616 | tf_op jit(solution)/shard_map/all_to_all | solution.py:296
  58.3 4.8 %all-to-all-start = ((bf16[64,128,128]{2,1,0:T(8,128)(2,1)}), bf16[64,128,128]{2,1,0:T(8,128)(2,1)}, u32[]{:S(2)}, u32[]{:S(2)}) async-start(bf16[64,128,128]{2,1,0:T(8,128)(2,1)} %shard_map.238), calls=%async_computation | async-start | bytes 4194304 | tf_op jit(solution)/shard_map/all_to_all | solution.py:296
  63.7 15.4 %shard_map.241 = (f32[1,512]{1,0:T(1,128)}, f32[1,128]{1,0:T(1,128)S(1)}) custom-call(s32[8,128]{1,0:T(8,128)S(1)} %copy-done.5, bf16[128,88,128]{2,1,0:T(8,128)(2,1)} %all-to-all-done.1.recv, f32[512,128]{1,0:T(8,128)S(1)} %fusion.6.bottom, bf16[896,1024]{1,0:T(8,128)(2,1)S(1)} %gather_fusion, f32[1,1024]{1,0:T(1,128)S(1)} %bitcast.14, ...), custom_call_target="tpu_custom_call" | custom-call | flops 6442450944 | bytes 5242880 | tf_op jit(solution)/shard_map/pallas_call | solution.py:271
  79.1 0.6 collective-permute-start
  79.7 3.0 %collective-permute-done = f32[1,128]{1,0:T(1,128)S(1)} collective-permute-done((f32[1,128]{1,0:T(1,128)S(1)}, f32[1,128]{1,0:T(1,128)S(1)}, u32[]{:S(2)}, u32[]{:S(2)}) %collective-permute-start) | collective-permute-done | bytes 544 | tf_op jit(solution)/shard_map/ppermute | solution.py:302
  82.7 1.0 collective-permute-start.1
  83.7 3.7 %collective-permute-done.1 = f32[1,128]{1,0:T(1,128)S(1)} collective-permute-done((f32[1,128]{1,0:T(1,128)S(1)}, f32[1,128]{1,0:T(1,128)S(1)}, u32[]{:S(2)}, u32[]{:S(2)}) %collective-permute-start.1) | collective-permute-done | bytes 544 | tf_op jit(solution)/shard_map/ppermute | solution.py:302
  87.5 1.1 collective-permute-done.2
  88.6 1.6 collective-permute-start.3
  90.2 1.9 %collective-permute-done.3 = f32[1,128]{1,0:T(1,128)S(1)} collective-permute-done((f32[1,128]{1,0:T(1,128)S(1)}, f32[1,128]{1,0:T(1,128)S(1)}, u32[]{:S(2)}, u32[]{:S(2)}) %collective-permute-start.3) | collective-permute-done | bytes 544 | tf_op jit(solution)/shard_map/ppermute | solution.py:302
  92.1 2.8 %collective-permute-start.4 = (f32[1,128]{1,0:T(1,128)S(1)}, f32[1,128]{1,0:T(1,128)S(1)}, u32[]{:S(2)}, u32[]{:S(2)}) collective-permute-start(f32[1,128]{1,0:T(1,128)S(1)} %add.66), channel_id=1, source_target_pairs={{0,6},{1,7},{2,4},{3,5},{4,2},{5,3},{6,0},{7,1},{8,14},{9,15},{10,... | collective-permute-start | bytes 1544 | tf_op jit(solution)/shard_map/ppermute | solution.py:302
  95.0 64.7 %shard_map.239 = bf16[64,128,128]{2,1,0:T(8,128)(2,1)} custom-call(bf16[64,128,128]{2,1,0:T(8,128)(2,1)} %all-to-all-done.given), custom_call_target="tpu_custom_call" | custom-call | bytes 4194304 | tf_op jit(solution)/shard_map/pallas_call | solution.py:319
  159.7 1.6 collective-permute-start.5
  161.3 2.0 %collective-permute-done.5 = f32[1,128]{1,0:T(1,128)S(1)} collective-permute-done((f32[1,128]{1,0:T(1,128)S(1)}, f32[1,128]{1,0:T(1,128)S(1)}, u32[]{:S(2)}, u32[]{:S(2)}) %collective-permute-start.5) | collective-permute-done | bytes 544 | tf_op jit(solution)/shard_map/ppermute | solution.py:302
  163.3 2.8 %collective-permute-start.6 = (f32[1,128]{1,0:T(1,128)S(1)}, f32[1,128]{1,0:T(1,128)S(1)}, u32[]{:S(2)}, u32[]{:S(2)}) collective-permute-start(f32[1,128]{1,0:T(1,128)S(1)} %add.68), channel_id=1, source_target_pairs={{0,24},{1,25},{2,26},{3,27},{4,28},{5,29},{6,30},{7,31},{8,16},{9,... | collective-permute-start | bytes 1544 | tf_op jit(solution)/shard_map/ppermute | solution.py:302
  166.2 1.9 %collective-permute-done.6 = f32[1,128]{1,0:T(1,128)S(1)} collective-permute-done((f32[1,128]{1,0:T(1,128)S(1)}, f32[1,128]{1,0:T(1,128)S(1)}, u32[]{:S(2)}, u32[]{:S(2)}) %collective-permute-start.6) | collective-permute-done | bytes 544 | tf_op jit(solution)/shard_map/ppermute | solution.py:302
  168.1 0.5 add.69
  (42 shorter events, 0.2 us)
Async XLA Ops:
  0.6 25.7 %copy-start = (bf16[512,256]{1,0:T(8,128)(2,1)S(1)}, bf16[512,256]{1,0:T(8,128)(2,1)}, u32[]{:S(2)}) copy-start(bf16[512,256]{1,0:T(8,128)(2,1)} %param.36) | copy-start | bytes 786436
  8.1 11.7 %copy-start.1 = (bf16[32,128,128]{2,1,0:T(8,128)(2,1)S(1)}, bf16[32,128,128]{2,1,0:T(8,128)(2,1)}, u32[]{:S(2)}) copy-start(bf16[32,128,128]{2,1,0:T(8,128)(2,1)} %refs_1_.1) | copy-start | bytes 3145732
  8.1 11.7 %copy-start.2 = (s32[32,1]{0,1:T(1,128)S(1)}, s32[32,1]{0,1:T(1,128)}, u32[]{:S(2)}) copy-start(s32[32,1]{0,1:T(1,128)} %param.31) | copy-start | bytes 388
  8.1 50.1 %all-to-all-start.1 = ((bf16[128,88,128]{2,1,0:T(8,128)(2,1)}), bf16[128,88,128]{2,1,0:T(8,128)(2,1)}, u32[]{:S(2)}, u32[]{:S(2)}) async-start(bf16[128,88,128]{2,1,0:T(8,128)(2,1)} %shard_map.240), calls=%async_computation.1 | async-start | bytes 5767168 | tf_op jit(solution)/shard_map/all_to_all | solution.py:296
  19.8 2.7 %copy-start.6 = (bf16[479,1024]{1,0:T(8,128)(2,1)S(1)}, bf16[479,1024]{1,0:T(8,128)(2,1)}, u32[]{:S(2)}) copy-start(bf16[479,1024]{1,0:T(8,128)(2,1)} %param.40) | copy-start | bytes 2942980
  19.8 2.8 %copy-start.8 = (s32[896]{0:T(1024)S(1)}, s32[896]{0:T(1024)}, u32[]{:S(2)}) copy-start(s32[896]{0:T(1024)} %constant.50) | copy-start | bytes 10756
  22.6 3.7 %copy-start.9 = (bf16[1024,1]{0,1:T(2,128)(2,1)S(1)}, bf16[1024,1]{0,1:T(2,128)(2,1)}, u32[]{:S(2)}) copy-start(bf16[1024,1]{0,1:T(2,128)(2,1)} %param.42) | copy-start | bytes 6148
  22.6 3.7 %copy-start.11 = (bf16[512,13]{0,1:T(8,128)(2,1)S(1)}, bf16[512,13]{0,1:T(8,128)(2,1)}, u32[]{:S(2)}) copy-start(bf16[512,13]{0,1:T(8,128)(2,1)} %param.32) | copy-start | bytes 39940
  22.6 3.7 %copy-start.12 = (bf16[13,512]{1,0:T(8,128)(2,1)S(1)}, bf16[13,512]{1,0:T(8,128)(2,1)}, u32[]{:S(2)}) copy-start(bf16[13,512]{1,0:T(8,128)(2,1)} %param.34) | copy-start | bytes 39940
  22.6 3.7 %copy-start.13 = (f32[512]{0:T(512)S(1)}, f32[512]{0:T(512)}, u32[]{:S(2)}) copy-start(f32[512]{0:T(512)} %param.35) | copy-start | bytes 6148
  22.6 3.7 %copy-start.14 = (f32[256]{0:T(256)S(1)}, f32[256]{0:T(256)}, u32[]{:S(2)}) copy-start(f32[256]{0:T(256)} %param.37) | copy-start | bytes 3076
  22.6 4.2 %copy-start.7 = (bf16[256,128]{1,0:T(8,128)(2,1)S(1)}, bf16[256,128]{1,0:T(8,128)(2,1)}, u32[]{:S(2)}) copy-start(bf16[256,128]{1,0:T(8,128)(2,1)} %param.38) | copy-start | bytes 196612
  22.7 4.2 %copy-start.10 = (f32[128]{0:T(128)S(1)}, f32[128]{0:T(128)}, u32[]{:S(2)}) copy-start(f32[128]{0:T(128)} %param.39) | copy-start | bytes 1540
  27.1 36.6 %copy-start.3 = (f32[1024]{0:T(1024)S(1)}, f32[1024]{0:T(1024)}, u32[]{:S(2)}) copy-start(f32[1024]{0:T(1024)} %param.41) | copy-start | bytes 12292
  27.1 36.6 %copy-start.4 = (s32[512]{0:T(512)S(1)}, s32[512]{0:T(512)}, u32[]{:S(2)}) copy-start(s32[512]{0:T(512)} %param.33) | copy-start | bytes 6148
  27.1 36.6 %copy-start.5 = (s32[8,128]{1,0:T(8,128)S(1)}, s32[8,128]{1,0:T(8,128)}, u32[]{:S(2)}) copy-start(s32[8,128]{1,0:T(8,128)} %constant.30.clone.label) | copy-start | bytes 12292
  58.3 36.7 %all-to-all-start = ((bf16[64,128,128]{2,1,0:T(8,128)(2,1)}), bf16[64,128,128]{2,1,0:T(8,128)(2,1)}, u32[]{:S(2)}, u32[]{:S(2)}) async-start(bf16[64,128,128]{2,1,0:T(8,128)(2,1)} %shard_map.238), calls=%async_computation | async-start | bytes 4194304 | tf_op jit(solution)/shard_map/all_to_all | solution.py:296
  79.1 3.5 %collective-permute-start = (f32[1,128]{1,0:T(1,128)S(1)}, f32[1,128]{1,0:T(1,128)S(1)}, u32[]{:S(2)}, u32[]{:S(2)}) collective-permute-start(f32[1,128]{1,0:T(1,128)S(1)} %get-tuple-element.15), channel_id=1, source_target_pairs={{0,32},{32,0},{64,96},{96,64},{1,33},{33,1},{65,97},{97,65},{2,34}... | collective-permute-start | bytes 1544 | tf_op jit(solution)/shard_map/ppermute | solution.py:302
  82.7 4.8 %collective-permute-start.1 = (f32[1,128]{1,0:T(1,128)S(1)}, f32[1,128]{1,0:T(1,128)S(1)}, u32[]{:S(2)}, u32[]{:S(2)}) collective-permute-start(f32[1,128]{1,0:T(1,128)S(1)} %add.63), channel_id=1, source_target_pairs={{0,96},{32,64},{64,32},{96,0},{1,97},{33,65},{65,33},{97,1},{2,98}... | collective-permute-start | bytes 1544 | tf_op jit(solution)/shard_map/ppermute | solution.py:302
  87.4 1.1 collective-permute-start.2
  88.6 3.5 %collective-permute-start.3 = (f32[1,128]{1,0:T(1,128)S(1)}, f32[1,128]{1,0:T(1,128)S(1)}, u32[]{:S(2)}, u32[]{:S(2)}) collective-permute-start(f32[1,128]{1,0:T(1,128)S(1)} %add.65), channel_id=1, source_target_pairs={{0,2},{1,3},{2,0},{3,1},{4,6},{5,7},{6,4},{7,5},{8,10},{9,11},{10,... | collective-permute-start | bytes 1544 | tf_op jit(solution)/shard_map/ppermute | solution.py:302
  92.1 67.6 %collective-permute-start.4 = (f32[1,128]{1,0:T(1,128)S(1)}, f32[1,128]{1,0:T(1,128)S(1)}, u32[]{:S(2)}, u32[]{:S(2)}) collective-permute-start(f32[1,128]{1,0:T(1,128)S(1)} %add.66), channel_id=1, source_target_pairs={{0,6},{1,7},{2,4},{3,5},{4,2},{5,3},{6,0},{7,1},{8,14},{9,15},{10,... | collective-permute-start | bytes 1544 | tf_op jit(solution)/shard_map/ppermute | solution.py:302
  159.7 3.6 %collective-permute-start.5 = (f32[1,128]{1,0:T(1,128)S(1)}, f32[1,128]{1,0:T(1,128)S(1)}, u32[]{:S(2)}, u32[]{:S(2)}) collective-permute-start(f32[1,128]{1,0:T(1,128)S(1)} %add.67), channel_id=1, source_target_pairs={{0,8},{1,9},{2,10},{3,11},{4,12},{5,13},{6,14},{7,15},{8,0},{9,1},... | collective-permute-start | bytes 1544 | tf_op jit(solution)/shard_map/ppermute | solution.py:302
  163.3 4.8 %collective-permute-start.6 = (f32[1,128]{1,0:T(1,128)S(1)}, f32[1,128]{1,0:T(1,128)S(1)}, u32[]{:S(2)}, u32[]{:S(2)}) collective-permute-start(f32[1,128]{1,0:T(1,128)S(1)} %add.68), channel_id=1, source_target_pairs={{0,24},{1,25},{2,26},{3,27},{4,28},{5,29},{6,30},{7,31},{8,16},{9,... | collective-permute-start | bytes 1544 | tf_op jit(solution)/shard_map/ppermute | solution.py:302

commit v4 on v3

--- a/solution.py
+++ b/solution.py
@@ -100,10 +100,18 @@
 
 
 def pool_kernel(*refs):
-    given, out, (wide, sam), held, sem = refs[:8], refs[8], refs[9:11], refs[11:19], refs[19]
-    copies = [pltpu.make_async_copy(g, h, sem.at[n]) for n, (g, h) in enumerate(zip(given, held))]
-    for copy in copies:
-        copy.start()
+    given, out, (wide, sam, ready), held, sem, sent = refs[:8], refs[8], refs[9:12], refs[12:20], refs[20], refs[21]
+    cuts = [(n, None) for n in range(2, 8)] + [(0, (0, 12)), (0, (26, 38)), (1, (0, 12))]
+    cuts = [cuts, [(0, (12, 26)), (0, (38, 48)), (1, (12, 32))]]
+    waves = []
+    for wave in cuts:
+        copies = []
+        for n, cut in wave:
+            at = pl.ds(cut[0], cut[1] - cut[0]) if cut else pl.ds(0, given[n].shape[0])
+            number = len(copies) + 9 * len(waves)
+            copies.append(pltpu.make_async_copy(given[n].at[at], held[n].at[at], sem.at[number]))
+            copies[-1].start()
+        waves.append(copies)
     home, orphan = (held[0],) + tuple(held[2:5]), (held[1],) + tuple(held[5:8])
     me = lax.axis_index("hst") * lax.axis_size("chip") + lax.axis_index("chip")
     rows = lax.broadcasted_iota(jnp.int32, (128, 128), 0).astype(F32).astype(BF)
@@ -112,7 +120,7 @@
     sam[...] = jnp.full(sam.shape, NONE, jnp.int32)
     for s in range(SLOTS + 2, ROWS):
         wide[pl.ds(s, 128, stride=ROWS), :] = jnp.zeros((128, 128), F32)
-    for copy in copies:
+    for copy in waves[0]:
         copy.wait()
 
     def piece(slot, b, blocks, off, length, samples):
@@ -142,7 +150,10 @@
         return 0
 
     both = HOME // 2 - PERIOD
-    lax.fori_loop(0, both, step, 0, unroll=2)
+    lax.fori_loop(0, 6, step, 0, unroll=3)
+    for copy in waves[1]:
+        copy.wait()
+    lax.fori_loop(6, both, step, 0, unroll=5)
     for k in range(both, PERIOD):
         pair(k, False)
     rest = [lax.rem(4 + 3 * me + i, PERIOD) for i in range(3)]
@@ -155,11 +166,22 @@
     wide[pl.ds(SLOTS, 128, stride=ROWS), :] = (index >> 4).astype(F32).T
     wide[pl.ds(SLOTS + 1, 128, stride=ROWS), :] = (index & 15).astype(F32).T
 
-    def narrow(q, _):
-        out[pl.ds(4 * q, 4)] = wide[pl.ds(4 * q * ROWS, 4 * ROWS), :].reshape(4, ROWS, 128).astype(BF)
-        return 0
-
-    lax.fori_loop(0, 32, narrow, 0, unroll=2)
+    parts = sent.shape[0]
+    span = 128 // parts
+    copies = []
+    for n in range(parts):
+
+        def narrow(q, _):
+            q = span // 4 * n + q
+            ready[pl.ds(4 * q, 4)] = wide[pl.ds(4 * q * ROWS, 4 * ROWS), :].reshape(4, ROWS, 128).astype(BF)
+            return 0
+
+        lax.fori_loop(0, span // 4, narrow, 0, unroll=2)
+        at = pl.ds(span * n, span)
+        copies.append(pltpu.make_async_copy(ready.at[at], out.at[at], sent.at[n]))
+        copies[-1].start()
+    for copy in copies:
+        copy.wait()
 
 
 def pool(*arrays):
@@ -167,16 +189,32 @@
         pool_kernel,
         out_shape=jax.ShapeDtypeStruct((128, ROWS, 128), BF),
         in_specs=[pl.BlockSpec(memory_space=pl.ANY)] * 8,
-        out_specs=VMEM,
-        scratch_shapes=[pltpu.VMEM((128 * ROWS, 128), F32), pltpu.VMEM((128, 128), jnp.int32)]
+        out_specs=pl.BlockSpec(memory_space=pl.ANY),
+        scratch_shapes=[
+            pltpu.VMEM((128 * ROWS, 128), F32),
+            pltpu.VMEM((128, 128), jnp.int32),
+            pltpu.VMEM((128, ROWS, 128), BF),
+        ]
         + [pltpu.VMEM(a.shape, a.dtype) for a in arrays]
-        + [pltpu.SemaphoreType.DMA((8,))],
+        + [pltpu.SemaphoreType.DMA((12,)), pltpu.SemaphoreType.DMA((4,))],
         compiler_params=pltpu.CompilerParams(vmem_limit_bytes=60 << 20),
         cost_estimate=pl.CostEstimate(flops=84 * 128 * 128 * 256, transcendentals=0, bytes_accessed=6 << 20),
     )(*arrays)
 
 
-def tail_kernel(label, recv, bottom, weights, bias, last, last_bias, marks, logits, loss, wide, hi, lo, stack, turned, packed):
+def tail_kernel(
+    label, given, bottom, given_weights, bias, last, last_bias, marks, logits, loss,
+    wide, hi, lo, stack, turned, packed, recv, weights, came, sem,
+):
+    parts = came.shape[0]
+    span = 128 // parts
+    copies = []
+    for n in range(parts):
+        at = pl.ds(span * n, span)
+        copies.append(pltpu.make_async_copy(given.at[at], recv.at[at], came.at[n]))
+        copies[-1].start()
+    fetch = pltpu.make_async_copy(given_weights, weights, sem)
+    fetch.start()
     zero = jnp.zeros((), BF)
     ones = lax.broadcasted_iota(jnp.int32, (16, 128), 0).astype(F32).astype(BF)
 
@@ -184,7 +222,9 @@
         wide[pl.ds(4 * p * ROWS, 4 * ROWS), :] = recv[pl.ds(4 * p, 4)].astype(F32).reshape(4 * ROWS, 128)
         return 0
 
-    lax.fori_loop(0, 32, widen, 0, unroll=2)
+    for n in range(parts):
+        copies[n].wait()
+        lax.fori_loop(span // 4 * n, span // 4 * (n + 1), widen, 0, unroll=2)
     hi[...] = wide[pl.ds(SLOTS, 128, stride=ROWS), :].T
     lo[...] = wide[pl.ds(SLOTS + 1, 128, stride=ROWS), :].T
 
@@ -255,6 +295,7 @@
 
     lax.fori_loop(0, BATCH // 16, interact, 0, unroll=4)
 
+    fetch.wait()
     for m in range(4):
         at = pl.ds(128 * m, 128)
         hidden = jnp.dot(packed[at, :], weights[...], preferred_element_type=F32)
@@ -271,7 +312,7 @@
     return pl.pallas_call(
         tail_kernel,
         out_shape=(jax.ShapeDtypeStruct((1, BATCH), F32), jax.ShapeDtypeStruct((1, 128), F32)),
-        in_specs=[VMEM] * 6 + [SMEM, VMEM],
+        in_specs=[VMEM, pl.BlockSpec(memory_space=pl.ANY)] * 2 + [VMEM, VMEM, SMEM, VMEM],
         out_specs=(VMEM, VMEM),
         scratch_shapes=[
             pltpu.VMEM((128 * ROWS, 128), F32),
@@ -280,8 +321,12 @@
             pltpu.VMEM((F + 1, BATCH, 128), F32),
             pltpu.VMEM((32 * BATCH, 128), F32),
             pltpu.VMEM((BATCH, QW), BF),
+            pltpu.VMEM((128, ROWS, 128), BF),
+            pltpu.VMEM((QW, 1024), BF),
+            pltpu.SemaphoreType.DMA((4,)),
+            pltpu.SemaphoreType.DMA,
         ],
-        compiler_params=pltpu.CompilerParams(vmem_limit_bytes=40 << 20),
+        compiler_params=pltpu.CompilerParams(vmem_limit_bytes=60 << 20),
         cost_estimate=pl.CostEstimate(flops=6 << 30, transcendentals=0, bytes_accessed=5 << 20),
     )(label, recv, bottom, weights, bias, last, last_bias, marks)
 
@@ -303,25 +348,18 @@
     return value
 
 
-def keep_kernel(given, out, sems):
-    part = given.shape[0] // sems.shape[0]
-    copies = []
-    for n in range(sems.shape[0]):
-        at = pl.ds(n * part, part)
-        copies.append(pltpu.make_async_copy(given.at[at], out.at[at], sems.at[n]))
-    for copy in copies:
-        copy.start()
-    for copy in copies:
-        copy.wait()
+def keep_kernel(given, out):
+    out[...] = given[...]
 
 
 def keep(value):
+    block = pl.BlockSpec((8,) + value.shape[1:], lambda n: (n, 0, 0))
     return pl.pallas_call(
         keep_kernel,
+        grid=(value.shape[0] // 8,),
         out_shape=jax.ShapeDtypeStruct(value.shape, value.dtype),
-        in_specs=[pl.BlockSpec(memory_space=pl.ANY)],
-        out_specs=pl.BlockSpec(memory_space=pl.ANY),
-        scratch_shapes=[pltpu.SemaphoreType.DMA((8,))],
+        in_specs=[block],
+        out_specs=block,
         compiler_params=pltpu.CompilerParams(vmem_limit_bytes=60 << 20),
         cost_estimate=pl.CostEstimate(flops=0, transcendentals=0, bytes_accessed=4 << 20),
     )(value)

time: 169 us -> 111 us (0.66)
  Pallas kernels: 90.3 us -> 31.1 us
  local copies, waits for them, and re-layouts: 3.78 us -> 6.27 us
  waiting for transfers between devices: 44.8 us -> 43.1 us
    pallas_call x1, Pallas kernels: 64.7 us -> 5.63 us  [keep(): pl.pallas_call(keep_kernel, grid=(value.shape[0] // 8,), out_shape=jax.Sh...]
    all_to_all x2, waiting for transfers between devices: 31.1 us -> 29.3 us  [exchange(): return lax.all_to_all(value, axes, split_axis=0, concat_axis=0, tiled=True)]
  transfers between devices with their start and end apart: 9 -> 9, of which waited for: 7 -> 7; matrix products, arithmetic and copies ran while one was open for 3% -> 6% of each run, Pallas kernels for 49% -> 22%
where the time goes in v4:
time: 111 us
  waiting for transfers between devices  43.1 us (39%)
  Pallas kernels  31.1 us (28%)
  starting transfers between devices  26.3 us (24%)
  local copies, waits for them, and re-layouts  6.27 us (6%)
  between operations  1.52 us (1%)
  matrix products  1.4 us (1%)
  other arithmetic  1.21 us (1%)
    all_to_all x2, waiting for transfers between devices, exchange(): return lax.all_to_all(value, axes, split_axis=0, concat_axis=0, tiled=True)  29.3 us
    pallas_call x1, Pallas kernels, tail(): pl.pallas_call(tail_kernel, out_shape=(jax.ShapeDtypeStruct((1, BATCH), F...  16.2 us
    all_to_all x2, starting transfers between devices, exchange(): return lax.all_to_all(value, axes, split_axis=0, concat_axis=0, tiled=True)  15.6 us
    ppermute x6, waiting for transfers between devices, ring_sum(): value = value + lax.ppermute(value, axis, pairs)  12.6 us
    ppermute x6, starting transfers between devices, ring_sum(): value = value + lax.ppermute(value, axis, pairs)  10.7 us
    pallas_call x1, Pallas kernels, pool(): pl.pallas_call(pool_kernel, out_shape=jax.ShapeDtypeStruct((128, ROWS, 12...  6.62 us
    pallas_call x1, Pallas kernels, keep(): pl.pallas_call(keep_kernel, grid=(value.shape[0] // 8,), out_shape=jax.Sh...  5.63 us
    gather x1, local copies, waits for them, and re-layouts, per_device(): weights = jnp.take(padded, jnp.asarray(FEATURE_ROWS), axis=0)  4.19 us
  transfers between devices with their start and end apart: 9, of which 7 were waited for; matrix products, arithmetic and copies ran while one was open for 6% of the time, Pallas kernels for 22%

profile of v4, /device:TPU:0, one launch (start us, length us, event | category | flops | bytes accessed | tf_op | source)
XLA Modules:
  0.0 110.9 jit_solution(10082318170533742114)
XLA Ops:
  0.6 6.6 %shard_map.240 = bf16[128,88,128]{2,1,0:T(8,128)(2,1)} custom-call(bf16[48,128,128]{2,1,0:T(8,128)(2,1)} %refs_0_.1, bf16[32,128,128]{2,1,0:T(8,128)(2,1)} %refs_1_.1, s32[48,8,128]{2,1,0:T(8,128)} %bitcast.14, s32[48,128]{1,0:T(8,128)} %refs_3_.1, s32[48,128]{1,0:T(8,128)} %refs_4_.1, s32[32,8,128]{2,1,0:T(8,128)} %bitcast.15, s32[32,128]{1,0:T(8,128)} %refs_6_.1, ...), custom_call_target="tpu_custom_call" | custom-call | flops 352321536 | bytes 6291456 | tf_op jit(solution)/shard_map/pallas_call | solution.py:188
  7.3 11.6 %all-to-all-start.1 = ((bf16[128,88,128]{2,1,0:T(8,128)(2,1)}), bf16[128,88,128]{2,1,0:T(8,128)(2,1)}, u32[]{:S(2)}, u32[]{:S(2)}) async-start(bf16[128,88,128]{2,1,0:T(8,128)(2,1)} %shard_map.240), calls=%async_computation.1 | async-start | bytes 5767168 | tf_op jit(solution)/shard_map/all_to_all | solution.py:341
  19.0 2.7 %shard_map.238 = bf16[64,128,128]{2,1,0:T(8,128)(2,1)} custom-call(s32[32]{0:T(128)S(1)} %bitcast.13, bf16[32,128,128]{2,1,0:T(8,128)(2,1)S(1)} %copy-done.1), custom_call_target="tpu_custom_call" | custom-call | bytes 3145728 | tf_op jit(solution)/shard_map/pallas_call | solution.py:91
  21.8 4.2 %gather_fusion = bf16[896,1024]{1,0:T(8,128)(2,1)} fusion(bf16[480,1024]{1,0:T(8,128)(2,1)S(1)} %concatenate.3, s32[1024]{0:T(1024)S(1)} %pad_clamp_fusion), kind=kCustom, calls=%fused_computation | custom fusion | bytes 3673600 | tf_op jit(solution)/shard_map/jit(_take)/gather | solution.py:412
  26.6 0.9 fusion.6.bottom
  27.5 0.6 broadcast_in_dim.33.last
  28.1 29.3 %all-to-all-done.1.given = bf16[128,88,128]{2,1,0:T(8,128)(2,1)} async-done(((bf16[128,88,128]{2,1,0:T(8,128)(2,1)}), bf16[128,88,128]{2,1,0:T(8,128)(2,1)}, u32[]{:S(2)}, u32[]{:S(2)}) %all-to-all-start.1) | async-done | bytes 2883616 | tf_op jit(solution)/shard_map/all_to_all | solution.py:341
  57.4 4.0 %all-to-all-start = ((bf16[64,128,128]{2,1,0:T(8,128)(2,1)}), bf16[64,128,128]{2,1,0:T(8,128)(2,1)S(1)}, u32[]{:S(2)}, u32[]{:S(2)}) async-start(bf16[64,128,128]{2,1,0:T(8,128)(2,1)} %shard_map.238), calls=%async_computation | async-start | bytes 4194304 | tf_op jit(solution)/shard_map/all_to_all | solution.py:341
  62.1 16.2 %shard_map.241 = (f32[1,512]{1,0:T(1,128)}, f32[1,128]{1,0:T(1,128)}) custom-call(s32[8,128]{1,0:T(8,128)} %constant.30.clone.label, bf16[128,88,128]{2,1,0:T(8,128)(2,1)} %all-to-all-done.1.given, f32[512,128]{1,0:T(8,128)} %fusion.6.bottom, bf16[896,1024]{1,0:T(8,128)(2,1)} %gather_fusion, f32[1,1024]{1,0:T(1,128)} %bitcast.16, ...), custom_call_target="tpu_custom_call" | custom-call | flops 6442450944 | bytes 5242880 | tf_op jit(solution)/shard_map/pallas_call | solution.py:312
  78.3 0.6 collective-permute-start
  78.9 3.1 %collective-permute-done = f32[1,128]{1,0:T(1,128)S(1)} collective-permute-done((f32[1,128]{1,0:T(1,128)}, f32[1,128]{1,0:T(1,128)S(1)}, u32[]{:S(2)}, u32[]{:S(2)}) %collective-permute-start) | collective-permute-done | bytes 544 | tf_op jit(solution)/shard_map/ppermute | solution.py:347
  82.0 0.7 add.63
  82.7 1.0 collective-permute-start.1
  83.7 3.7 %collective-permute-done.1 = f32[1,128]{1,0:T(1,128)S(1)} collective-permute-done((f32[1,128]{1,0:T(1,128)S(1)}, f32[1,128]{1,0:T(1,128)S(1)}, u32[]{:S(2)}, u32[]{:S(2)}) %collective-permute-start.1) | collective-permute-done | bytes 544 | tf_op jit(solution)/shard_map/ppermute | solution.py:347
  87.4 1.1 %collective-permute-done.2 = f32[1,128]{1,0:T(1,128)S(1)} collective-permute-done((f32[1,128]{1,0:T(1,128)S(1)}, f32[1,128]{1,0:T(1,128)S(1)}, u32[]{:S(2)}, u32[]{:S(2)}) %collective-permute-start.2) | collective-permute-done | bytes 544 | tf_op jit(solution)/shard_map/ppermute | solution.py:427
  88.6 1.7 %collective-permute-start.3 = (f32[1,128]{1,0:T(1,128)S(1)}, f32[1,128]{1,0:T(1,128)S(1)}, u32[]{:S(2)}, u32[]{:S(2)}) collective-permute-start(f32[1,128]{1,0:T(1,128)S(1)} %add.65), channel_id=1, source_target_pairs={{0,2},{1,3},{2,0},{3,1},{4,6},{5,7},{6,4},{7,5},{8,10},{9,11},{10,... | collective-permute-start | bytes 1544 | tf_op jit(solution)/shard_map/ppermute | solution.py:347
  90.3 1.9 %collective-permute-done.3 = f32[1,128]{1,0:T(1,128)S(1)} collective-permute-done((f32[1,128]{1,0:T(1,128)S(1)}, f32[1,128]{1,0:T(1,128)S(1)}, u32[]{:S(2)}, u32[]{:S(2)}) %collective-permute-start.3) | collective-permute-done | bytes 544 | tf_op jit(solution)/shard_map/ppermute | solution.py:347
  92.1 2.9 %collective-permute-start.4 = (f32[1,128]{1,0:T(1,128)S(1)}, f32[1,128]{1,0:T(1,128)S(1)}, u32[]{:S(2)}, u32[]{:S(2)}) collective-permute-start(f32[1,128]{1,0:T(1,128)S(1)} %add.66), channel_id=1, source_target_pairs={{0,6},{1,7},{2,4},{3,5},{4,2},{5,3},{6,0},{7,1},{8,14},{9,15},{10,... | collective-permute-start | bytes 1544 | tf_op jit(solution)/shard_map/ppermute | solution.py:347
  95.0 1.3 %copy-done.3 = bf16[64,128,128]{2,1,0:T(8,128)(2,1)} copy-done((bf16[64,128,128]{2,1,0:T(8,128)(2,1)}, bf16[64,128,128]{2,1,0:T(8,128)(2,1)S(1)}, u32[]{:S(2)}) %copy-start.3) | copy-done | bytes 2097176
  96.4 5.6 %shard_map.239 = bf16[64,128,128]{2,1,0:T(8,128)(2,1)} custom-call(bf16[64,128,128]{2,1,0:T(8,128)(2,1)} %copy-done.3), custom_call_target="tpu_custom_call" | custom-call | bytes 4194304 | tf_op jit(solution)/shard_map/pallas_call | solution.py:357
  102.0 1.6 %collective-permute-start.5 = (f32[1,128]{1,0:T(1,128)S(1)}, f32[1,128]{1,0:T(1,128)S(1)}, u32[]{:S(2)}, u32[]{:S(2)}) collective-permute-start(f32[1,128]{1,0:T(1,128)S(1)} %add.67), channel_id=1, source_target_pairs={{0,8},{1,9},{2,10},{3,11},{4,12},{5,13},{6,14},{7,15},{8,0},{9,1},... | collective-permute-start | bytes 1544 | tf_op jit(solution)/shard_map/ppermute | solution.py:347
  103.6 2.0 %collective-permute-done.5 = f32[1,128]{1,0:T(1,128)S(1)} collective-permute-done((f32[1,128]{1,0:T(1,128)S(1)}, f32[1,128]{1,0:T(1,128)S(1)}, u32[]{:S(2)}, u32[]{:S(2)}) %collective-permute-start.5) | collective-permute-done | bytes 544 | tf_op jit(solution)/shard_map/ppermute | solution.py:347
  105.6 2.8 %collective-permute-start.6 = (f32[1,128]{1,0:T(1,128)S(1)}, f32[1,128]{1,0:T(1,128)S(1)}, u32[]{:S(2)}, u32[]{:S(2)}) collective-permute-start(f32[1,128]{1,0:T(1,128)S(1)} %add.68), channel_id=1, source_target_pairs={{0,24},{1,25},{2,26},{3,27},{4,28},{5,29},{6,30},{7,31},{8,16},{9,... | collective-permute-start | bytes 1544 | tf_op jit(solution)/shard_map/ppermute | solution.py:347
  108.5 1.9 %collective-permute-done.6 = f32[1,128]{1,0:T(1,128)S(1)} collective-permute-done((f32[1,128]{1,0:T(1,128)S(1)}, f32[1,128]{1,0:T(1,128)S(1)}, u32[]{:S(2)}, u32[]{:S(2)}) %collective-permute-start.6) | collective-permute-done | bytes 544 | tf_op jit(solution)/shard_map/ppermute | solution.py:347
  (38 shorter events, 1.2 us)
Async XLA Ops:
  0.6 25.4 %copy-start = (bf16[512,256]{1,0:T(8,128)(2,1)S(1)}, bf16[512,256]{1,0:T(8,128)(2,1)}, u32[]{:S(2)}) copy-start(bf16[512,256]{1,0:T(8,128)(2,1)} %param.36) | copy-start | bytes 786436
  7.3 11.7 %copy-start.1 = (bf16[32,128,128]{2,1,0:T(8,128)(2,1)S(1)}, bf16[32,128,128]{2,1,0:T(8,128)(2,1)}, u32[]{:S(2)}) copy-start(bf16[32,128,128]{2,1,0:T(8,128)(2,1)} %refs_1_.1) | copy-start | bytes 3145732
  7.3 11.7 %copy-start.2 = (s32[32,1]{0,1:T(1,128)S(1)}, s32[32,1]{0,1:T(1,128)}, u32[]{:S(2)}) copy-start(s32[32,1]{0,1:T(1,128)} %param.31) | copy-start | bytes 388
  7.3 50.1 %all-to-all-start.1 = ((bf16[128,88,128]{2,1,0:T(8,128)(2,1)}), bf16[128,88,128]{2,1,0:T(8,128)(2,1)}, u32[]{:S(2)}, u32[]{:S(2)}) async-start(bf16[128,88,128]{2,1,0:T(8,128)(2,1)} %shard_map.240), calls=%async_computation.1 | async-start | bytes 5767168 | tf_op jit(solution)/shard_map/all_to_all | solution.py:341
  18.9 2.7 %copy-start.4 = (bf16[479,1024]{1,0:T(8,128)(2,1)S(1)}, bf16[479,1024]{1,0:T(8,128)(2,1)}, u32[]{:S(2)}) copy-start(bf16[479,1024]{1,0:T(8,128)(2,1)} %param.40) | copy-start | bytes 2942980
  19.0 2.8 %copy-start.6 = (s32[896]{0:T(1024)S(1)}, s32[896]{0:T(1024)}, u32[]{:S(2)}) copy-start(s32[896]{0:T(1024)} %constant.50) | copy-start | bytes 10756
  21.7 4.3 %copy-start.7 = (bf16[1024,1]{0,1:T(2,128)(2,1)S(1)}, bf16[1024,1]{0,1:T(2,128)(2,1)}, u32[]{:S(2)}) copy-start(bf16[1024,1]{0,1:T(2,128)(2,1)} %param.42) | copy-start | bytes 6148
  21.8 4.3 %copy-start.9 = (bf16[512,13]{0,1:T(8,128)(2,1)S(1)}, bf16[512,13]{0,1:T(8,128)(2,1)}, u32[]{:S(2)}) copy-start(bf16[512,13]{0,1:T(8,128)(2,1)} %param.32) | copy-start | bytes 39940
  21.8 4.3 %copy-start.10 = (bf16[13,512]{1,0:T(8,128)(2,1)S(1)}, bf16[13,512]{1,0:T(8,128)(2,1)}, u32[]{:S(2)}) copy-start(bf16[13,512]{1,0:T(8,128)(2,1)} %param.34) | copy-start | bytes 39940
  21.8 4.3 %copy-start.11 = (f32[512]{0:T(512)S(1)}, f32[512]{0:T(512)}, u32[]{:S(2)}) copy-start(f32[512]{0:T(512)} %param.35) | copy-start | bytes 6148
  21.8 4.3 %copy-start.12 = (f32[256]{0:T(256)S(1)}, f32[256]{0:T(256)}, u32[]{:S(2)}) copy-start(f32[256]{0:T(256)} %param.37) | copy-start | bytes 3076
  21.8 4.8 %copy-start.5 = (bf16[256,128]{1,0:T(8,128)(2,1)S(1)}, bf16[256,128]{1,0:T(8,128)(2,1)}, u32[]{:S(2)}) copy-start(bf16[256,128]{1,0:T(8,128)(2,1)} %param.38) | copy-start | bytes 196612
  21.8 4.8 %copy-start.8 = (f32[128]{0:T(128)S(1)}, f32[128]{0:T(128)}, u32[]{:S(2)}) copy-start(f32[128]{0:T(128)} %param.39) | copy-start | bytes 1540
  57.4 37.6 %all-to-all-start = ((bf16[64,128,128]{2,1,0:T(8,128)(2,1)}), bf16[64,128,128]{2,1,0:T(8,128)(2,1)S(1)}, u32[]{:S(2)}, u32[]{:S(2)}) async-start(bf16[64,128,128]{2,1,0:T(8,128)(2,1)} %shard_map.238), calls=%async_computation | async-start | bytes 4194304 | tf_op jit(solution)/shard_map/all_to_all | solution.py:341
  78.3 3.8 %collective-permute-start = (f32[1,128]{1,0:T(1,128)}, f32[1,128]{1,0:T(1,128)S(1)}, u32[]{:S(2)}, u32[]{:S(2)}) collective-permute-start(f32[1,128]{1,0:T(1,128)} %get-tuple-element.15), channel_id=1, source_target_pairs={{0,32},{32,0},{64,96},{96,64},{1,33},{33,1},{65,97},{97,65},{2,34}... | collective-permute-start | bytes 1544 | tf_op jit(solution)/shard_map/ppermute | solution.py:347
  82.7 4.8 %collective-permute-start.1 = (f32[1,128]{1,0:T(1,128)S(1)}, f32[1,128]{1,0:T(1,128)S(1)}, u32[]{:S(2)}, u32[]{:S(2)}) collective-permute-start(f32[1,128]{1,0:T(1,128)S(1)} %add.63), channel_id=1, source_target_pairs={{0,96},{32,64},{64,32},{96,0},{1,97},{33,65},{65,33},{97,1},{2,98}... | collective-permute-start | bytes 1544 | tf_op jit(solution)/shard_map/ppermute | solution.py:347
  87.4 1.1 %collective-permute-start.2 = (f32[1,128]{1,0:T(1,128)S(1)}, f32[1,128]{1,0:T(1,128)S(1)}, u32[]{:S(2)}, u32[]{:S(2)}) collective-permute-start(f32[1,128]{1,0:T(1,128)S(1)} %add.64), channel_id=1, source_target_pairs={{0,1},{1,0},{2,3},{3,2},{4,5},{5,4},{6,7},{7,6},{8,9},{9,8},{10,11... | collective-permute-start | bytes 1544 | tf_op jit(solution)/shard_map/ppermute | solution.py:427
  88.6 3.5 %collective-permute-start.3 = (f32[1,128]{1,0:T(1,128)S(1)}, f32[1,128]{1,0:T(1,128)S(1)}, u32[]{:S(2)}, u32[]{:S(2)}) collective-permute-start(f32[1,128]{1,0:T(1,128)S(1)} %add.65), channel_id=1, source_target_pairs={{0,2},{1,3},{2,0},{3,1},{4,6},{5,7},{6,4},{7,5},{8,10},{9,11},{10,... | collective-permute-start | bytes 1544 | tf_op jit(solution)/shard_map/ppermute | solution.py:347
  92.1 9.9 %collective-permute-start.4 = (f32[1,128]{1,0:T(1,128)S(1)}, f32[1,128]{1,0:T(1,128)S(1)}, u32[]{:S(2)}, u32[]{:S(2)}) collective-permute-start(f32[1,128]{1,0:T(1,128)S(1)} %add.66), channel_id=1, source_target_pairs={{0,6},{1,7},{2,4},{3,5},{4,2},{5,3},{6,0},{7,1},{8,14},{9,15},{10,... | collective-permute-start | bytes 1544 | tf_op jit(solution)/shard_map/ppermute | solution.py:347
  95.0 1.3 %copy-start.3 = (bf16[64,128,128]{2,1,0:T(8,128)(2,1)}, bf16[64,128,128]{2,1,0:T(8,128)(2,1)S(1)}, u32[]{:S(2)}) copy-start(bf16[64,128,128]{2,1,0:T(8,128)(2,1)S(1)} %all-to-all-done.given) | copy-start | bytes 6291460
  102.0 3.6 %collective-permute-start.5 = (f32[1,128]{1,0:T(1,128)S(1)}, f32[1,128]{1,0:T(1,128)S(1)}, u32[]{:S(2)}, u32[]{:S(2)}) collective-permute-start(f32[1,128]{1,0:T(1,128)S(1)} %add.67), channel_id=1, source_target_pairs={{0,8},{1,9},{2,10},{3,11},{4,12},{5,13},{6,14},{7,15},{8,0},{9,1},... | collective-permute-start | bytes 1544 | tf_op jit(solution)/shard_map/ppermute | solution.py:347
  105.6 4.8 %collective-permute-start.6 = (f32[1,128]{1,0:T(1,128)S(1)}, f32[1,128]{1,0:T(1,128)S(1)}, u32[]{:S(2)}, u32[]{:S(2)}) collective-permute-start(f32[1,128]{1,0:T(1,128)S(1)} %add.68), channel_id=1, source_target_pairs={{0,24},{1,25},{2,26},{3,27},{4,28},{5,29},{6,30},{7,31},{8,16},{9,... | collective-permute-start | bytes 1544 | tf_op jit(solution)/shard_map/ppermute | solution.py:347

commit v5 on v4

--- a/solution.py
+++ b/solution.py
@@ -204,7 +204,7 @@
 
 def tail_kernel(
     label, given, bottom, given_weights, bias, last, last_bias, marks, logits, loss,
-    wide, hi, lo, stack, turned, packed, recv, weights, came, sem,
+    wide, hi, lo, stack, packed, recv, weights, came, sem,
 ):
     parts = came.shape[0]
     span = 128 // parts
@@ -228,13 +228,7 @@
     hi[...] = wide[pl.ds(SLOTS, 128, stride=ROWS), :].T
     lo[...] = wide[pl.ds(SLOTS + 1, 128, stride=ROWS), :].T
 
-    def put(f, value):
-        stack[f] = value
-        for k in range(8):
-            turned[pl.ds(f * BATCH + k, BATCH // 8, stride=8), :] = stack[f, pl.ds(7 - k, BATCH // 8, stride=8), :]
-
-    put(0, bottom[...].astype(BF).astype(F32))
-    turned[(F + 1) * BATCH :, :] = jnp.zeros(((31 - F) * BATCH, 128), F32)
+    stack[0] = bottom[...].astype(BF).astype(F32)
 
     def hits(slot, keep=None):
         high = hi[pl.ds(slot, 1), :]
@@ -257,7 +251,7 @@
             left = jnp.concatenate([hits(s, keep) for s, keep in slots], axis=1)
             right = jnp.concatenate([rows(s) for s, _ in slots], axis=0)
             total = jnp.dot(left, right, preferred_element_type=F32)
-            put(1 + 2 * g + e, total.astype(BF).astype(F32))
+            stack[1 + 2 * g + e] = total.astype(BF).astype(F32)
 
     pooled(0, [0, 1, 2])
 
@@ -269,13 +263,15 @@
 
     packed[:, :128] = bottom[...].astype(BF)
     own = lax.broadcasted_iota(jnp.int32, (8, 128), 1) % 8 == 7 - lax.broadcasted_iota(jnp.int32, (8, 128), 0)
+
+    back = 7 - lax.broadcasted_iota(jnp.int32, (8, 128), 0)
 
     def interact(m, _):
         halves = []
         for half in range(2):
             left = stack[:, pl.ds(16 * m + 8 * half, 8), :].reshape(8 * (F + 1), 128).astype(BF)
-            right = [turned[pl.ds(j * BATCH + 16 * m + 8 * half, 8), :] for j in range(32)]
-            right = jnp.concatenate(right, axis=0).astype(BF)
+            right = [jnp.take_along_axis(stack[j, pl.ds(16 * m + 8 * half, 8), :], back, axis=0) for j in range(F + 1)]
+            right = jnp.concatenate(right + [jnp.zeros((8 * (31 - F), 128), F32)], axis=0).astype(BF)
             gram = lax.dot_general(left, right, (((1,), (1,)), ((), ())), preferred_element_type=F32)
             columns = []
             for a in range(4):
@@ -293,16 +289,14 @@
         packed[pl.ds(pl.multiple_of(16 * m, 16), 16), 128:] = jnp.concatenate(halves, axis=0).astype(BF)
         return 0
 
-    lax.fori_loop(0, BATCH // 16, interact, 0, unroll=4)
+    lax.fori_loop(0, BATCH // 16, interact, 0, unroll=8)
 
     fetch.wait()
-    for m in range(4):
-        at = pl.ds(128 * m, 128)
-        hidden = jnp.dot(packed[at, :], weights[...], preferred_element_type=F32)
-        hidden = jnp.maximum(hidden + bias[...], 0.0).astype(BF)
-        out = lax.dot_general(last[...], hidden, (((1,), (1,)), ((), ())), preferred_element_type=F32)
-        logits[:, at] = out[:1] + last_bias[0]
-    x = logits[...]
+    hidden = jnp.dot(packed[...], weights[...], preferred_element_type=F32)
+    hidden = jnp.maximum(hidden + bias[...], 0.0).astype(BF)
+    out = lax.dot_general(last[...], hidden, (((1,), (1,)), ((), ())), preferred_element_type=F32)
+    x = out[:1] + last_bias[0]
+    logits[...] = x
     soft = jnp.maximum(x, 0.0) + jnp.log1p(jnp.exp(-jnp.abs(x)))
     term = jnp.sum(soft - marks[...].astype(F32) * x)
     loss[...] = jnp.full(loss.shape, term, F32)
@@ -319,14 +313,13 @@
             pltpu.VMEM((128, 128), F32),
             pltpu.VMEM((128, 128), F32),
             pltpu.VMEM((F + 1, BATCH, 128), F32),
-            pltpu.VMEM((32 * BATCH, 128), F32),
             pltpu.VMEM((BATCH, QW), BF),
             pltpu.VMEM((128, ROWS, 128), BF),
             pltpu.VMEM((QW, 1024), BF),
             pltpu.SemaphoreType.DMA((4,)),
             pltpu.SemaphoreType.DMA,
         ],
-        compiler_params=pltpu.CompilerParams(vmem_limit_bytes=60 << 20),
+        compiler_params=pltpu.CompilerParams(vmem_limit_bytes=36 << 20),
         cost_estimate=pl.CostEstimate(flops=6 << 30, transcendentals=0, bytes_accessed=5 << 20),
     )(label, recv, bottom, weights, bias, last, last_bias, marks)
 
@@ -341,26 +334,37 @@
     return lax.all_to_all(value, axes, split_axis=0, concat_axis=0, tiled=True)
 
 
-def ring_sum(value, axis, size, step):
+def near_sum(value, axis, size, step):
     for other in ((1, 0, 3, 2), (3, 2, 1, 0)):
         pairs = [(i, i + (other[i // step % 4] - i // step % 4) * step) for i in range(size)]
         value = value + lax.ppermute(value, axis, pairs)
     return value
 
 
-def keep_kernel(given, out):
-    out[...] = given[...]
+def ring_sum(value, axis):
+    one, two, three = (lax.ppermute(value, axis, [(i, (i + k) % 4) for i in range(4)]) for k in (1, 2, 3))
+    return (value + two) + (one + three)
+
+
+def keep_kernel(given, out, sent):
+    span = given.shape[0] // sent.shape[0]
+    copies = []
+    for n in range(sent.shape[0]):
+        at = pl.ds(span * n, span)
+        copies.append(pltpu.make_async_copy(given.at[at], out.at[at], sent.at[n]))
+        copies[-1].start()
+    for copy in copies:
+        copy.wait()
 
 
 def keep(value):
-    block = pl.BlockSpec((8,) + value.shape[1:], lambda n: (n, 0, 0))
     return pl.pallas_call(
         keep_kernel,
-        grid=(value.shape[0] // 8,),
         out_shape=jax.ShapeDtypeStruct(value.shape, value.dtype),
-        in_specs=[block],
-        out_specs=block,
-        compiler_params=pltpu.CompilerParams(vmem_limit_bytes=60 << 20),
+        in_specs=[VMEM],
+        out_specs=pl.BlockSpec(memory_space=pl.ANY),
+        scratch_shapes=[pltpu.SemaphoreType.DMA((8,))],
+        compiler_params=pltpu.CompilerParams(vmem_limit_bytes=8 << 20),
         cost_estimate=pl.CostEstimate(flops=0, transcendentals=0, bytes_accessed=4 << 20),
     )(value)
 
@@ -423,11 +427,11 @@
         bias_logit,
         labels[None, :],
     )
-    term = ring_sum(term, "hst", lax.axis_size("hst"), 1)
+    term = ring_sum(term, "hst")
     term = term + lax.ppermute(term, "chip", [(i, i ^ 1) for i in range(chips)])
-    term = ring_sum(term, "chip", chips, 2)
+    term = near_sum(term, "chip", chips, 2)
     rehomed, term = lax.optimization_barrier((keep(rehomed), term))
-    term = ring_sum(term, "chip", chips, 8)
+    term = near_sum(term, "chip", chips, 8)
     return rehomed, logits[0], term[0, 0]
 
 

time: 111 us -> 101 us (0.910)
  Pallas kernels: 31.1 us -> 22.6 us
  waiting for transfers between devices: 43.1 us -> 41.5 us
  starting transfers between devices: 26.3 us -> 27.7 us
    ppermute x6 -> x7, waiting for transfers between devices: 12.6 us -> 8.34 us  [the longest x4 6.82 us: near_sum(): value = value + lax.ppermute(value, axis, pairs)]
    pallas_call x1, Pallas kernels: 5.63 us -> 1.37 us  [keep(): pl.pallas_call(keep_kernel, out_shape=jax.ShapeDtypeStruct(value.shape, v...]
    pallas_call x1, Pallas kernels: 16.2 us -> 11.9 us  [tail(): pl.pallas_call(tail_kernel, out_shape=(jax.ShapeDtypeStruct((1, BATCH), F...]
    all_to_all x2, waiting for transfers between devices: 29.3 us -> 32.1 us  [exchange(): return lax.all_to_all(value, axes, split_axis=0, concat_axis=0, tiled=True)]
    ppermute x6 -> x7, starting transfers between devices: 10.7 us -> 12 us  [the longest x4 8.02 us: near_sum(): value = value + lax.ppermute(value, axis, pairs)]
  transfers between devices with their start and end apart: 9 -> 10, of which waited for: 7 -> 8; matrix products, arithmetic and copies ran while one was open for 6% -> 5% of each run, Pallas kernels for 22% -> 16%
where the time goes in v5:
time: 101 us
  waiting for transfers between devices  41.5 us (41%)
  starting transfers between devices  27.7 us (27%)
  Pallas kernels  22.6 us (22%)
  local copies, waits for them, and re-layouts  5.87 us (6%)
  between operations  1.62 us (2%)
    all_to_all x2, waiting for transfers between devices, exchange(): return lax.all_to_all(value, axes, split_axis=0, concat_axis=0, tiled=True)  32.1 us
    all_to_all x2, starting transfers between devices, exchange(): return lax.all_to_all(value, axes, split_axis=0, concat_axis=0, tiled=True)  15.6 us
    pallas_call x1, Pallas kernels, tail(): pl.pallas_call(tail_kernel, out_shape=(jax.ShapeDtypeStruct((1, BATCH), F...  11.9 us
    ppermute x4, starting transfers between devices, near_sum(): value = value + lax.ppermute(value, axis, pairs)  8.02 us
    ppermute x4, waiting for transfers between devices, near_sum(): value = value + lax.ppermute(value, axis, pairs)  6.82 us
    pallas_call x1, Pallas kernels, pool(): pl.pallas_call(pool_kernel, out_shape=jax.ShapeDtypeStruct((128, ROWS, 12...  6.62 us
    gather x1, local copies, waits for them, and re-layouts, per_device(): weights = jnp.take(padded, jnp.asarray(FEATURE_ROWS), axis=0)  4.21 us
    ppermute x3, starting transfers between devices, ring_sum(): lax.ppermute(value, axis, [(i, (i + k) % 4) for i in range(4)])  4.02 us
  transfers between devices with their start and end apart: 10, of which 8 were waited for; matrix products, arithmetic and copies ran while one was open for 5% of the time, Pallas kernels for 16%

profile of v5, /device:TPU:0, one launch (start us, length us, event | category | flops | bytes accessed | tf_op | source)
XLA Modules:
  0.0 100.6 jit_solution(11086878860007520137)
XLA Ops:
  0.6 6.6 %shard_map.240 = bf16[128,88,128]{2,1,0:T(8,128)(2,1)} custom-call(bf16[48,128,128]{2,1,0:T(8,128)(2,1)} %refs_0_.1, bf16[32,128,128]{2,1,0:T(8,128)(2,1)} %refs_1_.1, s32[48,8,128]{2,1,0:T(8,128)} %bitcast.16, s32[48,128]{1,0:T(8,128)} %refs_3_.1, s32[48,128]{1,0:T(8,128)} %refs_4_.1, s32[32,8,128]{2,1,0:T(8,128)} %bitcast.17, s32[32,128]{1,0:T(8,128)} %refs_6_.1, ...), custom_call_target="tpu_custom_call" | custom-call | flops 352321536 | bytes 6291456 | tf_op jit(solution)/shard_map/pallas_call | solution.py:188
  7.3 11.6 %all-to-all-start.1 = ((bf16[128,88,128]{2,1,0:T(8,128)(2,1)}), bf16[128,88,128]{2,1,0:T(8,128)(2,1)}, u32[]{:S(2)}, u32[]{:S(2)}) async-start(bf16[128,88,128]{2,1,0:T(8,128)(2,1)} %shard_map.240), calls=%async_computation.1 | async-start | bytes 5767168 | tf_op jit(solution)/shard_map/all_to_all | solution.py:334
  19.0 2.7 %shard_map.238 = bf16[64,128,128]{2,1,0:T(8,128)(2,1)} custom-call(s32[32]{0:T(128)S(1)} %bitcast.13, bf16[32,128,128]{2,1,0:T(8,128)(2,1)S(1)} %copy-done.1), custom_call_target="tpu_custom_call" | custom-call | bytes 3145728 | tf_op jit(solution)/shard_map/pallas_call | solution.py:91
  21.8 4.2 %gather_fusion = bf16[896,1024]{1,0:T(8,128)(2,1)} fusion(bf16[480,1024]{1,0:T(8,128)(2,1)S(1)} %concatenate.3, s32[1024]{0:T(1024)S(1)} %pad_clamp_fusion), kind=kCustom, calls=%fused_computation | custom fusion | bytes 3673600 | tf_op jit(solution)/shard_map/jit(_take)/gather | solution.py:416
  26.1 0.5 fusion.5
  26.9 30.5 %all-to-all-done.1.given = bf16[128,88,128]{2,1,0:T(8,128)(2,1)} async-done(((bf16[128,88,128]{2,1,0:T(8,128)(2,1)}), bf16[128,88,128]{2,1,0:T(8,128)(2,1)}, u32[]{:S(2)}, u32[]{:S(2)}) %all-to-all-start.1) | async-done | bytes 2883616 | tf_op jit(solution)/shard_map/all_to_all | solution.py:334
  57.4 4.0 %all-to-all-start = ((bf16[64,128,128]{2,1,0:T(8,128)(2,1)}), bf16[64,128,128]{2,1,0:T(8,128)(2,1)S(1)}, u32[]{:S(2)}, u32[]{:S(2)}) async-start(bf16[64,128,128]{2,1,0:T(8,128)(2,1)} %shard_map.238), calls=%async_computation | async-start | bytes 4194304 | tf_op jit(solution)/shard_map/all_to_all | solution.py:334
  62.1 1.5 %copy-done.2 = bf16[896,1024]{1,0:T(8,128)(2,1)S(1)} copy-done((bf16[896,1024]{1,0:T(8,128)(2,1)S(1)}, bf16[896,1024]{1,0:T(8,128)(2,1)}, u32[]{:S(2)}) %copy-start.2) | copy-done | bytes 1835032
  63.6 11.9 %shard_map.241 = (f32[1,512]{1,0:T(1,128)}, f32[1,128]{1,0:T(1,128)S(1)}) custom-call(s32[8,128]{1,0:T(8,128)S(1)} %copy-done.6, bf16[128,88,128]{2,1,0:T(8,128)(2,1)} %all-to-all-done.1.given, f32[512,128]{1,0:T(8,128)S(1)} %fusion.6.bottom, bf16[896,1024]{1,0:T(8,128)(2,1)S(1)} %copy-done.2, f32[1,1024]{1,0:T(1,128)S(1)} %bitcast.14, ...), custom_call_target="tpu_custom_call" | custom-call | flops 6442450944 | bytes 5242880 | tf_op jit(solution)/shard_map/pallas_call | solution.py:306
  75.6 0.8 collective-permute-start
  76.4 1.2 %collective-permute-start.1 = (f32[1,128]{1,0:T(1,128)S(1)}, f32[1,128]{1,0:T(1,128)S(1)}, u32[]{:S(2)}, u32[]{:S(2)}) collective-permute-start(f32[1,128]{1,0:T(1,128)S(1)} %get-tuple-element.15), channel_id=1, source_target_pairs={{0,32},{32,64},{64,96},{96,0},{1,33},{33,65},{65,97},{97,1},{2,34}... | collective-permute-start | bytes 1544 | tf_op jit(solution)/shard_map/ppermute | solution.py:345
  77.5 2.0 %collective-permute-start.2 = (f32[1,128]{1,0:T(1,128)S(1)}, f32[1,128]{1,0:T(1,128)S(1)}, u32[]{:S(2)}, u32[]{:S(2)}) collective-permute-start(f32[1,128]{1,0:T(1,128)S(1)} %get-tuple-element.15), channel_id=1, source_target_pairs={{0,96},{32,0},{64,32},{96,64},{1,97},{33,1},{65,33},{97,65},{2,98}... | collective-permute-start | bytes 1544 | tf_op jit(solution)/shard_map/ppermute | solution.py:345
  79.6 1.1 %collective-permute-done = f32[1,128]{1,0:T(1,128)S(1)} collective-permute-done((f32[1,128]{1,0:T(1,128)S(1)}, f32[1,128]{1,0:T(1,128)S(1)}, u32[]{:S(2)}, u32[]{:S(2)}) %collective-permute-start) | collective-permute-done | bytes 544 | tf_op jit(solution)/shard_map/ppermute | solution.py:345
  81.2 1.1 %collective-permute-done.3 = f32[1,128]{1,0:T(1,128)S(1)} collective-permute-done((f32[1,128]{1,0:T(1,128)S(1)}, f32[1,128]{1,0:T(1,128)S(1)}, u32[]{:S(2)}, u32[]{:S(2)}) %collective-permute-start.3) | collective-permute-done | bytes 544 | tf_op jit(solution)/shard_map/ppermute | solution.py:431
  82.3 1.7 %collective-permute-start.4 = (f32[1,128]{1,0:T(1,128)S(1)}, f32[1,128]{1,0:T(1,128)S(1)}, u32[]{:S(2)}, u32[]{:S(2)}) collective-permute-start(f32[1,128]{1,0:T(1,128)S(1)} %add.69), channel_id=1, source_target_pairs={{0,2},{1,3},{2,0},{3,1},{4,6},{5,7},{6,4},{7,5},{8,10},{9,11},{10,... | collective-permute-start | bytes 1544 | tf_op jit(solution)/shard_map/ppermute | solution.py:340
  84.0 1.9 %collective-permute-done.4 = f32[1,128]{1,0:T(1,128)S(1)} collective-permute-done((f32[1,128]{1,0:T(1,128)S(1)}, f32[1,128]{1,0:T(1,128)S(1)}, u32[]{:S(2)}, u32[]{:S(2)}) %collective-permute-start.4) | collective-permute-done | bytes 544 | tf_op jit(solution)/shard_map/ppermute | solution.py:340
  85.9 2.9 %collective-permute-start.5 = (f32[1,128]{1,0:T(1,128)S(1)}, f32[1,128]{1,0:T(1,128)S(1)}, u32[]{:S(2)}, u32[]{:S(2)}) collective-permute-start(f32[1,128]{1,0:T(1,128)S(1)} %add.70), channel_id=1, source_target_pairs={{0,6},{1,7},{2,4},{3,5},{4,2},{5,3},{6,0},{7,1},{8,14},{9,15},{10,... | collective-permute-start | bytes 1544 | tf_op jit(solution)/shard_map/ppermute | solution.py:340
  88.8 1.6 %all-to-all-done.given = bf16[64,128,128]{2,1,0:T(8,128)(2,1)S(1)} async-done(((bf16[64,128,128]{2,1,0:T(8,128)(2,1)}), bf16[64,128,128]{2,1,0:T(8,128)(2,1)S(1)}, u32[]{:S(2)}, u32[]{:S(2)}) %all-to-all-start) | async-done | bytes 2097184 | tf_op jit(solution)/shard_map/all_to_all | solution.py:334
  90.3 1.4 %shard_map.239 = bf16[64,128,128]{2,1,0:T(8,128)(2,1)} custom-call(bf16[64,128,128]{2,1,0:T(8,128)(2,1)S(1)} %all-to-all-done.given), custom_call_target="tpu_custom_call" | custom-call | bytes 4194304 | tf_op jit(solution)/shard_map/pallas_call | solution.py:361
  91.8 1.0 collective-permute-start.6
  92.7 2.6 %collective-permute-done.6 = f32[1,128]{1,0:T(1,128)S(1)} collective-permute-done((f32[1,128]{1,0:T(1,128)S(1)}, f32[1,128]{1,0:T(1,128)S(1)}, u32[]{:S(2)}, u32[]{:S(2)}) %collective-permute-start.6) | collective-permute-done | bytes 544 | tf_op jit(solution)/shard_map/ppermute | solution.py:340
  95.4 2.4 %collective-permute-start.7 = (f32[1,128]{1,0:T(1,128)S(1)}, f32[1,128]{1,0:T(1,128)S(1)}, u32[]{:S(2)}, u32[]{:S(2)}) collective-permute-start(f32[1,128]{1,0:T(1,128)S(1)} %add.72), channel_id=1, source_target_pairs={{0,24},{1,25},{2,26},{3,27},{4,28},{5,29},{6,30},{7,31},{8,16},{9,... | collective-permute-start | bytes 1544 | tf_op jit(solution)/shard_map/ppermute | solution.py:340
  97.8 2.3 %collective-permute-done.7 = f32[1,128]{1,0:T(1,128)S(1)} collective-permute-done((f32[1,128]{1,0:T(1,128)S(1)}, f32[1,128]{1,0:T(1,128)S(1)}, u32[]{:S(2)}, u32[]{:S(2)}) %collective-permute-start.7) | collective-permute-done | bytes 544 | tf_op jit(solution)/shard_map/ppermute | solution.py:340
  100.1 0.5 add.73
  (45 shorter events, 0.9 us)
Async XLA Ops:
  0.6 25.4 %copy-start = (bf16[512,256]{1,0:T(8,128)(2,1)S(1)}, bf16[512,256]{1,0:T(8,128)(2,1)}, u32[]{:S(2)}) copy-start(bf16[512,256]{1,0:T(8,128)(2,1)} %param.36) | copy-start | bytes 786436
  7.3 11.7 %copy-start.1 = (bf16[32,128,128]{2,1,0:T(8,128)(2,1)S(1)}, bf16[32,128,128]{2,1,0:T(8,128)(2,1)}, u32[]{:S(2)}) copy-start(bf16[32,128,128]{2,1,0:T(8,128)(2,1)} %refs_1_.1) | copy-start | bytes 3145732
  7.3 11.7 %copy-start.3 = (s32[32,1]{0,1:T(1,128)S(1)}, s32[32,1]{0,1:T(1,128)}, u32[]{:S(2)}) copy-start(s32[32,1]{0,1:T(1,128)} %param.31) | copy-start | bytes 388
  7.3 50.1 %all-to-all-start.1 = ((bf16[128,88,128]{2,1,0:T(8,128)(2,1)}), bf16[128,88,128]{2,1,0:T(8,128)(2,1)}, u32[]{:S(2)}, u32[]{:S(2)}) async-start(bf16[128,88,128]{2,1,0:T(8,128)(2,1)} %shard_map.240), calls=%async_computation.1 | async-start | bytes 5767168 | tf_op jit(solution)/shard_map/all_to_all | solution.py:334
  19.0 2.8 %copy-start.9 = (s32[896]{0:T(1024)S(1)}, s32[896]{0:T(1024)}, u32[]{:S(2)}) copy-start(s32[896]{0:T(1024)} %constant.50) | copy-start | bytes 10756
  21.7 4.3 %copy-start.10 = (bf16[1024,1]{0,1:T(2,128)(2,1)S(1)}, bf16[1024,1]{0,1:T(2,128)(2,1)}, u32[]{:S(2)}) copy-start(bf16[1024,1]{0,1:T(2,128)(2,1)} %param.42) | copy-start | bytes 6148
  21.8 4.3 %copy-start.12 = (bf16[512,13]{0,1:T(8,128)(2,1)S(1)}, bf16[512,13]{0,1:T(8,128)(2,1)}, u32[]{:S(2)}) copy-start(bf16[512,13]{0,1:T(8,128)(2,1)} %param.32) | copy-start | bytes 39940
  21.8 4.3 %copy-start.13 = (bf16[13,512]{1,0:T(8,128)(2,1)S(1)}, bf16[13,512]{1,0:T(8,128)(2,1)}, u32[]{:S(2)}) copy-start(bf16[13,512]{1,0:T(8,128)(2,1)} %param.34) | copy-start | bytes 39940
  21.8 4.3 %copy-start.14 = (f32[512]{0:T(512)S(1)}, f32[512]{0:T(512)}, u32[]{:S(2)}) copy-start(f32[512]{0:T(512)} %param.35) | copy-start | bytes 6148
  21.8 4.3 %copy-start.15 = (f32[256]{0:T(256)S(1)}, f32[256]{0:T(256)}, u32[]{:S(2)}) copy-start(f32[256]{0:T(256)} %param.37) | copy-start | bytes 3076
  21.8 4.8 %copy-start.8 = (bf16[256,128]{1,0:T(8,128)(2,1)S(1)}, bf16[256,128]{1,0:T(8,128)(2,1)}, u32[]{:S(2)}) copy-start(bf16[256,128]{1,0:T(8,128)(2,1)} %param.38) | copy-start | bytes 196612
  21.8 4.8 %copy-start.11 = (f32[128]{0:T(128)S(1)}, f32[128]{0:T(128)}, u32[]{:S(2)}) copy-start(f32[128]{0:T(128)} %param.39) | copy-start | bytes 1540
  26.8 35.2 %copy-start.4 = (f32[1024]{0:T(1024)S(1)}, f32[1024]{0:T(1024)}, u32[]{:S(2)}) copy-start(f32[1024]{0:T(1024)} %param.41) | copy-start | bytes 12292
  26.9 35.2 %copy-start.5 = (s32[512]{0:T(512)S(1)}, s32[512]{0:T(512)}, u32[]{:S(2)}) copy-start(s32[512]{0:T(512)} %param.33) | copy-start | bytes 6148
  26.9 35.2 %copy-start.6 = (s32[8,128]{1,0:T(8,128)S(1)}, s32[8,128]{1,0:T(8,128)}, u32[]{:S(2)}) copy-start(s32[8,128]{1,0:T(8,128)} %constant.30.clone.label) | copy-start | bytes 12292
  57.4 32.9 %all-to-all-start = ((bf16[64,128,128]{2,1,0:T(8,128)(2,1)}), bf16[64,128,128]{2,1,0:T(8,128)(2,1)S(1)}, u32[]{:S(2)}, u32[]{:S(2)}) async-start(bf16[64,128,128]{2,1,0:T(8,128)(2,1)} %shard_map.238), calls=%async_computation | async-start | bytes 4194304 | tf_op jit(solution)/shard_map/all_to_all | solution.py:334
  75.6 5.1 %collective-permute-start = (f32[1,128]{1,0:T(1,128)S(1)}, f32[1,128]{1,0:T(1,128)S(1)}, u32[]{:S(2)}, u32[]{:S(2)}) collective-permute-start(f32[1,128]{1,0:T(1,128)S(1)} %get-tuple-element.15), channel_id=1, source_target_pairs={{0,64},{32,96},{64,0},{96,32},{1,65},{33,97},{65,1},{97,33},{2,66}... | collective-permute-start | bytes 1544 | tf_op jit(solution)/shard_map/ppermute | solution.py:345
  76.4 4.8 %collective-permute-start.1 = (f32[1,128]{1,0:T(1,128)S(1)}, f32[1,128]{1,0:T(1,128)S(1)}, u32[]{:S(2)}, u32[]{:S(2)}) collective-permute-start(f32[1,128]{1,0:T(1,128)S(1)} %get-tuple-element.15), channel_id=1, source_target_pairs={{0,32},{32,64},{64,96},{96,0},{1,33},{33,65},{65,97},{97,1},{2,34}... | collective-permute-start | bytes 1544 | tf_op jit(solution)/shard_map/ppermute | solution.py:345
  77.5 3.6 %collective-permute-start.2 = (f32[1,128]{1,0:T(1,128)S(1)}, f32[1,128]{1,0:T(1,128)S(1)}, u32[]{:S(2)}, u32[]{:S(2)}) collective-permute-start(f32[1,128]{1,0:T(1,128)S(1)} %get-tuple-element.15), channel_id=1, source_target_pairs={{0,96},{32,0},{64,32},{96,64},{1,97},{33,1},{65,33},{97,65},{2,98}... | collective-permute-start | bytes 1544 | tf_op jit(solution)/shard_map/ppermute | solution.py:345
  81.1 1.2 %collective-permute-start.3 = (f32[1,128]{1,0:T(1,128)S(1)}, f32[1,128]{1,0:T(1,128)S(1)}, u32[]{:S(2)}, u32[]{:S(2)}) collective-permute-start(f32[1,128]{1,0:T(1,128)S(1)} %add_add_fusion), channel_id=1, source_target_pairs={{0,1},{1,0},{2,3},{3,2},{4,5},{5,4},{6,7},{7,6},{8,9},{9,8},{10,11... | collective-permute-start | bytes 1544 | tf_op jit(solution)/shard_map/ppermute | solution.py:431
  82.3 3.5 %collective-permute-start.4 = (f32[1,128]{1,0:T(1,128)S(1)}, f32[1,128]{1,0:T(1,128)S(1)}, u32[]{:S(2)}, u32[]{:S(2)}) collective-permute-start(f32[1,128]{1,0:T(1,128)S(1)} %add.69), channel_id=1, source_target_pairs={{0,2},{1,3},{2,0},{3,1},{4,6},{5,7},{6,4},{7,5},{8,10},{9,11},{10,... | collective-permute-start | bytes 1544 | tf_op jit(solution)/shard_map/ppermute | solution.py:340
  85.9 5.9 %collective-permute-start.5 = (f32[1,128]{1,0:T(1,128)S(1)}, f32[1,128]{1,0:T(1,128)S(1)}, u32[]{:S(2)}, u32[]{:S(2)}) collective-permute-start(f32[1,128]{1,0:T(1,128)S(1)} %add.70), channel_id=1, source_target_pairs={{0,6},{1,7},{2,4},{3,5},{4,2},{5,3},{6,0},{7,1},{8,14},{9,15},{10,... | collective-permute-start | bytes 1544 | tf_op jit(solution)/shard_map/ppermute | solution.py:340
  91.8 3.6 %collective-permute-start.6 = (f32[1,128]{1,0:T(1,128)S(1)}, f32[1,128]{1,0:T(1,128)S(1)}, u32[]{:S(2)}, u32[]{:S(2)}) collective-permute-start(f32[1,128]{1,0:T(1,128)S(1)} %add.71), channel_id=1, source_target_pairs={{0,8},{1,9},{2,10},{3,11},{4,12},{5,13},{6,14},{7,15},{8,0},{9,1},... | collective-permute-start | bytes 1544 | tf_op jit(solution)/shard_map/ppermute | solution.py:340
  95.4 4.8 %collective-permute-start.7 = (f32[1,128]{1,0:T(1,128)S(1)}, f32[1,128]{1,0:T(1,128)S(1)}, u32[]{:S(2)}, u32[]{:S(2)}) collective-permute-start(f32[1,128]{1,0:T(1,128)S(1)} %add.72), channel_id=1, source_target_pairs={{0,24},{1,25},{2,26},{3,27},{4,28},{5,29},{6,30},{7,31},{8,16},{9,... | collective-permute-start | bytes 1544 | tf_op jit(solution)/shard_map/ppermute | solution.py:340
  (2 other events, 4.2 us)

commit v6 on v5

--- a/solution.py
+++ b/solution.py
@@ -202,10 +202,10 @@
     )(*arrays)
 
 
-def tail_kernel(
-    label, given, bottom, given_weights, bias, last, last_bias, marks, logits, loss,
-    wide, hi, lo, stack, packed, recv, weights, came, sem,
-):
+def tail_kernel(*refs):
+    (given, *others), (logits, loss), refs = refs[:8], refs[8:10], refs[10:]
+    recv, (label, bottom, weights, bias, last, last_bias, marks), refs = refs[0], refs[1:8], refs[8:]
+    wide, hi, lo, stack, packed, came, sems = refs
     parts = came.shape[0]
     span = 128 // parts
     copies = []
@@ -213,8 +213,10 @@
         at = pl.ds(span * n, span)
         copies.append(pltpu.make_async_copy(given.at[at], recv.at[at], came.at[n]))
         copies[-1].start()
-    fetch = pltpu.make_async_copy(given_weights, weights, sem)
-    fetch.start()
+    held = (label, bottom, weights, bias, last, last_bias, marks)
+    fetches = [pltpu.make_async_copy(g, h, sems.at[n]) for n, (g, h) in enumerate(zip(others, held))]
+    for fetch in fetches:
+        fetch.start()
     zero = jnp.zeros((), BF)
     ones = lax.broadcasted_iota(jnp.int32, (16, 128), 0).astype(F32).astype(BF)
 
@@ -228,6 +230,8 @@
     hi[...] = wide[pl.ds(SLOTS, 128, stride=ROWS), :].T
     lo[...] = wide[pl.ds(SLOTS + 1, 128, stride=ROWS), :].T
 
+    for fetch in fetches[:2]:
+        fetch.wait()
     stack[0] = bottom[...].astype(BF).astype(F32)
 
     def hits(slot, keep=None):
@@ -291,37 +295,38 @@
 
     lax.fori_loop(0, BATCH // 16, interact, 0, unroll=8)
 
-    fetch.wait()
+    for fetch in fetches[2:]:
+        fetch.wait()
     hidden = jnp.dot(packed[...], weights[...], preferred_element_type=F32)
     hidden = jnp.maximum(hidden + bias[...], 0.0).astype(BF)
     out = lax.dot_general(last[...], hidden, (((1,), (1,)), ((), ())), preferred_element_type=F32)
-    x = out[:1] + last_bias[0]
+    x = out[:1] + last_bias[:, :1]
     logits[...] = x
     soft = jnp.maximum(x, 0.0) + jnp.log1p(jnp.exp(-jnp.abs(x)))
     term = jnp.sum(soft - marks[...].astype(F32) * x)
     loss[...] = jnp.full(loss.shape, term, F32)
 
 
-def tail(label, recv, bottom, weights, bias, last, last_bias, marks):
+def tail(given, *others):
+    anywhere = pl.BlockSpec(memory_space=pl.ANY)
     return pl.pallas_call(
         tail_kernel,
         out_shape=(jax.ShapeDtypeStruct((1, BATCH), F32), jax.ShapeDtypeStruct((1, 128), F32)),
-        in_specs=[VMEM, pl.BlockSpec(memory_space=pl.ANY)] * 2 + [VMEM, VMEM, SMEM, VMEM],
+        in_specs=[anywhere] * 8,
         out_specs=(VMEM, VMEM),
-        scratch_shapes=[
+        scratch_shapes=[pltpu.VMEM(a.shape, a.dtype) for a in (given,) + others]
+        + [
             pltpu.VMEM((128 * ROWS, 128), F32),
             pltpu.VMEM((128, 128), F32),
             pltpu.VMEM((128, 128), F32),
             pltpu.VMEM((F + 1, BATCH, 128), F32),
             pltpu.VMEM((BATCH, QW), BF),
-            pltpu.VMEM((128, ROWS, 128), BF),
-            pltpu.VMEM((QW, 1024), BF),
             pltpu.SemaphoreType.DMA((4,)),
-            pltpu.SemaphoreType.DMA,
+            pltpu.SemaphoreType.DMA((7,)),
         ],
-        compiler_params=pltpu.CompilerParams(vmem_limit_bytes=36 << 20),
+        compiler_params=pltpu.CompilerParams(vmem_limit_bytes=60 << 20),
         cost_estimate=pl.CostEstimate(flops=6 << 30, transcendentals=0, bytes_accessed=5 << 20),
-    )(label, recv, bottom, weights, bias, last, last_bias, marks)
+    )(given, *others)
 
 
 def labels_by_holder():
@@ -334,11 +339,10 @@
     return lax.all_to_all(value, axes, split_axis=0, concat_axis=0, tiled=True)
 
 
-def near_sum(value, axis, size, step):
-    for other in ((1, 0, 3, 2), (3, 2, 1, 0)):
-        pairs = [(i, i + (other[i // step % 4] - i // step % 4) * step) for i in range(size)]
-        value = value + lax.ppermute(value, axis, pairs)
-    return value
+def near_hop(value, axis, size, step, hop):
+    other = ((1, 0, 3, 2), (3, 2, 1, 0))[hop]
+    pairs = [(i, i + (other[i // step % 4] - i // step % 4) * step) for i in range(size)]
+    return value + lax.ppermute(value, axis, pairs)
 
 
 def ring_sum(value, axis):
@@ -415,23 +419,27 @@
     padded = jnp.concatenate([top_hidden, jnp.zeros((1, top_hidden.shape[1]), BF)], axis=0)
     weights = jnp.take(padded, jnp.asarray(FEATURE_ROWS), axis=0)
     last = jnp.broadcast_to(top_logit.reshape(1, -1), (8, top_logit.shape[0]))
-    outgoing, weights, bottom, last = lax.optimization_barrier((outgoing, weights, bottom, last))
+    last_bias = jnp.broadcast_to(bias_logit[None, :], (1, 128))
+    outgoing, weights, bottom, last, last_bias = lax.optimization_barrier(
+        (outgoing, weights, bottom, last, last_bias)
+    )
     rehomed = exchange(outgoing, "chip")
     logits, term = tail(
+        arrived,
         jnp.asarray(labels_by_holder()),
-        arrived,
         bottom,
         weights,
         bias_hidden[None, :],
         last,
-        bias_logit,
+        last_bias,
         labels[None, :],
     )
     term = ring_sum(term, "hst")
     term = term + lax.ppermute(term, "chip", [(i, i ^ 1) for i in range(chips)])
-    term = near_sum(term, "chip", chips, 2)
+    for step, hop in ((2, 0), (2, 1), (8, 0)):
+        term = near_hop(term, "chip", chips, step, hop)
     rehomed, term = lax.optimization_barrier((keep(rehomed), term))
-    term = near_sum(term, "chip", chips, 8)
+    term = near_hop(term, "chip", chips, 8, 1)
     return rehomed, logits[0], term[0, 0]
 
 

time: 101 us -> 101 us (level)
  waiting for transfers between devices: 41.5 us -> 39.5 us
    all_to_all x2, waiting for transfers between devices: 32.1 us -> 28.1 us  [exchange(): return lax.all_to_all(value, axes, split_axis=0, concat_axis=0, tiled=True)]
    ppermute x3, waiting for transfers between devices: 1.52 us -> 4.48 us  [ring_sum(): lax.ppermute(value, axis, [(i, (i + k) % 4) for i in range(4)])]
    unnamed x32 -> x24, local copies, waits for them, and re-layouts: 1.59 us -> 0.08 us
    ppermute x4, starting transfers between devices: 8.02 us -> 9.39 us  [near_hop(): return value + lax.ppermute(value, axis, pairs)]
    ppermute x3, starting transfers between devices: 4.02 us -> 2.8 us  [ring_sum(): lax.ppermute(value, axis, [(i, (i + k) % 4) for i in range(4)])]
    ppermute x4, waiting for transfers between devices: 6.82 us -> 5.8 us  [near_hop(): return value + lax.ppermute(value, axis, pairs)]
  transfers between devices with their start and end apart: 10 -> 10, of which waited for: 8 -> 9; matrix products, arithmetic and copies ran while one was open for 5% -> 7% of each run, Pallas kernels for 16% -> 17%
where the time goes in v6:
time: 101 us; the launch traced here: 100 us
  waiting for transfers between devices  39.5 us (39%)
  starting transfers between devices  27.8 us (28%)
  Pallas kernels  23.5 us (23%)
  local copies, waits for them, and re-layouts  5.44 us (5%)
  between operations  1.6 us (2%)
  matrix products  1.4 us (1%)
  other arithmetic  1.21 us (1%)
    all_to_all x2, waiting for transfers between devices, exchange(): return lax.all_to_all(value, axes, split_axis=0, concat_axis=0, tiled=True)  28.1 us
    all_to_all x2, starting transfers between devices, exchange(): return lax.all_to_all(value, axes, split_axis=0, concat_axis=0, tiled=True)  15.6 us
    pallas_call x1, Pallas kernels, tail(): pl.pallas_call(tail_kernel, out_shape=(jax.ShapeDtypeStruct((1, BATCH), F...  12.9 us
    ppermute x4, starting transfers between devices, near_hop(): return value + lax.ppermute(value, axis, pairs)  9.39 us
    pallas_call x1, Pallas kernels, pool(): pl.pallas_call(pool_kernel, out_shape=jax.ShapeDtypeStruct((128, ROWS, 12...  6.62 us
    ppermute x4, waiting for transfers between devices, near_hop(): return value + lax.ppermute(value, axis, pairs)  5.8 us
    ppermute x3, waiting for transfers between devices, ring_sum(): lax.ppermute(value, axis, [(i, (i + k) % 4) for i in range(4)])  4.48 us
    gather x1, local copies, waits for them, and re-layouts, per_device(): weights = jnp.take(padded, jnp.asarray(FEATURE_ROWS), axis=0)  4.19 us
  transfers between devices with their start and end apart: 10, of which 9 were waited for; matrix products, arithmetic and copies ran while one was open for 7% of the time, Pallas kernels for 17%

profile of v6, /device:TPU:0, one launch (start us, length us, event | category | flops | bytes accessed | tf_op | source)
XLA Modules:
  0.0 100.5 jit_solution(2536144921114221439)
XLA Ops:
  0.6 6.6 %shard_map.240 = bf16[128,88,128]{2,1,0:T(8,128)(2,1)} custom-call(bf16[48,128,128]{2,1,0:T(8,128)(2,1)} %refs_0_.1, bf16[32,128,128]{2,1,0:T(8,128)(2,1)} %refs_1_.2, s32[48,8,128]{2,1,0:T(8,128)} %bitcast.16, s32[48,128]{1,0:T(8,128)} %refs_3_.1, s32[48,128]{1,0:T(8,128)} %refs_4_.1, s32[32,8,128]{2,1,0:T(8,128)} %bitcast.17, s32[32,128]{1,0:T(8,128)} %refs_6_.1, ...), custom_call_target="tpu_custom_call" | custom-call | flops 352321536 | bytes 6291456 | tf_op jit(solution)/shard_map/pallas_call | solution.py:188
  7.3 11.6 %all-to-all-start.1 = ((bf16[128,88,128]{2,1,0:T(8,128)(2,1)}), bf16[128,88,128]{2,1,0:T(8,128)(2,1)}, u32[]{:S(2)}, u32[]{:S(2)}) async-start(bf16[128,88,128]{2,1,0:T(8,128)(2,1)} %shard_map.240), calls=%async_computation.1 | async-start | bytes 5767168 | tf_op jit(solution)/shard_map/all_to_all | solution.py:339
  19.7 2.7 %shard_map.238 = bf16[64,128,128]{2,1,0:T(8,128)(2,1)} custom-call(s32[32]{0:T(128)S(1)} %bitcast.15, bf16[32,128,128]{2,1,0:T(8,128)(2,1)S(1)} %copy-done.1), custom_call_target="tpu_custom_call" | custom-call | bytes 3145728 | tf_op jit(solution)/shard_map/pallas_call | solution.py:91
  22.6 4.2 %gather_fusion = bf16[896,1024]{1,0:T(8,128)(2,1)} fusion(bf16[480,1024]{1,0:T(8,128)(2,1)S(1)} %concatenate.3, s32[1024]{0:T(1024)S(1)} %pad_clamp_fusion), kind=kCustom, calls=%fused_computation | custom fusion | bytes 3673600 | tf_op jit(solution)/shard_map/jit(_take)/gather | solution.py:420
  27.3 0.9 fusion.6.refs_2_
  29.3 28.1 %all-to-all-done.1.refs_0_ = bf16[128,88,128]{2,1,0:T(8,128)(2,1)} async-done(((bf16[128,88,128]{2,1,0:T(8,128)(2,1)}), bf16[128,88,128]{2,1,0:T(8,128)(2,1)}, u32[]{:S(2)}, u32[]{:S(2)}) %all-to-all-start.1) | async-done | bytes 2883616 | tf_op jit(solution)/shard_map/all_to_all | solution.py:339
  57.4 4.0 %all-to-all-start = ((bf16[64,128,128]{2,1,0:T(8,128)(2,1)}), bf16[64,128,128]{2,1,0:T(8,128)(2,1)S(1)}, u32[]{:S(2)}, u32[]{:S(2)}) async-start(bf16[64,128,128]{2,1,0:T(8,128)(2,1)} %shard_map.238), calls=%async_computation | async-start | bytes 4194304 | tf_op jit(solution)/shard_map/all_to_all | solution.py:339
  61.4 12.9 %shard_map.241 = (f32[1,512]{1,0:T(1,128)}, f32[1,128]{1,0:T(1,128)}) custom-call(bf16[128,88,128]{2,1,0:T(8,128)(2,1)} %all-to-all-done.1.refs_0_, s32[8,128]{1,0:T(8,128)} %constant.30.clone.refs_1_, f32[512,128]{1,0:T(8,128)} %fusion.6.refs_2_, bf16[896,1024]{1,0:T(8,128)(2,1)} %gather_fusion, f32[1,1024]{1,0:T(1,128)} %bitcast.18, ...), custom_call_target="tpu_custom_call" | custom-call | flops 6442450944 | bytes 5242880 | tf_op jit(solution)/shard_map/pallas_call | solution.py:312
  74.3 1.1 %collective-permute-start.2 = (f32[1,128]{1,0:T(1,128)}, f32[1,128]{1,0:T(1,128)S(1)}, u32[]{:S(2)}, u32[]{:S(2)}) collective-permute-start(f32[1,128]{1,0:T(1,128)} %get-tuple-element.17), channel_id=1, source_target_pairs={{0,96},{32,0},{64,32},{96,64},{1,97},{33,1},{65,33},{97,65},{2,98}... | collective-permute-start | bytes 1544 | tf_op jit(solution)/shard_map/ppermute | solution.py:349
  75.4 1.0 collective-permute-start.1
  76.4 0.7 collective-permute-start
  77.1 0.9 collective-permute-done.2
  78.1 2.3 %collective-permute-done.1 = f32[1,128]{1,0:T(1,128)S(1)} collective-permute-done((f32[1,128]{1,0:T(1,128)}, f32[1,128]{1,0:T(1,128)S(1)}, u32[]{:S(2)}, u32[]{:S(2)}) %collective-permute-start.1) | collective-permute-done | bytes 544 | tf_op jit(solution)/shard_map/ppermute | solution.py:349
  80.3 1.3 %collective-permute-done = f32[1,128]{1,0:T(1,128)S(1)} collective-permute-done((f32[1,128]{1,0:T(1,128)}, f32[1,128]{1,0:T(1,128)S(1)}, u32[]{:S(2)}, u32[]{:S(2)}) %collective-permute-start) | collective-permute-done | bytes 544 | tf_op jit(solution)/shard_map/ppermute | solution.py:349
  81.6 0.7 add_add_fusion
  82.3 1.1 %collective-permute-done.3 = f32[1,128]{1,0:T(1,128)S(1)} collective-permute-done((f32[1,128]{1,0:T(1,128)S(1)}, f32[1,128]{1,0:T(1,128)S(1)}, u32[]{:S(2)}, u32[]{:S(2)}) %collective-permute-start.3) | collective-permute-done | bytes 544 | tf_op jit(solution)/shard_map/ppermute | solution.py:438
  83.4 1.7 %collective-permute-start.4 = (f32[1,128]{1,0:T(1,128)S(1)}, f32[1,128]{1,0:T(1,128)S(1)}, u32[]{:S(2)}, u32[]{:S(2)}) collective-permute-start(f32[1,128]{1,0:T(1,128)S(1)} %add.69), channel_id=1, source_target_pairs={{0,2},{1,3},{2,0},{3,1},{4,6},{5,7},{6,4},{7,5},{8,10},{9,11},{10,... | collective-permute-start | bytes 1544 | tf_op jit(solution)/shard_map/ppermute | solution.py:345
  85.1 1.9 %collective-permute-done.4 = f32[1,128]{1,0:T(1,128)S(1)} collective-permute-done((f32[1,128]{1,0:T(1,128)S(1)}, f32[1,128]{1,0:T(1,128)S(1)}, u32[]{:S(2)}, u32[]{:S(2)}) %collective-permute-start.4) | collective-permute-done | bytes 544 | tf_op jit(solution)/shard_map/ppermute | solution.py:345
  86.9 2.9 %collective-permute-start.5 = (f32[1,128]{1,0:T(1,128)S(1)}, f32[1,128]{1,0:T(1,128)S(1)}, u32[]{:S(2)}, u32[]{:S(2)}) collective-permute-start(f32[1,128]{1,0:T(1,128)S(1)} %add.70), channel_id=1, source_target_pairs={{0,6},{1,7},{2,4},{3,5},{4,2},{5,3},{6,0},{7,1},{8,14},{9,15},{10,... | collective-permute-start | bytes 1544 | tf_op jit(solution)/shard_map/ppermute | solution.py:345
  89.8 1.8 %collective-permute-done.5 = f32[1,128]{1,0:T(1,128)S(1)} collective-permute-done((f32[1,128]{1,0:T(1,128)S(1)}, f32[1,128]{1,0:T(1,128)S(1)}, u32[]{:S(2)}, u32[]{:S(2)}) %collective-permute-start.5) | collective-permute-done | bytes 544 | tf_op jit(solution)/shard_map/ppermute | solution.py:345
  91.7 1.7 %collective-permute-start.6 = (f32[1,128]{1,0:T(1,128)S(1)}, f32[1,128]{1,0:T(1,128)S(1)}, u32[]{:S(2)}, u32[]{:S(2)}) collective-permute-start(f32[1,128]{1,0:T(1,128)S(1)} %add.71), channel_id=1, source_target_pairs={{0,8},{1,9},{2,10},{3,11},{4,12},{5,13},{6,14},{7,15},{8,0},{9,1},... | collective-permute-start | bytes 1544 | tf_op jit(solution)/shard_map/ppermute | solution.py:345
  93.4 1.4 %shard_map.239 = bf16[64,128,128]{2,1,0:T(8,128)(2,1)} custom-call(bf16[64,128,128]{2,1,0:T(8,128)(2,1)S(1)} %all-to-all-done.given), custom_call_target="tpu_custom_call" | custom-call | bytes 4194304 | tf_op jit(solution)/shard_map/pallas_call | solution.py:365
  95.2 3.0 %collective-permute-start.7 = (f32[1,128]{1,0:T(1,128)S(1)}, f32[1,128]{1,0:T(1,128)S(1)}, u32[]{:S(2)}, u32[]{:S(2)}) collective-permute-start(f32[1,128]{1,0:T(1,128)S(1)} %add.72), channel_id=1, source_target_pairs={{0,24},{1,25},{2,26},{3,27},{4,28},{5,29},{6,30},{7,31},{8,16},{9,... | collective-permute-start | bytes 1544 | tf_op jit(solution)/shard_map/ppermute | solution.py:345
  98.3 1.7 %collective-permute-done.7 = f32[1,128]{1,0:T(1,128)S(1)} collective-permute-done((f32[1,128]{1,0:T(1,128)S(1)}, f32[1,128]{1,0:T(1,128)S(1)}, u32[]{:S(2)}, u32[]{:S(2)}) %collective-permute-start.7) | collective-permute-done | bytes 544 | tf_op jit(solution)/shard_map/ppermute | solution.py:345
  (38 shorter events, 2.7 us)
Async XLA Ops:
  0.6 26.2 %copy-start = (bf16[512,256]{1,0:T(8,128)(2,1)S(1)}, bf16[512,256]{1,0:T(8,128)(2,1)}, u32[]{:S(2)}) copy-start(bf16[512,256]{1,0:T(8,128)(2,1)} %param.36) | copy-start | bytes 786436
  7.3 12.4 %copy-start.1 = (bf16[32,128,128]{2,1,0:T(8,128)(2,1)S(1)}, bf16[32,128,128]{2,1,0:T(8,128)(2,1)}, u32[]{:S(2)}) copy-start(bf16[32,128,128]{2,1,0:T(8,128)(2,1)} %refs_1_.2) | copy-start | bytes 3145732
  7.3 12.4 %copy-start.2 = (s32[32,1]{0,1:T(1,128)S(1)}, s32[32,1]{0,1:T(1,128)}, u32[]{:S(2)}) copy-start(s32[32,1]{0,1:T(1,128)} %param.31) | copy-start | bytes 388
  7.3 50.1 %all-to-all-start.1 = ((bf16[128,88,128]{2,1,0:T(8,128)(2,1)}), bf16[128,88,128]{2,1,0:T(8,128)(2,1)}, u32[]{:S(2)}, u32[]{:S(2)}) async-start(bf16[128,88,128]{2,1,0:T(8,128)(2,1)} %shard_map.240), calls=%async_computation.1 | async-start | bytes 5767168 | tf_op jit(solution)/shard_map/all_to_all | solution.py:339
  18.9 3.5 %copy-start.6 = (bf16[1024,1]{0,1:T(2,128)(2,1)S(1)}, bf16[1024,1]{0,1:T(2,128)(2,1)}, u32[]{:S(2)}) copy-start(bf16[1024,1]{0,1:T(2,128)(2,1)} %param.42) | copy-start | bytes 6148
  18.9 3.5 %copy-start.3 = (bf16[479,1024]{1,0:T(8,128)(2,1)S(1)}, bf16[479,1024]{1,0:T(8,128)(2,1)}, u32[]{:S(2)}) copy-start(bf16[479,1024]{1,0:T(8,128)(2,1)} %param.40) | copy-start | bytes 2942980
  19.7 2.8 %copy-start.5 = (s32[896]{0:T(1024)S(1)}, s32[896]{0:T(1024)}, u32[]{:S(2)}) copy-start(s32[896]{0:T(1024)} %constant.50) | copy-start | bytes 10756
  22.5 4.3 %copy-start.8 = (bf16[512,13]{0,1:T(8,128)(2,1)S(1)}, bf16[512,13]{0,1:T(8,128)(2,1)}, u32[]{:S(2)}) copy-start(bf16[512,13]{0,1:T(8,128)(2,1)} %param.32) | copy-start | bytes 39940
  22.5 4.3 %copy-start.9 = (bf16[13,512]{1,0:T(8,128)(2,1)S(1)}, bf16[13,512]{1,0:T(8,128)(2,1)}, u32[]{:S(2)}) copy-start(bf16[13,512]{1,0:T(8,128)(2,1)} %param.34) | copy-start | bytes 39940
  22.5 4.3 %copy-start.10 = (f32[512]{0:T(512)S(1)}, f32[512]{0:T(512)}, u32[]{:S(2)}) copy-start(f32[512]{0:T(512)} %param.35) | copy-start | bytes 6148
  22.6 4.3 %copy-start.11 = (f32[256]{0:T(256)S(1)}, f32[256]{0:T(256)}, u32[]{:S(2)}) copy-start(f32[256]{0:T(256)} %param.37) | copy-start | bytes 3076
  22.6 4.7 %copy-start.4 = (bf16[256,128]{1,0:T(8,128)(2,1)S(1)}, bf16[256,128]{1,0:T(8,128)(2,1)}, u32[]{:S(2)}) copy-start(bf16[256,128]{1,0:T(8,128)(2,1)} %param.38) | copy-start | bytes 196612
  22.6 4.7 %copy-start.7 = (f32[128]{0:T(128)S(1)}, f32[128]{0:T(128)}, u32[]{:S(2)}) copy-start(f32[128]{0:T(128)} %param.39) | copy-start | bytes 1540
  57.4 36.0 %all-to-all-start = ((bf16[64,128,128]{2,1,0:T(8,128)(2,1)}), bf16[64,128,128]{2,1,0:T(8,128)(2,1)S(1)}, u32[]{:S(2)}, u32[]{:S(2)}) async-start(bf16[64,128,128]{2,1,0:T(8,128)(2,1)} %shard_map.238), calls=%async_computation | async-start | bytes 4194304 | tf_op jit(solution)/shard_map/all_to_all | solution.py:339
  74.3 3.7 %collective-permute-start.2 = (f32[1,128]{1,0:T(1,128)}, f32[1,128]{1,0:T(1,128)S(1)}, u32[]{:S(2)}, u32[]{:S(2)}) collective-permute-start(f32[1,128]{1,0:T(1,128)} %get-tuple-element.17), channel_id=1, source_target_pairs={{0,96},{32,0},{64,32},{96,64},{1,97},{33,1},{65,33},{97,65},{2,98}... | collective-permute-start | bytes 1544 | tf_op jit(solution)/shard_map/ppermute | solution.py:349
  75.4 4.9 %collective-permute-start.1 = (f32[1,128]{1,0:T(1,128)}, f32[1,128]{1,0:T(1,128)S(1)}, u32[]{:S(2)}, u32[]{:S(2)}) collective-permute-start(f32[1,128]{1,0:T(1,128)} %get-tuple-element.17), channel_id=1, source_target_pairs={{0,32},{32,64},{64,96},{96,0},{1,33},{33,65},{65,97},{97,1},{2,34}... | collective-permute-start | bytes 1544 | tf_op jit(solution)/shard_map/ppermute | solution.py:349
  76.4 5.2 %collective-permute-start = (f32[1,128]{1,0:T(1,128)}, f32[1,128]{1,0:T(1,128)S(1)}, u32[]{:S(2)}, u32[]{:S(2)}) collective-permute-start(f32[1,128]{1,0:T(1,128)} %get-tuple-element.17), channel_id=1, source_target_pairs={{0,64},{32,96},{64,0},{96,32},{1,65},{33,97},{65,1},{97,33},{2,66}... | collective-permute-start | bytes 1544 | tf_op jit(solution)/shard_map/ppermute | solution.py:349
  82.2 1.1 %collective-permute-start.3 = (f32[1,128]{1,0:T(1,128)S(1)}, f32[1,128]{1,0:T(1,128)S(1)}, u32[]{:S(2)}, u32[]{:S(2)}) collective-permute-start(f32[1,128]{1,0:T(1,128)S(1)} %add_add_fusion), channel_id=1, source_target_pairs={{0,1},{1,0},{2,3},{3,2},{4,5},{5,4},{6,7},{7,6},{8,9},{9,8},{10,11... | collective-permute-start | bytes 1544 | tf_op jit(solution)/shard_map/ppermute | solution.py:438
  83.4 3.5 %collective-permute-start.4 = (f32[1,128]{1,0:T(1,128)S(1)}, f32[1,128]{1,0:T(1,128)S(1)}, u32[]{:S(2)}, u32[]{:S(2)}) collective-permute-start(f32[1,128]{1,0:T(1,128)S(1)} %add.69), channel_id=1, source_target_pairs={{0,2},{1,3},{2,0},{3,1},{4,6},{5,7},{6,4},{7,5},{8,10},{9,11},{10,... | collective-permute-start | bytes 1544 | tf_op jit(solution)/shard_map/ppermute | solution.py:345
  86.9 4.8 %collective-permute-start.5 = (f32[1,128]{1,0:T(1,128)S(1)}, f32[1,128]{1,0:T(1,128)S(1)}, u32[]{:S(2)}, u32[]{:S(2)}) collective-permute-start(f32[1,128]{1,0:T(1,128)S(1)} %add.70), channel_id=1, source_target_pairs={{0,6},{1,7},{2,4},{3,5},{4,2},{5,3},{6,0},{7,1},{8,14},{9,15},{10,... | collective-permute-start | bytes 1544 | tf_op jit(solution)/shard_map/ppermute | solution.py:345
  91.7 3.5 %collective-permute-start.6 = (f32[1,128]{1,0:T(1,128)S(1)}, f32[1,128]{1,0:T(1,128)S(1)}, u32[]{:S(2)}, u32[]{:S(2)}) collective-permute-start(f32[1,128]{1,0:T(1,128)S(1)} %add.71), channel_id=1, source_target_pairs={{0,8},{1,9},{2,10},{3,11},{4,12},{5,13},{6,14},{7,15},{8,0},{9,1},... | collective-permute-start | bytes 1544 | tf_op jit(solution)/shard_map/ppermute | solution.py:345
  95.2 4.8 %collective-permute-start.7 = (f32[1,128]{1,0:T(1,128)S(1)}, f32[1,128]{1,0:T(1,128)S(1)}, u32[]{:S(2)}, u32[]{:S(2)}) collective-permute-start(f32[1,128]{1,0:T(1,128)S(1)} %add.72), channel_id=1, source_target_pairs={{0,24},{1,25},{2,26},{3,27},{4,28},{5,29},{6,30},{7,31},{8,16},{9,... | collective-permute-start | bytes 1544 | tf_op jit(solution)/shard_map/ppermute | solution.py:345

commit v7 on v6

--- a/solution.py
+++ b/solution.py
@@ -339,15 +339,8 @@
     return lax.all_to_all(value, axes, split_axis=0, concat_axis=0, tiled=True)
 
 
-def near_hop(value, axis, size, step, hop):
-    other = ((1, 0, 3, 2), (3, 2, 1, 0))[hop]
-    pairs = [(i, i + (other[i // step % 4] - i // step % 4) * step) for i in range(size)]
-    return value + lax.ppermute(value, axis, pairs)
-
-
-def ring_sum(value, axis):
-    one, two, three = (lax.ppermute(value, axis, [(i, (i + k) % 4) for i in range(4)]) for k in (1, 2, 3))
-    return (value + two) + (one + three)
+def swap_sum(value, axis, step):
+    return value + lax.ppermute(value, axis, [(i, i ^ step) for i in range(lax.axis_size(axis))])
 
 
 def keep_kernel(given, out, sent):
@@ -434,12 +427,10 @@
         last_bias,
         labels[None, :],
     )
-    term = ring_sum(term, "hst")
-    term = term + lax.ppermute(term, "chip", [(i, i ^ 1) for i in range(chips)])
-    for step, hop in ((2, 0), (2, 1), (8, 0)):
-        term = near_hop(term, "chip", chips, step, hop)
+    for axis, step in (("hst", 1), ("hst", 2), ("chip", 1), ("chip", 8), ("chip", 16), ("chip", 2)):
+        term = swap_sum(term, axis, step)
     rehomed, term = lax.optimization_barrier((keep(rehomed), term))
-    term = near_hop(term, "chip", chips, 8, 1)
+    term = swap_sum(term, "chip", 4)
     return rehomed, logits[0], term[0, 0]
 
 

time: 101 us -> 103 us (1.020)
  waiting for transfers between devices: 39.5 us -> 42.6 us
    ppermute x8 -> x7, waiting for transfers between devices: 11.4 us -> 14.5 us  [swap_sum(): lax.ppermute(value, axis, [(i, i ^ step) for i in range(lax.axis_size(axi...]
    ppermute x8 -> x7, starting transfers between devices: 12.2 us -> 11.2 us  [swap_sum(): lax.ppermute(value, axis, [(i, i ^ step) for i in range(lax.axis_size(axi...]
  transfers between devices with their start and end apart: 10 -> 9, of which waited for: 9 -> 8; matrix products, arithmetic and copies ran while one was open for 7% -> 7% of each run, Pallas kernels for 17% -> 16%
where the time goes in v7:
time: 103 us
  waiting for transfers between devices  42.6 us (41%)
  starting transfers between devices  26.9 us (26%)
  Pallas kernels  23.5 us (23%)
  local copies, waits for them, and re-layouts  5.42 us (5%)
  between operations  1.6 us (2%)
  matrix products  1.4 us (1%)
  other arithmetic  1.21 us (1%)
    all_to_all x2, waiting for transfers between devices, exchange(): return lax.all_to_all(value, axes, split_axis=0, concat_axis=0, tiled=True)  28.1 us
    all_to_all x2, starting transfers between devices, exchange(): return lax.all_to_all(value, axes, split_axis=0, concat_axis=0, tiled=True)  15.6 us
    ppermute x7, waiting for transfers between devices, swap_sum(): lax.ppermute(value, axis, [(i, i ^ step) for i in range(lax.axis_size(axi...  14.5 us
    pallas_call x1, Pallas kernels, tail(): pl.pallas_call(tail_kernel, out_shape=(jax.ShapeDtypeStruct((1, BATCH), F...  12.9 us
    ppermute x7, starting transfers between devices, swap_sum(): lax.ppermute(value, axis, [(i, i ^ step) for i in range(lax.axis_size(axi...  11.2 us
    pallas_call x1, Pallas kernels, pool(): pl.pallas_call(pool_kernel, out_shape=jax.ShapeDtypeStruct((128, ROWS, 12...  6.63 us
    gather x1, local copies, waits for them, and re-layouts, per_device(): weights = jnp.take(padded, jnp.asarray(FEATURE_ROWS), axis=0)  4.19 us
    pallas_call x1, Pallas kernels, route(): pl.pallas_call(route_kernel, out_shape=jax.ShapeDtypeStruct((2 * chips,)...  2.68 us
  transfers between devices with their start and end apart: 9, of which 8 were waited for; matrix products, arithmetic and copies ran while one was open for 7% of the time, Pallas kernels for 16%

profile of v7, /device:TPU:0, one launch (start us, length us, event | category | flops | bytes accessed | tf_op | source)
XLA Modules:
  0.0 102.6 jit_solution(6144954214314471088)
XLA Ops:
  0.6 6.6 %shard_map.240 = bf16[128,88,128]{2,1,0:T(8,128)(2,1)} custom-call(bf16[48,128,128]{2,1,0:T(8,128)(2,1)} %refs_0_.1, bf16[32,128,128]{2,1,0:T(8,128)(2,1)} %refs_1_.2, s32[48,8,128]{2,1,0:T(8,128)} %bitcast.16, s32[48,128]{1,0:T(8,128)} %refs_3_.1, s32[48,128]{1,0:T(8,128)} %refs_4_.1, s32[32,8,128]{2,1,0:T(8,128)} %bitcast.17, s32[32,128]{1,0:T(8,128)} %refs_6_.1, ...), custom_call_target="tpu_custom_call" | custom-call | flops 352321536 | bytes 6291456 | tf_op jit(solution)/shard_map/pallas_call | solution.py:188
  7.3 11.6 %all-to-all-start.1 = ((bf16[128,88,128]{2,1,0:T(8,128)(2,1)}), bf16[128,88,128]{2,1,0:T(8,128)(2,1)}, u32[]{:S(2)}, u32[]{:S(2)}) async-start(bf16[128,88,128]{2,1,0:T(8,128)(2,1)} %shard_map.240), calls=%async_computation.1 | async-start | bytes 5767168 | tf_op jit(solution)/shard_map/all_to_all | solution.py:339
  19.7 2.7 %shard_map.238 = bf16[64,128,128]{2,1,0:T(8,128)(2,1)} custom-call(s32[32]{0:T(128)S(1)} %bitcast.15, bf16[32,128,128]{2,1,0:T(8,128)(2,1)S(1)} %copy-done.1), custom_call_target="tpu_custom_call" | custom-call | bytes 3145728 | tf_op jit(solution)/shard_map/pallas_call | solution.py:91
  22.6 4.2 %gather_fusion = bf16[896,1024]{1,0:T(8,128)(2,1)} fusion(bf16[480,1024]{1,0:T(8,128)(2,1)S(1)} %concatenate.3, s32[1024]{0:T(1024)S(1)} %pad_clamp_fusion), kind=kCustom, calls=%fused_computation | custom fusion | bytes 3673600 | tf_op jit(solution)/shard_map/jit(_take)/gather | solution.py:413
  27.3 0.9 fusion.6.refs_2_
  28.7 0.6 broadcast_in_dim.41.refs_5_
  29.3 28.1 %all-to-all-done.1.refs_0_ = bf16[128,88,128]{2,1,0:T(8,128)(2,1)} async-done(((bf16[128,88,128]{2,1,0:T(8,128)(2,1)}), bf16[128,88,128]{2,1,0:T(8,128)(2,1)}, u32[]{:S(2)}, u32[]{:S(2)}) %all-to-all-start.1) | async-done | bytes 2883616 | tf_op jit(solution)/shard_map/all_to_all | solution.py:339
  57.4 4.0 %all-to-all-start = ((bf16[64,128,128]{2,1,0:T(8,128)(2,1)}), bf16[64,128,128]{2,1,0:T(8,128)(2,1)S(1)}, u32[]{:S(2)}, u32[]{:S(2)}) async-start(bf16[64,128,128]{2,1,0:T(8,128)(2,1)} %shard_map.238), calls=%async_computation | async-start | bytes 4194304 | tf_op jit(solution)/shard_map/all_to_all | solution.py:339
  61.4 12.9 %shard_map.241 = (f32[1,512]{1,0:T(1,128)}, f32[1,128]{1,0:T(1,128)}) custom-call(bf16[128,88,128]{2,1,0:T(8,128)(2,1)} %all-to-all-done.1.refs_0_, s32[8,128]{1,0:T(8,128)} %constant.30.clone.refs_1_, f32[512,128]{1,0:T(8,128)} %fusion.6.refs_2_, bf16[896,1024]{1,0:T(8,128)(2,1)} %gather_fusion, f32[1,1024]{1,0:T(1,128)} %bitcast.18, ...), custom_call_target="tpu_custom_call" | custom-call | flops 6442450944 | bytes 5242880 | tf_op jit(solution)/shard_map/pallas_call | solution.py:312
  74.3 0.6 collective-permute-start
  75.0 3.1 %collective-permute-done = f32[1,128]{1,0:T(1,128)S(1)} collective-permute-done((f32[1,128]{1,0:T(1,128)}, f32[1,128]{1,0:T(1,128)S(1)}, u32[]{:S(2)}, u32[]{:S(2)}) %collective-permute-start) | collective-permute-done | bytes 544 | tf_op jit(solution)/shard_map/ppermute | solution.py:343
  78.1 0.7 add.63
  78.7 0.7 collective-permute-start.1
  79.4 4.3 %collective-permute-done.1 = f32[1,128]{1,0:T(1,128)S(1)} collective-permute-done((f32[1,128]{1,0:T(1,128)S(1)}, f32[1,128]{1,0:T(1,128)S(1)}, u32[]{:S(2)}, u32[]{:S(2)}) %collective-permute-start.1) | collective-permute-done | bytes 544 | tf_op jit(solution)/shard_map/ppermute | solution.py:343
  83.8 1.1 %collective-permute-done.2 = f32[1,128]{1,0:T(1,128)S(1)} collective-permute-done((f32[1,128]{1,0:T(1,128)S(1)}, f32[1,128]{1,0:T(1,128)S(1)}, u32[]{:S(2)}, u32[]{:S(2)}) %collective-permute-start.2) | collective-permute-done | bytes 544 | tf_op jit(solution)/shard_map/ppermute | solution.py:343
  84.9 1.7 %collective-permute-start.3 = (f32[1,128]{1,0:T(1,128)S(1)}, f32[1,128]{1,0:T(1,128)S(1)}, u32[]{:S(2)}, u32[]{:S(2)}) collective-permute-start(f32[1,128]{1,0:T(1,128)S(1)} %add.65), channel_id=1, source_target_pairs={{0,8},{1,9},{2,10},{3,11},{4,12},{5,13},{6,14},{7,15},{8,0},{9,1},... | collective-permute-start | bytes 1544 | tf_op jit(solution)/shard_map/ppermute | solution.py:343
  86.6 1.8 %collective-permute-done.3 = f32[1,128]{1,0:T(1,128)S(1)} collective-permute-done((f32[1,128]{1,0:T(1,128)S(1)}, f32[1,128]{1,0:T(1,128)S(1)}, u32[]{:S(2)}, u32[]{:S(2)}) %collective-permute-start.3) | collective-permute-done | bytes 544 | tf_op jit(solution)/shard_map/ppermute | solution.py:343
  88.5 3.3 %collective-permute-start.4 = (f32[1,128]{1,0:T(1,128)S(1)}, f32[1,128]{1,0:T(1,128)S(1)}, u32[]{:S(2)}, u32[]{:S(2)}) collective-permute-start(f32[1,128]{1,0:T(1,128)S(1)} %add.66), channel_id=1, source_target_pairs={{0,16},{1,17},{2,18},{3,19},{4,20},{5,21},{6,22},{7,23},{8,24},{9,... | collective-permute-start | bytes 1544 | tf_op jit(solution)/shard_map/ppermute | solution.py:343
  91.7 1.8 %collective-permute-done.4 = f32[1,128]{1,0:T(1,128)S(1)} collective-permute-done((f32[1,128]{1,0:T(1,128)S(1)}, f32[1,128]{1,0:T(1,128)S(1)}, u32[]{:S(2)}, u32[]{:S(2)}) %collective-permute-start.4) | collective-permute-done | bytes 544 | tf_op jit(solution)/shard_map/ppermute | solution.py:343
  93.5 1.7 %collective-permute-start.5 = (f32[1,128]{1,0:T(1,128)S(1)}, f32[1,128]{1,0:T(1,128)S(1)}, u32[]{:S(2)}, u32[]{:S(2)}) collective-permute-start(f32[1,128]{1,0:T(1,128)S(1)} %add.67), channel_id=1, source_target_pairs={{0,2},{1,3},{2,0},{3,1},{4,6},{5,7},{6,4},{7,5},{8,10},{9,11},{10,... | collective-permute-start | bytes 1544 | tf_op jit(solution)/shard_map/ppermute | solution.py:343
  95.2 1.4 %shard_map.239 = bf16[64,128,128]{2,1,0:T(8,128)(2,1)} custom-call(bf16[64,128,128]{2,1,0:T(8,128)(2,1)S(1)} %all-to-all-done.given), custom_call_target="tpu_custom_call" | custom-call | bytes 4194304 | tf_op jit(solution)/shard_map/pallas_call | solution.py:358
  97.0 3.2 %collective-permute-start.6 = (f32[1,128]{1,0:T(1,128)S(1)}, f32[1,128]{1,0:T(1,128)S(1)}, u32[]{:S(2)}, u32[]{:S(2)}) collective-permute-start(f32[1,128]{1,0:T(1,128)S(1)} %add.68), channel_id=1, source_target_pairs={{0,4},{1,5},{2,6},{3,7},{4,0},{5,1},{6,2},{7,3},{8,12},{9,13},{10,... | collective-permute-start | bytes 1544 | tf_op jit(solution)/shard_map/ppermute | solution.py:343
  100.2 1.8 %collective-permute-done.6 = f32[1,128]{1,0:T(1,128)S(1)} collective-permute-done((f32[1,128]{1,0:T(1,128)S(1)}, f32[1,128]{1,0:T(1,128)S(1)}, u32[]{:S(2)}, u32[]{:S(2)}) %collective-permute-start.6) | collective-permute-done | bytes 544 | tf_op jit(solution)/shard_map/ppermute | solution.py:343
  102.1 0.5 add.69
  (37 shorter events, 1.6 us)
Async XLA Ops:
  0.6 26.2 %copy-start = (bf16[512,256]{1,0:T(8,128)(2,1)S(1)}, bf16[512,256]{1,0:T(8,128)(2,1)}, u32[]{:S(2)}) copy-start(bf16[512,256]{1,0:T(8,128)(2,1)} %param.36) | copy-start | bytes 786436
  7.3 12.4 %copy-start.1 = (bf16[32,128,128]{2,1,0:T(8,128)(2,1)S(1)}, bf16[32,128,128]{2,1,0:T(8,128)(2,1)}, u32[]{:S(2)}) copy-start(bf16[32,128,128]{2,1,0:T(8,128)(2,1)} %refs_1_.2) | copy-start | bytes 3145732
  7.3 12.4 %copy-start.2 = (s32[32,1]{0,1:T(1,128)S(1)}, s32[32,1]{0,1:T(1,128)}, u32[]{:S(2)}) copy-start(s32[32,1]{0,1:T(1,128)} %param.31) | copy-start | bytes 388
  7.3 50.1 %all-to-all-start.1 = ((bf16[128,88,128]{2,1,0:T(8,128)(2,1)}), bf16[128,88,128]{2,1,0:T(8,128)(2,1)}, u32[]{:S(2)}, u32[]{:S(2)}) async-start(bf16[128,88,128]{2,1,0:T(8,128)(2,1)} %shard_map.240), calls=%async_computation.1 | async-start | bytes 5767168 | tf_op jit(solution)/shard_map/all_to_all | solution.py:339
  18.9 3.5 %copy-start.6 = (bf16[1024,1]{0,1:T(2,128)(2,1)S(1)}, bf16[1024,1]{0,1:T(2,128)(2,1)}, u32[]{:S(2)}) copy-start(bf16[1024,1]{0,1:T(2,128)(2,1)} %param.42) | copy-start | bytes 6148
  18.9 3.5 %copy-start.3 = (bf16[479,1024]{1,0:T(8,128)(2,1)S(1)}, bf16[479,1024]{1,0:T(8,128)(2,1)}, u32[]{:S(2)}) copy-start(bf16[479,1024]{1,0:T(8,128)(2,1)} %param.40) | copy-start | bytes 2942980
  19.7 2.8 %copy-start.5 = (s32[896]{0:T(1024)S(1)}, s32[896]{0:T(1024)}, u32[]{:S(2)}) copy-start(s32[896]{0:T(1024)} %constant.50) | copy-start | bytes 10756
  22.5 4.3 %copy-start.8 = (bf16[512,13]{0,1:T(8,128)(2,1)S(1)}, bf16[512,13]{0,1:T(8,128)(2,1)}, u32[]{:S(2)}) copy-start(bf16[512,13]{0,1:T(8,128)(2,1)} %param.32) | copy-start | bytes 39940
  22.5 4.3 %copy-start.9 = (bf16[13,512]{1,0:T(8,128)(2,1)S(1)}, bf16[13,512]{1,0:T(8,128)(2,1)}, u32[]{:S(2)}) copy-start(bf16[13,512]{1,0:T(8,128)(2,1)} %param.34) | copy-start | bytes 39940
  22.6 4.3 %copy-start.10 = (f32[512]{0:T(512)S(1)}, f32[512]{0:T(512)}, u32[]{:S(2)}) copy-start(f32[512]{0:T(512)} %param.35) | copy-start | bytes 6148
  22.6 4.3 %copy-start.11 = (f32[256]{0:T(256)S(1)}, f32[256]{0:T(256)}, u32[]{:S(2)}) copy-start(f32[256]{0:T(256)} %param.37) | copy-start | bytes 3076
  22.6 4.7 %copy-start.4 = (bf16[256,128]{1,0:T(8,128)(2,1)S(1)}, bf16[256,128]{1,0:T(8,128)(2,1)}, u32[]{:S(2)}) copy-start(bf16[256,128]{1,0:T(8,128)(2,1)} %param.38) | copy-start | bytes 196612
  22.6 4.7 %copy-start.7 = (f32[128]{0:T(128)S(1)}, f32[128]{0:T(128)}, u32[]{:S(2)}) copy-start(f32[128]{0:T(128)} %param.39) | copy-start | bytes 1540
  57.4 37.8 %all-to-all-start = ((bf16[64,128,128]{2,1,0:T(8,128)(2,1)}), bf16[64,128,128]{2,1,0:T(8,128)(2,1)S(1)}, u32[]{:S(2)}, u32[]{:S(2)}) async-start(bf16[64,128,128]{2,1,0:T(8,128)(2,1)} %shard_map.238), calls=%async_computation | async-start | bytes 4194304 | tf_op jit(solution)/shard_map/all_to_all | solution.py:339
  74.3 3.8 %collective-permute-start = (f32[1,128]{1,0:T(1,128)}, f32[1,128]{1,0:T(1,128)S(1)}, u32[]{:S(2)}, u32[]{:S(2)}) collective-permute-start(f32[1,128]{1,0:T(1,128)} %get-tuple-element.17), channel_id=1, source_target_pairs={{0,32},{32,0},{64,96},{96,64},{1,33},{33,1},{65,97},{97,65},{2,34}... | collective-permute-start | bytes 1544 | tf_op jit(solution)/shard_map/ppermute | solution.py:343
  78.7 5.0 %collective-permute-start.1 = (f32[1,128]{1,0:T(1,128)S(1)}, f32[1,128]{1,0:T(1,128)S(1)}, u32[]{:S(2)}, u32[]{:S(2)}) collective-permute-start(f32[1,128]{1,0:T(1,128)S(1)} %add.63), channel_id=1, source_target_pairs={{0,64},{32,96},{64,0},{96,32},{1,65},{33,97},{65,1},{97,33},{2,66}... | collective-permute-start | bytes 1544 | tf_op jit(solution)/shard_map/ppermute | solution.py:343
  83.8 1.1 %collective-permute-start.2 = (f32[1,128]{1,0:T(1,128)S(1)}, f32[1,128]{1,0:T(1,128)S(1)}, u32[]{:S(2)}, u32[]{:S(2)}) collective-permute-start(f32[1,128]{1,0:T(1,128)S(1)} %add.64), channel_id=1, source_target_pairs={{0,1},{1,0},{2,3},{3,2},{4,5},{5,4},{6,7},{7,6},{8,9},{9,8},{10,11... | collective-permute-start | bytes 1544 | tf_op jit(solution)/shard_map/ppermute | solution.py:343
  84.9 3.5 %collective-permute-start.3 = (f32[1,128]{1,0:T(1,128)S(1)}, f32[1,128]{1,0:T(1,128)S(1)}, u32[]{:S(2)}, u32[]{:S(2)}) collective-permute-start(f32[1,128]{1,0:T(1,128)S(1)} %add.65), channel_id=1, source_target_pairs={{0,8},{1,9},{2,10},{3,11},{4,12},{5,13},{6,14},{7,15},{8,0},{9,1},... | collective-permute-start | bytes 1544 | tf_op jit(solution)/shard_map/ppermute | solution.py:343
  88.5 5.0 %collective-permute-start.4 = (f32[1,128]{1,0:T(1,128)S(1)}, f32[1,128]{1,0:T(1,128)S(1)}, u32[]{:S(2)}, u32[]{:S(2)}) collective-permute-start(f32[1,128]{1,0:T(1,128)S(1)} %add.66), channel_id=1, source_target_pairs={{0,16},{1,17},{2,18},{3,19},{4,20},{5,21},{6,22},{7,23},{8,24},{9,... | collective-permute-start | bytes 1544 | tf_op jit(solution)/shard_map/ppermute | solution.py:343
  93.5 3.5 %collective-permute-start.5 = (f32[1,128]{1,0:T(1,128)S(1)}, f32[1,128]{1,0:T(1,128)S(1)}, u32[]{:S(2)}, u32[]{:S(2)}) collective-permute-start(f32[1,128]{1,0:T(1,128)S(1)} %add.67), channel_id=1, source_target_pairs={{0,2},{1,3},{2,0},{3,1},{4,6},{5,7},{6,4},{7,5},{8,10},{9,11},{10,... | collective-permute-start | bytes 1544 | tf_op jit(solution)/shard_map/ppermute | solution.py:343
  97.0 5.0 %collective-permute-start.6 = (f32[1,128]{1,0:T(1,128)S(1)}, f32[1,128]{1,0:T(1,128)S(1)}, u32[]{:S(2)}, u32[]{:S(2)}) collective-permute-start(f32[1,128]{1,0:T(1,128)S(1)} %add.68), channel_id=1, source_target_pairs={{0,4},{1,5},{2,6},{3,7},{4,0},{5,1},{6,2},{7,3},{8,12},{9,13},{10,... | collective-permute-start | bytes 1544 | tf_op jit(solution)/shard_map/ppermute | solution.py:343

commit v8 on v7

--- a/solution.py
+++ b/solution.py
@@ -150,7 +150,7 @@
         return 0
 
     both = HOME // 2 - PERIOD
-    lax.fori_loop(0, 6, step, 0, unroll=3)
+    lax.fori_loop(0, 6, step, 0, unroll=6)
     for copy in waves[1]:
         copy.wait()
     lax.fori_loop(6, both, step, 0, unroll=5)
@@ -196,7 +196,7 @@
             pltpu.VMEM((128, ROWS, 128), BF),
         ]
         + [pltpu.VMEM(a.shape, a.dtype) for a in arrays]
-        + [pltpu.SemaphoreType.DMA((12,)), pltpu.SemaphoreType.DMA((4,))],
+        + [pltpu.SemaphoreType.DMA((12,)), pltpu.SemaphoreType.DMA((8,))],
         compiler_params=pltpu.CompilerParams(vmem_limit_bytes=60 << 20),
         cost_estimate=pl.CostEstimate(flops=84 * 128 * 128 * 256, transcendentals=0, bytes_accessed=6 << 20),
     )(*arrays)
@@ -321,7 +321,7 @@
             pltpu.VMEM((128, 128), F32),
             pltpu.VMEM((F + 1, BATCH, 128), F32),
             pltpu.VMEM((BATCH, QW), BF),
-            pltpu.SemaphoreType.DMA((4,)),
+            pltpu.SemaphoreType.DMA((8,)),
             pltpu.SemaphoreType.DMA((7,)),
         ],
         compiler_params=pltpu.CompilerParams(vmem_limit_bytes=60 << 20),
@@ -339,8 +339,17 @@
     return lax.all_to_all(value, axes, split_axis=0, concat_axis=0, tiled=True)
 
 
-def swap_sum(value, axis, step):
-    return value + lax.ppermute(value, axis, [(i, i ^ step) for i in range(lax.axis_size(axis))])
+def ring_sum(value, axis):
+    one, two, three = (lax.ppermute(value, axis, [(i, (i + k) % 4) for i in range(4)]) for k in (1, 2, 3))
+    return (value + two) + (one + three)
+
+
+def part_ring(value, axis, size, step):
+    one, two, three = (
+        lax.ppermute(value, axis, [(i, i - i // step % 4 * step + (i // step + k) % 4 * step) for i in range(size)])
+        for k in (1, 2, 3)
+    )
+    return (value + two) + (one + three)
 
 
 def keep_kernel(given, out, sent):
@@ -427,10 +436,11 @@
         last_bias,
         labels[None, :],
     )
-    for axis, step in (("hst", 1), ("hst", 2), ("chip", 1), ("chip", 8), ("chip", 16), ("chip", 2)):
-        term = swap_sum(term, axis, step)
+    term = ring_sum(term, "hst")
+    term = term + lax.ppermute(term, "chip", [(i, i ^ 1) for i in range(chips)])
+    term = part_ring(term, "chip", chips, 2)
     rehomed, term = lax.optimization_barrier((keep(rehomed), term))
-    term = swap_sum(term, "chip", 4)
+    term = part_ring(term, "chip", chips, 8)
     return rehomed, logits[0], term[0, 0]
 
 

time: 103 us -> 100 us (0.971)
  waiting for transfers between devices: 42.6 us -> 38.2 us
  starting transfers between devices: 26.9 us -> 28.3 us
    ppermute x7 -> x10, waiting for transfers between devices: 14.5 us -> 8.4 us  [the longest x3 4.48 us: ring_sum(): lax.ppermute(value, axis, [(i, (i + k) % 4) for i in range(4)])]
    all_to_all x2, waiting for transfers between devices: 28.1 us -> 29.8 us  [exchange(): return lax.all_to_all(value, axes, split_axis=0, concat_axis=0, tiled=True)]
    ppermute x7 -> x10, starting transfers between devices: 11.2 us -> 12.6 us  [the longest x6 9.86 us: part_ring(): lax.ppermute(value, axis, [(i, i - i // step % 4 * step + (i // step + k)...]
  transfers between devices with their start and end apart: 9 -> 12, of which waited for: 8 -> 8; matrix products, arithmetic and copies ran while one was open for 7% -> 8% of each run, Pallas kernels for 16% -> 17%
where the time goes in v8:
time: 100 us; the launch traced here: 99.4 us
  waiting for transfers between devices  38.2 us (38%)
  starting transfers between devices  28.3 us (28%)
  Pallas kernels  23.2 us (23%)
  local copies, waits for them, and re-layouts  5.52 us (6%)
  between operations  1.63 us (2%)
  matrix products  1.39 us (1%)
  other arithmetic  1.21 us (1%)
    all_to_all x2, waiting for transfers between devices, exchange(): return lax.all_to_all(value, axes, split_axis=0, concat_axis=0, tiled=True)  29.8 us
    all_to_all x2, starting transfers between devices, exchange(): return lax.all_to_all(value, axes, split_axis=0, concat_axis=0, tiled=True)  15.6 us
    pallas_call x1, Pallas kernels, tail(): pl.pallas_call(tail_kernel, out_shape=(jax.ShapeDtypeStruct((1, BATCH), F...  12.8 us
    ppermute x6, starting transfers between devices, part_ring(): lax.ppermute(value, axis, [(i, i - i // step % 4 * step + (i // step + k)...  9.86 us
    pallas_call x1, Pallas kernels, pool(): pl.pallas_call(pool_kernel, out_shape=jax.ShapeDtypeStruct((128, ROWS, 12...  6.36 us
    ppermute x3, waiting for transfers between devices, ring_sum(): lax.ppermute(value, axis, [(i, (i + k) % 4) for i in range(4)])  4.48 us
    gather x1, local copies, waits for them, and re-layouts, per_device(): weights = jnp.take(padded, jnp.asarray(FEATURE_ROWS), axis=0)  4.21 us
    ppermute x6, waiting for transfers between devices, part_ring(): lax.ppermute(value, axis, [(i, i - i // step % 4 * step + (i // step + k)...  2.8 us
  transfers between devices with their start and end apart: 12, of which 8 were waited for; matrix products, arithmetic and copies ran while one was open for 8% of the time, Pallas kernels for 17%

profile of v8, /device:TPU:0, one launch (start us, length us, event | category | flops | bytes accessed | tf_op | source)
XLA Modules:
  0.0 99.4 jit_solution(7865713792958229007)
XLA Ops:
  0.6 6.4 %shard_map.240 = bf16[128,88,128]{2,1,0:T(8,128)(2,1)} custom-call(bf16[48,128,128]{2,1,0:T(8,128)(2,1)} %refs_0_.1, bf16[32,128,128]{2,1,0:T(8,128)(2,1)} %refs_1_.2, s32[48,8,128]{2,1,0:T(8,128)} %bitcast.16, s32[48,128]{1,0:T(8,128)} %refs_3_.1, s32[48,128]{1,0:T(8,128)} %refs_4_.1, s32[32,8,128]{2,1,0:T(8,128)} %bitcast.17, s32[32,128]{1,0:T(8,128)} %refs_6_.1, ...), custom_call_target="tpu_custom_call" | custom-call | flops 352321536 | bytes 6291456 | tf_op jit(solution)/shard_map/pallas_call | solution.py:188
  7.0 11.6 %all-to-all-start.1 = ((bf16[128,88,128]{2,1,0:T(8,128)(2,1)}), bf16[128,88,128]{2,1,0:T(8,128)(2,1)}, u32[]{:S(2)}, u32[]{:S(2)}) async-start(bf16[128,88,128]{2,1,0:T(8,128)(2,1)} %shard_map.240), calls=%async_computation.1 | async-start | bytes 5767168 | tf_op jit(solution)/shard_map/all_to_all | solution.py:339
  19.5 2.7 %shard_map.238 = bf16[64,128,128]{2,1,0:T(8,128)(2,1)} custom-call(s32[32]{0:T(128)S(1)} %bitcast.15, bf16[32,128,128]{2,1,0:T(8,128)(2,1)S(1)} %copy-done.1), custom_call_target="tpu_custom_call" | custom-call | bytes 3145728 | tf_op jit(solution)/shard_map/pallas_call | solution.py:91
  22.3 4.2 %gather_fusion = bf16[896,1024]{1,0:T(8,128)(2,1)} fusion(bf16[480,1024]{1,0:T(8,128)(2,1)S(1)} %concatenate.3, s32[1024]{0:T(1024)S(1)} %pad_clamp_fusion), kind=kCustom, calls=%fused_computation | custom fusion | bytes 3673600 | tf_op jit(solution)/shard_map/jit(_take)/gather | solution.py:422
  27.1 0.9 fusion.6.refs_2_
  28.6 0.6 broadcast_in_dim.41.refs_5_
  29.2 28.0 %all-to-all-done.1.refs_0_ = bf16[128,88,128]{2,1,0:T(8,128)(2,1)} async-done(((bf16[128,88,128]{2,1,0:T(8,128)(2,1)}), bf16[128,88,128]{2,1,0:T(8,128)(2,1)}, u32[]{:S(2)}, u32[]{:S(2)}) %all-to-all-start.1) | async-done | bytes 2883616 | tf_op jit(solution)/shard_map/all_to_all | solution.py:339
  57.2 4.0 %all-to-all-start = ((bf16[64,128,128]{2,1,0:T(8,128)(2,1)}), bf16[64,128,128]{2,1,0:T(8,128)(2,1)S(1)}, u32[]{:S(2)}, u32[]{:S(2)}) async-start(bf16[64,128,128]{2,1,0:T(8,128)(2,1)} %shard_map.238), calls=%async_computation | async-start | bytes 4194304 | tf_op jit(solution)/shard_map/all_to_all | solution.py:339
  61.2 12.8 %shard_map.241 = (f32[1,512]{1,0:T(1,128)}, f32[1,128]{1,0:T(1,128)}) custom-call(bf16[128,88,128]{2,1,0:T(8,128)(2,1)} %all-to-all-done.1.refs_0_, s32[8,128]{1,0:T(8,128)} %constant.30.clone.refs_1_, f32[512,128]{1,0:T(8,128)} %fusion.6.refs_2_, bf16[896,1024]{1,0:T(8,128)(2,1)} %gather_fusion, f32[1,1024]{1,0:T(1,128)} %bitcast.19, ...), custom_call_target="tpu_custom_call" | custom-call | flops 6442450944 | bytes 5242880 | tf_op jit(solution)/shard_map/pallas_call | solution.py:312
  74.0 1.1 %collective-permute-start.2 = (f32[1,128]{1,0:T(1,128)}, f32[1,128]{1,0:T(1,128)S(1)}, u32[]{:S(2)}, u32[]{:S(2)}) collective-permute-start(f32[1,128]{1,0:T(1,128)} %get-tuple-element.17), channel_id=1, source_target_pairs={{0,96},{32,0},{64,32},{96,64},{1,97},{33,1},{65,33},{97,65},{2,98}... | collective-permute-start | bytes 1544 | tf_op jit(solution)/shard_map/ppermute | solution.py:343
  75.1 1.0 collective-permute-start.1
  76.1 0.7 collective-permute-start
  76.8 1.0 collective-permute-done.2
  77.7 2.2 %collective-permute-done.1 = f32[1,128]{1,0:T(1,128)S(1)} collective-permute-done((f32[1,128]{1,0:T(1,128)}, f32[1,128]{1,0:T(1,128)S(1)}, u32[]{:S(2)}, u32[]{:S(2)}) %collective-permute-start.1) | collective-permute-done | bytes 544 | tf_op jit(solution)/shard_map/ppermute | solution.py:343
  80.0 1.3 %collective-permute-done = f32[1,128]{1,0:T(1,128)S(1)} collective-permute-done((f32[1,128]{1,0:T(1,128)}, f32[1,128]{1,0:T(1,128)S(1)}, u32[]{:S(2)}, u32[]{:S(2)}) %collective-permute-start) | collective-permute-done | bytes 544 | tf_op jit(solution)/shard_map/ppermute | solution.py:343
  81.3 0.7 add_add_fusion.2
  81.9 1.1 %collective-permute-done.3 = f32[1,128]{1,0:T(1,128)S(1)} collective-permute-done((f32[1,128]{1,0:T(1,128)S(1)}, f32[1,128]{1,0:T(1,128)S(1)}, u32[]{:S(2)}, u32[]{:S(2)}) %collective-permute-start.3) | collective-permute-done | bytes 544 | tf_op jit(solution)/shard_map/ppermute | solution.py:440
  83.1 2.9 %collective-permute-start.6 = (f32[1,128]{1,0:T(1,128)S(1)}, f32[1,128]{1,0:T(1,128)S(1)}, u32[]{:S(2)}, u32[]{:S(2)}) collective-permute-start(f32[1,128]{1,0:T(1,128)S(1)} %add.75), channel_id=1, source_target_pairs={{0,6},{1,7},{2,0},{3,1},{4,2},{5,3},{6,4},{7,5},{8,14},{9,15},{10,... | collective-permute-start | bytes 1544 | tf_op jit(solution)/shard_map/ppermute | solution.py:349
  86.0 2.3 %collective-permute-start.4 = (f32[1,128]{1,0:T(1,128)S(1)}, f32[1,128]{1,0:T(1,128)S(1)}, u32[]{:S(2)}, u32[]{:S(2)}) collective-permute-start(f32[1,128]{1,0:T(1,128)S(1)} %add.75), channel_id=1, source_target_pairs={{0,4},{1,5},{2,6},{3,7},{4,0},{5,1},{6,2},{7,3},{8,12},{9,13},{10,... | collective-permute-start | bytes 1544 | tf_op jit(solution)/shard_map/ppermute | solution.py:349
  88.3 1.8 %all-to-all-done.given = bf16[64,128,128]{2,1,0:T(8,128)(2,1)S(1)} async-done(((bf16[64,128,128]{2,1,0:T(8,128)(2,1)}), bf16[64,128,128]{2,1,0:T(8,128)(2,1)S(1)}, u32[]{:S(2)}, u32[]{:S(2)}) %all-to-all-start) | async-done | bytes 2097184 | tf_op jit(solution)/shard_map/all_to_all | solution.py:339
  90.1 1.4 %shard_map.239 = bf16[64,128,128]{2,1,0:T(8,128)(2,1)} custom-call(bf16[64,128,128]{2,1,0:T(8,128)(2,1)S(1)} %all-to-all-done.given), custom_call_target="tpu_custom_call" | custom-call | bytes 4194304 | tf_op jit(solution)/shard_map/pallas_call | solution.py:367
  91.5 2.4 %collective-permute-start.9 = (f32[1,128]{1,0:T(1,128)S(1)}, f32[1,128]{1,0:T(1,128)S(1)}, u32[]{:S(2)}, u32[]{:S(2)}) collective-permute-start(f32[1,128]{1,0:T(1,128)S(1)} %add_add_fusion.1), channel_id=1, source_target_pairs={{0,24},{1,25},{2,26},{3,27},{4,28},{5,29},{6,30},{7,31},{8,0},{9,1... | collective-permute-start | bytes 1544 | tf_op jit(solution)/shard_map/ppermute | solution.py:349
  93.9 2.3 %collective-permute-start.7 = (f32[1,128]{1,0:T(1,128)S(1)}, f32[1,128]{1,0:T(1,128)S(1)}, u32[]{:S(2)}, u32[]{:S(2)}) collective-permute-start(f32[1,128]{1,0:T(1,128)S(1)} %add_add_fusion.1), channel_id=1, source_target_pairs={{0,16},{1,17},{2,18},{3,19},{4,20},{5,21},{6,22},{7,23},{8,24},{9,... | collective-permute-start | bytes 1544 | tf_op jit(solution)/shard_map/ppermute | solution.py:349
  96.1 2.5 %collective-permute-done.8 = f32[1,128]{1,0:T(1,128)S(1)} collective-permute-done((f32[1,128]{1,0:T(1,128)S(1)}, f32[1,128]{1,0:T(1,128)S(1)}, u32[]{:S(2)}, u32[]{:S(2)}) %collective-permute-start.8) | collective-permute-done | bytes 544 | tf_op jit(solution)/shard_map/ppermute | solution.py:349
  (40 shorter events, 2.0 us)
Async XLA Ops:
  0.6 25.9 %copy-start = (bf16[512,256]{1,0:T(8,128)(2,1)S(1)}, bf16[512,256]{1,0:T(8,128)(2,1)}, u32[]{:S(2)}) copy-start(bf16[512,256]{1,0:T(8,128)(2,1)} %param.36) | copy-start | bytes 786436
  7.0 12.4 %copy-start.1 = (bf16[32,128,128]{2,1,0:T(8,128)(2,1)S(1)}, bf16[32,128,128]{2,1,0:T(8,128)(2,1)}, u32[]{:S(2)}) copy-start(bf16[32,128,128]{2,1,0:T(8,128)(2,1)} %refs_1_.2) | copy-start | bytes 3145732
  7.0 12.4 %copy-start.2 = (s32[32,1]{0,1:T(1,128)S(1)}, s32[32,1]{0,1:T(1,128)}, u32[]{:S(2)}) copy-start(s32[32,1]{0,1:T(1,128)} %param.31) | copy-start | bytes 388
  7.0 50.1 %all-to-all-start.1 = ((bf16[128,88,128]{2,1,0:T(8,128)(2,1)}), bf16[128,88,128]{2,1,0:T(8,128)(2,1)}, u32[]{:S(2)}, u32[]{:S(2)}) async-start(bf16[128,88,128]{2,1,0:T(8,128)(2,1)} %shard_map.240), calls=%async_computation.1 | async-start | bytes 5767168 | tf_op jit(solution)/shard_map/all_to_all | solution.py:339
  18.7 3.5 %copy-start.6 = (bf16[1024,1]{0,1:T(2,128)(2,1)S(1)}, bf16[1024,1]{0,1:T(2,128)(2,1)}, u32[]{:S(2)}) copy-start(bf16[1024,1]{0,1:T(2,128)(2,1)} %param.42) | copy-start | bytes 6148
  18.7 3.5 %copy-start.3 = (bf16[479,1024]{1,0:T(8,128)(2,1)S(1)}, bf16[479,1024]{1,0:T(8,128)(2,1)}, u32[]{:S(2)}) copy-start(bf16[479,1024]{1,0:T(8,128)(2,1)} %param.40) | copy-start | bytes 2942980
  19.4 2.8 %copy-start.5 = (s32[896]{0:T(1024)S(1)}, s32[896]{0:T(1024)}, u32[]{:S(2)}) copy-start(s32[896]{0:T(1024)} %constant.50) | copy-start | bytes 10756
  22.3 4.3 %copy-start.8 = (bf16[512,13]{0,1:T(8,128)(2,1)S(1)}, bf16[512,13]{0,1:T(8,128)(2,1)}, u32[]{:S(2)}) copy-start(bf16[512,13]{0,1:T(8,128)(2,1)} %param.32) | copy-start | bytes 39940
  22.3 4.3 %copy-start.9 = (bf16[13,512]{1,0:T(8,128)(2,1)S(1)}, bf16[13,512]{1,0:T(8,128)(2,1)}, u32[]{:S(2)}) copy-start(bf16[13,512]{1,0:T(8,128)(2,1)} %param.34) | copy-start | bytes 39940
  22.3 4.3 %copy-start.10 = (f32[512]{0:T(512)S(1)}, f32[512]{0:T(512)}, u32[]{:S(2)}) copy-start(f32[512]{0:T(512)} %param.35) | copy-start | bytes 6148
  22.3 4.3 %copy-start.11 = (f32[256]{0:T(256)S(1)}, f32[256]{0:T(256)}, u32[]{:S(2)}) copy-start(f32[256]{0:T(256)} %param.37) | copy-start | bytes 3076
  22.3 4.7 %copy-start.4 = (bf16[256,128]{1,0:T(8,128)(2,1)S(1)}, bf16[256,128]{1,0:T(8,128)(2,1)}, u32[]{:S(2)}) copy-start(bf16[256,128]{1,0:T(8,128)(2,1)} %param.38) | copy-start | bytes 196612
  22.3 4.7 %copy-start.7 = (f32[128]{0:T(128)S(1)}, f32[128]{0:T(128)}, u32[]{:S(2)}) copy-start(f32[128]{0:T(128)} %param.39) | copy-start | bytes 1540
  57.2 32.9 %all-to-all-start = ((bf16[64,128,128]{2,1,0:T(8,128)(2,1)}), bf16[64,128,128]{2,1,0:T(8,128)(2,1)S(1)}, u32[]{:S(2)}, u32[]{:S(2)}) async-start(bf16[64,128,128]{2,1,0:T(8,128)(2,1)} %shard_map.238), calls=%async_computation | async-start | bytes 4194304 | tf_op jit(solution)/shard_map/all_to_all | solution.py:339
  74.0 3.7 %collective-permute-start.2 = (f32[1,128]{1,0:T(1,128)}, f32[1,128]{1,0:T(1,128)S(1)}, u32[]{:S(2)}, u32[]{:S(2)}) collective-permute-start(f32[1,128]{1,0:T(1,128)} %get-tuple-element.17), channel_id=1, source_target_pairs={{0,96},{32,0},{64,32},{96,64},{1,97},{33,1},{65,33},{97,65},{2,98}... | collective-permute-start | bytes 1544 | tf_op jit(solution)/shard_map/ppermute | solution.py:343
  75.1 4.9 %collective-permute-start.1 = (f32[1,128]{1,0:T(1,128)}, f32[1,128]{1,0:T(1,128)S(1)}, u32[]{:S(2)}, u32[]{:S(2)}) collective-permute-start(f32[1,128]{1,0:T(1,128)} %get-tuple-element.17), channel_id=1, source_target_pairs={{0,32},{32,64},{64,96},{96,0},{1,33},{33,65},{65,97},{97,1},{2,34}... | collective-permute-start | bytes 1544 | tf_op jit(solution)/shard_map/ppermute | solution.py:343
  76.1 5.2 %collective-permute-start = (f32[1,128]{1,0:T(1,128)}, f32[1,128]{1,0:T(1,128)S(1)}, u32[]{:S(2)}, u32[]{:S(2)}) collective-permute-start(f32[1,128]{1,0:T(1,128)} %get-tuple-element.17), channel_id=1, source_target_pairs={{0,64},{32,96},{64,0},{96,32},{1,65},{33,97},{65,1},{97,33},{2,66}... | collective-permute-start | bytes 1544 | tf_op jit(solution)/shard_map/ppermute | solution.py:343
  81.9 1.1 %collective-permute-start.3 = (f32[1,128]{1,0:T(1,128)S(1)}, f32[1,128]{1,0:T(1,128)S(1)}, u32[]{:S(2)}, u32[]{:S(2)}) collective-permute-start(f32[1,128]{1,0:T(1,128)S(1)} %add_add_fusion.2), channel_id=1, source_target_pairs={{0,1},{1,0},{2,3},{3,2},{4,5},{5,4},{6,7},{7,6},{8,9},{9,8},{10,11... | collective-permute-start | bytes 1544 | tf_op jit(solution)/shard_map/ppermute | solution.py:440
  83.1 8.4 %collective-permute-start.6 = (f32[1,128]{1,0:T(1,128)S(1)}, f32[1,128]{1,0:T(1,128)S(1)}, u32[]{:S(2)}, u32[]{:S(2)}) collective-permute-start(f32[1,128]{1,0:T(1,128)S(1)} %add.75), channel_id=1, source_target_pairs={{0,6},{1,7},{2,0},{3,1},{4,2},{5,3},{6,4},{7,5},{8,14},{9,15},{10,... | collective-permute-start | bytes 1544 | tf_op jit(solution)/shard_map/ppermute | solution.py:349
  86.0 5.5 %collective-permute-start.5 = (f32[1,128]{1,0:T(1,128)S(1)}, f32[1,128]{1,0:T(1,128)S(1)}, u32[]{:S(2)}, u32[]{:S(2)}) collective-permute-start(f32[1,128]{1,0:T(1,128)S(1)} %add.75), channel_id=1, source_target_pairs={{0,2},{1,3},{2,4},{3,5},{4,6},{5,7},{6,0},{7,1},{8,10},{9,11},{10,... | collective-permute-start | bytes 1544 | tf_op jit(solution)/shard_map/ppermute | solution.py:349
  86.0 5.5 %collective-permute-start.4 = (f32[1,128]{1,0:T(1,128)S(1)}, f32[1,128]{1,0:T(1,128)S(1)}, u32[]{:S(2)}, u32[]{:S(2)}) collective-permute-start(f32[1,128]{1,0:T(1,128)S(1)} %add.75), channel_id=1, source_target_pairs={{0,4},{1,5},{2,6},{3,7},{4,0},{5,1},{6,2},{7,3},{8,12},{9,13},{10,... | collective-permute-start | bytes 1544 | tf_op jit(solution)/shard_map/ppermute | solution.py:349
  91.5 4.6 %collective-permute-start.9 = (f32[1,128]{1,0:T(1,128)S(1)}, f32[1,128]{1,0:T(1,128)S(1)}, u32[]{:S(2)}, u32[]{:S(2)}) collective-permute-start(f32[1,128]{1,0:T(1,128)S(1)} %add_add_fusion.1), channel_id=1, source_target_pairs={{0,24},{1,25},{2,26},{3,27},{4,28},{5,29},{6,30},{7,31},{8,0},{9,1... | collective-permute-start | bytes 1544 | tf_op jit(solution)/shard_map/ppermute | solution.py:349
  93.9 4.8 %collective-permute-start.8 = (f32[1,128]{1,0:T(1,128)S(1)}, f32[1,128]{1,0:T(1,128)S(1)}, u32[]{:S(2)}, u32[]{:S(2)}) collective-permute-start(f32[1,128]{1,0:T(1,128)S(1)} %add_add_fusion.1), channel_id=1, source_target_pairs={{0,8},{1,9},{2,10},{3,11},{4,12},{5,13},{6,14},{7,15},{8,16},{9,17... | collective-permute-start | bytes 1544 | tf_op jit(solution)/shard_map/ppermute | solution.py:349
  93.9 5.0 %collective-permute-start.7 = (f32[1,128]{1,0:T(1,128)S(1)}, f32[1,128]{1,0:T(1,128)S(1)}, u32[]{:S(2)}, u32[]{:S(2)}) collective-permute-start(f32[1,128]{1,0:T(1,128)S(1)} %add_add_fusion.1), channel_id=1, source_target_pairs={{0,16},{1,17},{2,18},{3,19},{4,20},{5,21},{6,22},{7,23},{8,24},{9,... | collective-permute-start | bytes 1544 | tf_op jit(solution)/shard_map/ppermute | solution.py:349

commit v9 on v8

--- a/solution.py
+++ b/solution.py
@@ -293,7 +293,7 @@
         packed[pl.ds(pl.multiple_of(16 * m, 16), 16), 128:] = jnp.concatenate(halves, axis=0).astype(BF)
         return 0
 
-    lax.fori_loop(0, BATCH // 16, interact, 0, unroll=8)
+    lax.fori_loop(0, BATCH // 16, interact, 0, unroll=16)
 
     for fetch in fetches[2:]:
         fetch.wait()

time: 100 us -> 99.7 us (level)
  no operation moved by 1% of the time
where the time goes in v9:
time: 99.7 us; the launch traced here: 99.2 us
  waiting for transfers between devices  38.8 us (39%)
  starting transfers between devices  27.8 us (28%)
  Pallas kernels  22.8 us (23%)
  local copies, waits for them, and re-layouts  5.52 us (6%)
  between operations  1.63 us (2%)
  matrix products  1.39 us (1%)
  other arithmetic  1.21 us (1%)
    all_to_all x2, waiting for transfers between devices, exchange(): return lax.all_to_all(value, axes, split_axis=0, concat_axis=0, tiled=True)  30.2 us
    all_to_all x2, starting transfers between devices, exchange(): return lax.all_to_all(value, axes, split_axis=0, concat_axis=0, tiled=True)  15.6 us
    pallas_call x1, Pallas kernels, tail(): pl.pallas_call(tail_kernel, out_shape=(jax.ShapeDtypeStruct((1, BATCH), F...  12.4 us
    ppermute x6, starting transfers between devices, part_ring(): lax.ppermute(value, axis, [(i, i - i // step % 4 * step + (i // step + k)...  9.41 us
    pallas_call x1, Pallas kernels, pool(): pl.pallas_call(pool_kernel, out_shape=jax.ShapeDtypeStruct((128, ROWS, 12...  6.36 us
    ppermute x3, waiting for transfers between devices, ring_sum(): lax.ppermute(value, axis, [(i, (i + k) % 4) for i in range(4)])  4.48 us
    gather x1, local copies, waits for them, and re-layouts, per_device(): weights = jnp.take(padded, jnp.asarray(FEATURE_ROWS), axis=0)  4.21 us
    ppermute x6, waiting for transfers between devices, part_ring(): lax.ppermute(value, axis, [(i, i - i // step % 4 * step + (i // step + k)...  2.97 us
  transfers between devices with their start and end apart: 12, of which 8 were waited for; matrix products, arithmetic and copies ran while one was open for 8% of the time, Pallas kernels for 17%

profile of v9, /device:TPU:0, one launch (start us, length us, event | category | flops | bytes accessed | tf_op | source)
XLA Modules:
  0.0 99.2 jit_solution(1833907010607672607)
XLA Ops:
  0.6 6.4 %shard_map.240 = bf16[128,88,128]{2,1,0:T(8,128)(2,1)} custom-call(bf16[48,128,128]{2,1,0:T(8,128)(2,1)} %refs_0_.1, bf16[32,128,128]{2,1,0:T(8,128)(2,1)} %refs_1_.2, s32[48,8,128]{2,1,0:T(8,128)} %bitcast.16, s32[48,128]{1,0:T(8,128)} %refs_3_.1, s32[48,128]{1,0:T(8,128)} %refs_4_.1, s32[32,8,128]{2,1,0:T(8,128)} %bitcast.17, s32[32,128]{1,0:T(8,128)} %refs_6_.1, ...), custom_call_target="tpu_custom_call" | custom-call | flops 352321536 | bytes 6291456 | tf_op jit(solution)/shard_map/pallas_call | solution.py:188
  7.0 11.6 %all-to-all-start.1 = ((bf16[128,88,128]{2,1,0:T(8,128)(2,1)}), bf16[128,88,128]{2,1,0:T(8,128)(2,1)}, u32[]{:S(2)}, u32[]{:S(2)}) async-start(bf16[128,88,128]{2,1,0:T(8,128)(2,1)} %shard_map.240), calls=%async_computation.1 | async-start | bytes 5767168 | tf_op jit(solution)/shard_map/all_to_all | solution.py:339
  19.5 2.7 %shard_map.238 = bf16[64,128,128]{2,1,0:T(8,128)(2,1)} custom-call(s32[32]{0:T(128)S(1)} %bitcast.15, bf16[32,128,128]{2,1,0:T(8,128)(2,1)S(1)} %copy-done.1), custom_call_target="tpu_custom_call" | custom-call | bytes 3145728 | tf_op jit(solution)/shard_map/pallas_call | solution.py:91
  22.3 4.2 %gather_fusion = bf16[896,1024]{1,0:T(8,128)(2,1)} fusion(bf16[480,1024]{1,0:T(8,128)(2,1)S(1)} %concatenate.3, s32[1024]{0:T(1024)S(1)} %pad_clamp_fusion), kind=kCustom, calls=%fused_computation | custom fusion | bytes 3673600 | tf_op jit(solution)/shard_map/jit(_take)/gather | solution.py:422
  27.1 0.9 fusion.6.refs_2_
  28.6 0.6 broadcast_in_dim.41.refs_5_
  29.2 28.0 %all-to-all-done.1.refs_0_ = bf16[128,88,128]{2,1,0:T(8,128)(2,1)} async-done(((bf16[128,88,128]{2,1,0:T(8,128)(2,1)}), bf16[128,88,128]{2,1,0:T(8,128)(2,1)}, u32[]{:S(2)}, u32[]{:S(2)}) %all-to-all-start.1) | async-done | bytes 2883616 | tf_op jit(solution)/shard_map/all_to_all | solution.py:339
  57.2 4.0 %all-to-all-start = ((bf16[64,128,128]{2,1,0:T(8,128)(2,1)}), bf16[64,128,128]{2,1,0:T(8,128)(2,1)S(1)}, u32[]{:S(2)}, u32[]{:S(2)}) async-start(bf16[64,128,128]{2,1,0:T(8,128)(2,1)} %shard_map.238), calls=%async_computation | async-start | bytes 4194304 | tf_op jit(solution)/shard_map/all_to_all | solution.py:339
  61.2 12.4 %shard_map.241 = (f32[1,512]{1,0:T(1,128)}, f32[1,128]{1,0:T(1,128)}) custom-call(bf16[128,88,128]{2,1,0:T(8,128)(2,1)} %all-to-all-done.1.refs_0_, s32[8,128]{1,0:T(8,128)} %constant.30.clone.refs_1_, f32[512,128]{1,0:T(8,128)} %fusion.6.refs_2_, bf16[896,1024]{1,0:T(8,128)(2,1)} %gather_fusion, f32[1,1024]{1,0:T(1,128)} %bitcast.19, ...), custom_call_target="tpu_custom_call" | custom-call | flops 6442450944 | bytes 5242880 | tf_op jit(solution)/shard_map/pallas_call | solution.py:312
  73.6 1.1 %collective-permute-start.2 = (f32[1,128]{1,0:T(1,128)}, f32[1,128]{1,0:T(1,128)S(1)}, u32[]{:S(2)}, u32[]{:S(2)}) collective-permute-start(f32[1,128]{1,0:T(1,128)} %get-tuple-element.17), channel_id=1, source_target_pairs={{0,96},{32,0},{64,32},{96,64},{1,97},{33,1},{65,33},{97,65},{2,98}... | collective-permute-start | bytes 1544 | tf_op jit(solution)/shard_map/ppermute | solution.py:343
  74.7 1.0 collective-permute-start.1
  75.6 0.7 collective-permute-start
  76.3 1.0 collective-permute-done.2
  77.3 2.2 %collective-permute-done.1 = f32[1,128]{1,0:T(1,128)S(1)} collective-permute-done((f32[1,128]{1,0:T(1,128)}, f32[1,128]{1,0:T(1,128)S(1)}, u32[]{:S(2)}, u32[]{:S(2)}) %collective-permute-start.1) | collective-permute-done | bytes 544 | tf_op jit(solution)/shard_map/ppermute | solution.py:343
  79.5 1.3 %collective-permute-done = f32[1,128]{1,0:T(1,128)S(1)} collective-permute-done((f32[1,128]{1,0:T(1,128)}, f32[1,128]{1,0:T(1,128)S(1)}, u32[]{:S(2)}, u32[]{:S(2)}) %collective-permute-start) | collective-permute-done | bytes 544 | tf_op jit(solution)/shard_map/ppermute | solution.py:343
  80.8 0.7 add_add_fusion.2
  81.5 1.1 %collective-permute-done.3 = f32[1,128]{1,0:T(1,128)S(1)} collective-permute-done((f32[1,128]{1,0:T(1,128)S(1)}, f32[1,128]{1,0:T(1,128)S(1)}, u32[]{:S(2)}, u32[]{:S(2)}) %collective-permute-start.3) | collective-permute-done | bytes 544 | tf_op jit(solution)/shard_map/ppermute | solution.py:440
  82.6 2.9 %collective-permute-start.6 = (f32[1,128]{1,0:T(1,128)S(1)}, f32[1,128]{1,0:T(1,128)S(1)}, u32[]{:S(2)}, u32[]{:S(2)}) collective-permute-start(f32[1,128]{1,0:T(1,128)S(1)} %add.75), channel_id=1, source_target_pairs={{0,6},{1,7},{2,0},{3,1},{4,2},{5,3},{6,4},{7,5},{8,14},{9,15},{10,... | collective-permute-start | bytes 1544 | tf_op jit(solution)/shard_map/ppermute | solution.py:349
  85.5 2.3 %collective-permute-start.4 = (f32[1,128]{1,0:T(1,128)S(1)}, f32[1,128]{1,0:T(1,128)S(1)}, u32[]{:S(2)}, u32[]{:S(2)}) collective-permute-start(f32[1,128]{1,0:T(1,128)S(1)} %add.75), channel_id=1, source_target_pairs={{0,4},{1,5},{2,6},{3,7},{4,0},{5,1},{6,2},{7,3},{8,12},{9,13},{10,... | collective-permute-start | bytes 1544 | tf_op jit(solution)/shard_map/ppermute | solution.py:349
  87.8 2.2 %all-to-all-done.given = bf16[64,128,128]{2,1,0:T(8,128)(2,1)S(1)} async-done(((bf16[64,128,128]{2,1,0:T(8,128)(2,1)}), bf16[64,128,128]{2,1,0:T(8,128)(2,1)S(1)}, u32[]{:S(2)}, u32[]{:S(2)}) %all-to-all-start) | async-done | bytes 2097184 | tf_op jit(solution)/shard_map/all_to_all | solution.py:339
  90.1 1.4 %shard_map.239 = bf16[64,128,128]{2,1,0:T(8,128)(2,1)} custom-call(bf16[64,128,128]{2,1,0:T(8,128)(2,1)S(1)} %all-to-all-done.given), custom_call_target="tpu_custom_call" | custom-call | bytes 4194304 | tf_op jit(solution)/shard_map/pallas_call | solution.py:367
  91.5 1.9 %collective-permute-start.9 = (f32[1,128]{1,0:T(1,128)S(1)}, f32[1,128]{1,0:T(1,128)S(1)}, u32[]{:S(2)}, u32[]{:S(2)}) collective-permute-start(f32[1,128]{1,0:T(1,128)S(1)} %add_add_fusion.1), channel_id=1, source_target_pairs={{0,24},{1,25},{2,26},{3,27},{4,28},{5,29},{6,30},{7,31},{8,0},{9,1... | collective-permute-start | bytes 1544 | tf_op jit(solution)/shard_map/ppermute | solution.py:349
  93.6 2.1 %collective-permute-start.7 = (f32[1,128]{1,0:T(1,128)S(1)}, f32[1,128]{1,0:T(1,128)S(1)}, u32[]{:S(2)}, u32[]{:S(2)}) collective-permute-start(f32[1,128]{1,0:T(1,128)S(1)} %add_add_fusion.1), channel_id=1, source_target_pairs={{0,16},{1,17},{2,18},{3,19},{4,20},{5,21},{6,22},{7,23},{8,24},{9,... | collective-permute-start | bytes 1544 | tf_op jit(solution)/shard_map/ppermute | solution.py:349
  95.7 2.5 %collective-permute-done.8 = f32[1,128]{1,0:T(1,128)S(1)} collective-permute-done((f32[1,128]{1,0:T(1,128)S(1)}, f32[1,128]{1,0:T(1,128)S(1)}, u32[]{:S(2)}, u32[]{:S(2)}) %collective-permute-start.8) | collective-permute-done | bytes 544 | tf_op jit(solution)/shard_map/ppermute | solution.py:349
  (40 shorter events, 2.4 us)
Async XLA Ops:
  0.6 25.9 %copy-start = (bf16[512,256]{1,0:T(8,128)(2,1)S(1)}, bf16[512,256]{1,0:T(8,128)(2,1)}, u32[]{:S(2)}) copy-start(bf16[512,256]{1,0:T(8,128)(2,1)} %param.36) | copy-start | bytes 786436
  7.0 12.4 %copy-start.1 = (bf16[32,128,128]{2,1,0:T(8,128)(2,1)S(1)}, bf16[32,128,128]{2,1,0:T(8,128)(2,1)}, u32[]{:S(2)}) copy-start(bf16[32,128,128]{2,1,0:T(8,128)(2,1)} %refs_1_.2) | copy-start | bytes 3145732
  7.0 12.4 %copy-start.2 = (s32[32,1]{0,1:T(1,128)S(1)}, s32[32,1]{0,1:T(1,128)}, u32[]{:S(2)}) copy-start(s32[32,1]{0,1:T(1,128)} %param.31) | copy-start | bytes 388
  7.0 50.1 %all-to-all-start.1 = ((bf16[128,88,128]{2,1,0:T(8,128)(2,1)}), bf16[128,88,128]{2,1,0:T(8,128)(2,1)}, u32[]{:S(2)}, u32[]{:S(2)}) async-start(bf16[128,88,128]{2,1,0:T(8,128)(2,1)} %shard_map.240), calls=%async_computation.1 | async-start | bytes 5767168 | tf_op jit(solution)/shard_map/all_to_all | solution.py:339
  18.7 3.5 %copy-start.6 = (bf16[1024,1]{0,1:T(2,128)(2,1)S(1)}, bf16[1024,1]{0,1:T(2,128)(2,1)}, u32[]{:S(2)}) copy-start(bf16[1024,1]{0,1:T(2,128)(2,1)} %param.42) | copy-start | bytes 6148
  18.7 3.5 %copy-start.3 = (bf16[479,1024]{1,0:T(8,128)(2,1)S(1)}, bf16[479,1024]{1,0:T(8,128)(2,1)}, u32[]{:S(2)}) copy-start(bf16[479,1024]{1,0:T(8,128)(2,1)} %param.40) | copy-start | bytes 2942980
  19.4 2.8 %copy-start.5 = (s32[896]{0:T(1024)S(1)}, s32[896]{0:T(1024)}, u32[]{:S(2)}) copy-start(s32[896]{0:T(1024)} %constant.50) | copy-start | bytes 10756
  22.3 4.3 %copy-start.8 = (bf16[512,13]{0,1:T(8,128)(2,1)S(1)}, bf16[512,13]{0,1:T(8,128)(2,1)}, u32[]{:S(2)}) copy-start(bf16[512,13]{0,1:T(8,128)(2,1)} %param.32) | copy-start | bytes 39940
  22.3 4.3 %copy-start.9 = (bf16[13,512]{1,0:T(8,128)(2,1)S(1)}, bf16[13,512]{1,0:T(8,128)(2,1)}, u32[]{:S(2)}) copy-start(bf16[13,512]{1,0:T(8,128)(2,1)} %param.34) | copy-start | bytes 39940
  22.3 4.3 %copy-start.10 = (f32[512]{0:T(512)S(1)}, f32[512]{0:T(512)}, u32[]{:S(2)}) copy-start(f32[512]{0:T(512)} %param.35) | copy-start | bytes 6148
  22.3 4.3 %copy-start.11 = (f32[256]{0:T(256)S(1)}, f32[256]{0:T(256)}, u32[]{:S(2)}) copy-start(f32[256]{0:T(256)} %param.37) | copy-start | bytes 3076
  22.3 4.7 %copy-start.4 = (bf16[256,128]{1,0:T(8,128)(2,1)S(1)}, bf16[256,128]{1,0:T(8,128)(2,1)}, u32[]{:S(2)}) copy-start(bf16[256,128]{1,0:T(8,128)(2,1)} %param.38) | copy-start | bytes 196612
  22.3 4.7 %copy-start.7 = (f32[128]{0:T(128)S(1)}, f32[128]{0:T(128)}, u32[]{:S(2)}) copy-start(f32[128]{0:T(128)} %param.39) | copy-start | bytes 1540
  57.2 32.9 %all-to-all-start = ((bf16[64,128,128]{2,1,0:T(8,128)(2,1)}), bf16[64,128,128]{2,1,0:T(8,128)(2,1)S(1)}, u32[]{:S(2)}, u32[]{:S(2)}) async-start(bf16[64,128,128]{2,1,0:T(8,128)(2,1)} %shard_map.238), calls=%async_computation | async-start | bytes 4194304 | tf_op jit(solution)/shard_map/all_to_all | solution.py:339
  73.6 3.7 %collective-permute-start.2 = (f32[1,128]{1,0:T(1,128)}, f32[1,128]{1,0:T(1,128)S(1)}, u32[]{:S(2)}, u32[]{:S(2)}) collective-permute-start(f32[1,128]{1,0:T(1,128)} %get-tuple-element.17), channel_id=1, source_target_pairs={{0,96},{32,0},{64,32},{96,64},{1,97},{33,1},{65,33},{97,65},{2,98}... | collective-permute-start | bytes 1544 | tf_op jit(solution)/shard_map/ppermute | solution.py:343
  74.7 4.9 %collective-permute-start.1 = (f32[1,128]{1,0:T(1,128)}, f32[1,128]{1,0:T(1,128)S(1)}, u32[]{:S(2)}, u32[]{:S(2)}) collective-permute-start(f32[1,128]{1,0:T(1,128)} %get-tuple-element.17), channel_id=1, source_target_pairs={{0,32},{32,64},{64,96},{96,0},{1,33},{33,65},{65,97},{97,1},{2,34}... | collective-permute-start | bytes 1544 | tf_op jit(solution)/shard_map/ppermute | solution.py:343
  75.6 5.2 %collective-permute-start = (f32[1,128]{1,0:T(1,128)}, f32[1,128]{1,0:T(1,128)S(1)}, u32[]{:S(2)}, u32[]{:S(2)}) collective-permute-start(f32[1,128]{1,0:T(1,128)} %get-tuple-element.17), channel_id=1, source_target_pairs={{0,64},{32,96},{64,0},{96,32},{1,65},{33,97},{65,1},{97,33},{2,66}... | collective-permute-start | bytes 1544 | tf_op jit(solution)/shard_map/ppermute | solution.py:343
  81.5 1.1 %collective-permute-start.3 = (f32[1,128]{1,0:T(1,128)S(1)}, f32[1,128]{1,0:T(1,128)S(1)}, u32[]{:S(2)}, u32[]{:S(2)}) collective-permute-start(f32[1,128]{1,0:T(1,128)S(1)} %add_add_fusion.2), channel_id=1, source_target_pairs={{0,1},{1,0},{2,3},{3,2},{4,5},{5,4},{6,7},{7,6},{8,9},{9,8},{10,11... | collective-permute-start | bytes 1544 | tf_op jit(solution)/shard_map/ppermute | solution.py:440
  82.6 8.9 %collective-permute-start.6 = (f32[1,128]{1,0:T(1,128)S(1)}, f32[1,128]{1,0:T(1,128)S(1)}, u32[]{:S(2)}, u32[]{:S(2)}) collective-permute-start(f32[1,128]{1,0:T(1,128)S(1)} %add.75), channel_id=1, source_target_pairs={{0,6},{1,7},{2,0},{3,1},{4,2},{5,3},{6,4},{7,5},{8,14},{9,15},{10,... | collective-permute-start | bytes 1544 | tf_op jit(solution)/shard_map/ppermute | solution.py:349
  85.5 5.9 %collective-permute-start.5 = (f32[1,128]{1,0:T(1,128)S(1)}, f32[1,128]{1,0:T(1,128)S(1)}, u32[]{:S(2)}, u32[]{:S(2)}) collective-permute-start(f32[1,128]{1,0:T(1,128)S(1)} %add.75), channel_id=1, source_target_pairs={{0,2},{1,3},{2,4},{3,5},{4,6},{5,7},{6,0},{7,1},{8,10},{9,11},{10,... | collective-permute-start | bytes 1544 | tf_op jit(solution)/shard_map/ppermute | solution.py:349
  85.5 5.9 %collective-permute-start.4 = (f32[1,128]{1,0:T(1,128)S(1)}, f32[1,128]{1,0:T(1,128)S(1)}, u32[]{:S(2)}, u32[]{:S(2)}) collective-permute-start(f32[1,128]{1,0:T(1,128)S(1)} %add.75), channel_id=1, source_target_pairs={{0,4},{1,5},{2,6},{3,7},{4,0},{5,1},{6,2},{7,3},{8,12},{9,13},{10,... | collective-permute-start | bytes 1544 | tf_op jit(solution)/shard_map/ppermute | solution.py:349
  91.5 4.2 %collective-permute-start.9 = (f32[1,128]{1,0:T(1,128)S(1)}, f32[1,128]{1,0:T(1,128)S(1)}, u32[]{:S(2)}, u32[]{:S(2)}) collective-permute-start(f32[1,128]{1,0:T(1,128)S(1)} %add_add_fusion.1), channel_id=1, source_target_pairs={{0,24},{1,25},{2,26},{3,27},{4,28},{5,29},{6,30},{7,31},{8,0},{9,1... | collective-permute-start | bytes 1544 | tf_op jit(solution)/shard_map/ppermute | solution.py:349
  93.4 4.8 %collective-permute-start.8 = (f32[1,128]{1,0:T(1,128)S(1)}, f32[1,128]{1,0:T(1,128)S(1)}, u32[]{:S(2)}, u32[]{:S(2)}) collective-permute-start(f32[1,128]{1,0:T(1,128)S(1)} %add_add_fusion.1), channel_id=1, source_target_pairs={{0,8},{1,9},{2,10},{3,11},{4,12},{5,13},{6,14},{7,15},{8,16},{9,17... | collective-permute-start | bytes 1544 | tf_op jit(solution)/shard_map/ppermute | solution.py:349
  93.6 5.0 %collective-permute-start.7 = (f32[1,128]{1,0:T(1,128)S(1)}, f32[1,128]{1,0:T(1,128)S(1)}, u32[]{:S(2)}, u32[]{:S(2)}) collective-permute-start(f32[1,128]{1,0:T(1,128)S(1)} %add_add_fusion.1), channel_id=1, source_target_pairs={{0,16},{1,17},{2,18},{3,19},{4,20},{5,21},{6,22},{7,23},{8,24},{9,... | collective-permute-start | bytes 1544 | tf_op jit(solution)/shard_map/ppermute | solution.py:349

commit v10 on v9

--- a/solution.py
+++ b/solution.py
@@ -191,7 +191,7 @@
         in_specs=[pl.BlockSpec(memory_space=pl.ANY)] * 8,
         out_specs=pl.BlockSpec(memory_space=pl.ANY),
         scratch_shapes=[
-            pltpu.VMEM((128 * ROWS, 128), F32),
+            pltpu.VMEM((129 * ROWS, 128), F32),
             pltpu.VMEM((128, 128), jnp.int32),
             pltpu.VMEM((128, ROWS, 128), BF),
         ]
@@ -316,7 +316,7 @@
         out_specs=(VMEM, VMEM),
         scratch_shapes=[pltpu.VMEM(a.shape, a.dtype) for a in (given,) + others]
         + [
-            pltpu.VMEM((128 * ROWS, 128), F32),
+            pltpu.VMEM((129 * ROWS, 128), F32),
             pltpu.VMEM((128, 128), F32),
             pltpu.VMEM((128, 128), F32),
             pltpu.VMEM((F + 1, BATCH, 128), F32),

time: 99.7 us -> 99.7 us (level)
  no operation moved by 1% of the time
where the time goes in v10:
time: 99.7 us; the launch traced here: 99.2 us
  waiting for transfers between devices  38.7 us (39%)
  starting transfers between devices  27.9 us (28%)
  Pallas kernels  22.8 us (23%)
  local copies, waits for them, and re-layouts  5.52 us (6%)
  between operations  1.63 us (2%)
  matrix products  1.39 us (1%)
  other arithmetic  1.21 us (1%)
    all_to_all x2, waiting for transfers between devices, exchange(): return lax.all_to_all(value, axes, split_axis=0, concat_axis=0, tiled=True)  30.2 us
    all_to_all x2, starting transfers between devices, exchange(): return lax.all_to_all(value, axes, split_axis=0, concat_axis=0, tiled=True)  15.6 us
    pallas_call x1, Pallas kernels, tail(): pl.pallas_call(tail_kernel, out_shape=(jax.ShapeDtypeStruct((1, BATCH), F...  12.4 us
    ppermute x6, starting transfers between devices, part_ring(): lax.ppermute(value, axis, [(i, i - i // step % 4 * step + (i // step + k)...  9.47 us
    pallas_call x1, Pallas kernels, pool(): pl.pallas_call(pool_kernel, out_shape=jax.ShapeDtypeStruct((128, ROWS, 12...  6.36 us
    ppermute x3, waiting for transfers between devices, ring_sum(): lax.ppermute(value, axis, [(i, (i + k) % 4) for i in range(4)])  4.48 us
    gather x1, local copies, waits for them, and re-layouts, per_device(): weights = jnp.take(padded, jnp.asarray(FEATURE_ROWS), axis=0)  4.21 us
    ppermute x6, waiting for transfers between devices, part_ring(): lax.ppermute(value, axis, [(i, i - i // step % 4 * step + (i // step + k)...  2.91 us
  transfers between devices with their start and end apart: 12, of which 8 were waited for; matrix products, arithmetic and copies ran while one was open for 8% of the time, Pallas kernels for 17%

profile of v10, /device:TPU:0, one launch (start us, length us, event | category | flops | bytes accessed | tf_op | source)
XLA Modules:
  0.0 99.2 jit_solution(15281800739022678905)
XLA Ops:
  0.6 6.4 %shard_map.240 = bf16[128,88,128]{2,1,0:T(8,128)(2,1)} custom-call(bf16[48,128,128]{2,1,0:T(8,128)(2,1)} %refs_0_.1, bf16[32,128,128]{2,1,0:T(8,128)(2,1)} %refs_1_.2, s32[48,8,128]{2,1,0:T(8,128)} %bitcast.16, s32[48,128]{1,0:T(8,128)} %refs_3_.1, s32[48,128]{1,0:T(8,128)} %refs_4_.1, s32[32,8,128]{2,1,0:T(8,128)} %bitcast.17, s32[32,128]{1,0:T(8,128)} %refs_6_.1, ...), custom_call_target="tpu_custom_call" | custom-call | flops 352321536 | bytes 6291456 | tf_op jit(solution)/shard_map/pallas_call | solution.py:188
  7.0 11.6 %all-to-all-start.1 = ((bf16[128,88,128]{2,1,0:T(8,128)(2,1)}), bf16[128,88,128]{2,1,0:T(8,128)(2,1)}, u32[]{:S(2)}, u32[]{:S(2)}) async-start(bf16[128,88,128]{2,1,0:T(8,128)(2,1)} %shard_map.240), calls=%async_computation.1 | async-start | bytes 5767168 | tf_op jit(solution)/shard_map/all_to_all | solution.py:339
  19.5 2.7 %shard_map.238 = bf16[64,128,128]{2,1,0:T(8,128)(2,1)} custom-call(s32[32]{0:T(128)S(1)} %bitcast.15, bf16[32,128,128]{2,1,0:T(8,128)(2,1)S(1)} %copy-done.1), custom_call_target="tpu_custom_call" | custom-call | bytes 3145728 | tf_op jit(solution)/shard_map/pallas_call | solution.py:91
  22.3 4.2 %gather_fusion = bf16[896,1024]{1,0:T(8,128)(2,1)} fusion(bf16[480,1024]{1,0:T(8,128)(2,1)S(1)} %concatenate.3, s32[1024]{0:T(1024)S(1)} %pad_clamp_fusion), kind=kCustom, calls=%fused_computation | custom fusion | bytes 3673600 | tf_op jit(solution)/shard_map/jit(_take)/gather | solution.py:422
  27.1 0.9 fusion.6.refs_2_
  28.6 0.6 broadcast_in_dim.41.refs_5_
  29.2 28.0 %all-to-all-done.1.refs_0_ = bf16[128,88,128]{2,1,0:T(8,128)(2,1)} async-done(((bf16[128,88,128]{2,1,0:T(8,128)(2,1)}), bf16[128,88,128]{2,1,0:T(8,128)(2,1)}, u32[]{:S(2)}, u32[]{:S(2)}) %all-to-all-start.1) | async-done | bytes 2883616 | tf_op jit(solution)/shard_map/all_to_all | solution.py:339
  57.2 4.0 %all-to-all-start = ((bf16[64,128,128]{2,1,0:T(8,128)(2,1)}), bf16[64,128,128]{2,1,0:T(8,128)(2,1)S(1)}, u32[]{:S(2)}, u32[]{:S(2)}) async-start(bf16[64,128,128]{2,1,0:T(8,128)(2,1)} %shard_map.238), calls=%async_computation | async-start | bytes 4194304 | tf_op jit(solution)/shard_map/all_to_all | solution.py:339
  61.2 12.4 %shard_map.241 = (f32[1,512]{1,0:T(1,128)}, f32[1,128]{1,0:T(1,128)}) custom-call(bf16[128,88,128]{2,1,0:T(8,128)(2,1)} %all-to-all-done.1.refs_0_, s32[8,128]{1,0:T(8,128)} %constant.30.clone.refs_1_, f32[512,128]{1,0:T(8,128)} %fusion.6.refs_2_, bf16[896,1024]{1,0:T(8,128)(2,1)} %gather_fusion, f32[1,1024]{1,0:T(1,128)} %bitcast.19, ...), custom_call_target="tpu_custom_call" | custom-call | flops 6442450944 | bytes 5242880 | tf_op jit(solution)/shard_map/pallas_call | solution.py:312
  73.6 1.1 %collective-permute-start.2 = (f32[1,128]{1,0:T(1,128)}, f32[1,128]{1,0:T(1,128)S(1)}, u32[]{:S(2)}, u32[]{:S(2)}) collective-permute-start(f32[1,128]{1,0:T(1,128)} %get-tuple-element.17), channel_id=1, source_target_pairs={{0,96},{32,0},{64,32},{96,64},{1,97},{33,1},{65,33},{97,65},{2,98}... | collective-permute-start | bytes 1544 | tf_op jit(solution)/shard_map/ppermute | solution.py:343
  74.7 1.0 collective-permute-start.1
  75.7 0.7 collective-permute-start
  76.4 1.0 collective-permute-done.2
  77.3 2.2 %collective-permute-done.1 = f32[1,128]{1,0:T(1,128)S(1)} collective-permute-done((f32[1,128]{1,0:T(1,128)}, f32[1,128]{1,0:T(1,128)S(1)}, u32[]{:S(2)}, u32[]{:S(2)}) %collective-permute-start.1) | collective-permute-done | bytes 544 | tf_op jit(solution)/shard_map/ppermute | solution.py:343
  79.6 1.3 %collective-permute-done = f32[1,128]{1,0:T(1,128)S(1)} collective-permute-done((f32[1,128]{1,0:T(1,128)}, f32[1,128]{1,0:T(1,128)S(1)}, u32[]{:S(2)}, u32[]{:S(2)}) %collective-permute-start) | collective-permute-done | bytes 544 | tf_op jit(solution)/shard_map/ppermute | solution.py:343
  80.9 0.7 add_add_fusion.2
  81.5 1.1 %collective-permute-done.3 = f32[1,128]{1,0:T(1,128)S(1)} collective-permute-done((f32[1,128]{1,0:T(1,128)S(1)}, f32[1,128]{1,0:T(1,128)S(1)}, u32[]{:S(2)}, u32[]{:S(2)}) %collective-permute-start.3) | collective-permute-done | bytes 544 | tf_op jit(solution)/shard_map/ppermute | solution.py:440
  82.7 2.9 %collective-permute-start.6 = (f32[1,128]{1,0:T(1,128)S(1)}, f32[1,128]{1,0:T(1,128)S(1)}, u32[]{:S(2)}, u32[]{:S(2)}) collective-permute-start(f32[1,128]{1,0:T(1,128)S(1)} %add.75), channel_id=1, source_target_pairs={{0,6},{1,7},{2,0},{3,1},{4,2},{5,3},{6,4},{7,5},{8,14},{9,15},{10,... | collective-permute-start | bytes 1544 | tf_op jit(solution)/shard_map/ppermute | solution.py:349
  85.6 2.3 %collective-permute-start.4 = (f32[1,128]{1,0:T(1,128)S(1)}, f32[1,128]{1,0:T(1,128)S(1)}, u32[]{:S(2)}, u32[]{:S(2)}) collective-permute-start(f32[1,128]{1,0:T(1,128)S(1)} %add.75), channel_id=1, source_target_pairs={{0,4},{1,5},{2,6},{3,7},{4,0},{5,1},{6,2},{7,3},{8,12},{9,13},{10,... | collective-permute-start | bytes 1544 | tf_op jit(solution)/shard_map/ppermute | solution.py:349
  87.9 2.2 %all-to-all-done.given = bf16[64,128,128]{2,1,0:T(8,128)(2,1)S(1)} async-done(((bf16[64,128,128]{2,1,0:T(8,128)(2,1)}), bf16[64,128,128]{2,1,0:T(8,128)(2,1)S(1)}, u32[]{:S(2)}, u32[]{:S(2)}) %all-to-all-start) | async-done | bytes 2097184 | tf_op jit(solution)/shard_map/all_to_all | solution.py:339
  90.1 1.4 %shard_map.239 = bf16[64,128,128]{2,1,0:T(8,128)(2,1)} custom-call(bf16[64,128,128]{2,1,0:T(8,128)(2,1)S(1)} %all-to-all-done.given), custom_call_target="tpu_custom_call" | custom-call | bytes 4194304 | tf_op jit(solution)/shard_map/pallas_call | solution.py:367
  91.5 2.0 %collective-permute-start.9 = (f32[1,128]{1,0:T(1,128)S(1)}, f32[1,128]{1,0:T(1,128)S(1)}, u32[]{:S(2)}, u32[]{:S(2)}) collective-permute-start(f32[1,128]{1,0:T(1,128)S(1)} %add_add_fusion.1), channel_id=1, source_target_pairs={{0,24},{1,25},{2,26},{3,27},{4,28},{5,29},{6,30},{7,31},{8,0},{9,1... | collective-permute-start | bytes 1544 | tf_op jit(solution)/shard_map/ppermute | solution.py:349
  93.6 2.1 %collective-permute-start.7 = (f32[1,128]{1,0:T(1,128)S(1)}, f32[1,128]{1,0:T(1,128)S(1)}, u32[]{:S(2)}, u32[]{:S(2)}) collective-permute-start(f32[1,128]{1,0:T(1,128)S(1)} %add_add_fusion.1), channel_id=1, source_target_pairs={{0,16},{1,17},{2,18},{3,19},{4,20},{5,21},{6,22},{7,23},{8,24},{9,... | collective-permute-start | bytes 1544 | tf_op jit(solution)/shard_map/ppermute | solution.py:349
  95.7 2.5 %collective-permute-done.8 = f32[1,128]{1,0:T(1,128)S(1)} collective-permute-done((f32[1,128]{1,0:T(1,128)S(1)}, f32[1,128]{1,0:T(1,128)S(1)}, u32[]{:S(2)}, u32[]{:S(2)}) %collective-permute-start.8) | collective-permute-done | bytes 544 | tf_op jit(solution)/shard_map/ppermute | solution.py:349
  (40 shorter events, 2.3 us)
Async XLA Ops:
  0.6 25.9 %copy-start = (bf16[512,256]{1,0:T(8,128)(2,1)S(1)}, bf16[512,256]{1,0:T(8,128)(2,1)}, u32[]{:S(2)}) copy-start(bf16[512,256]{1,0:T(8,128)(2,1)} %param.36) | copy-start | bytes 786436
  7.0 12.4 %copy-start.1 = (bf16[32,128,128]{2,1,0:T(8,128)(2,1)S(1)}, bf16[32,128,128]{2,1,0:T(8,128)(2,1)}, u32[]{:S(2)}) copy-start(bf16[32,128,128]{2,1,0:T(8,128)(2,1)} %refs_1_.2) | copy-start | bytes 3145732
  7.0 12.4 %copy-start.2 = (s32[32,1]{0,1:T(1,128)S(1)}, s32[32,1]{0,1:T(1,128)}, u32[]{:S(2)}) copy-start(s32[32,1]{0,1:T(1,128)} %param.31) | copy-start | bytes 388
  7.0 50.1 %all-to-all-start.1 = ((bf16[128,88,128]{2,1,0:T(8,128)(2,1)}), bf16[128,88,128]{2,1,0:T(8,128)(2,1)}, u32[]{:S(2)}, u32[]{:S(2)}) async-start(bf16[128,88,128]{2,1,0:T(8,128)(2,1)} %shard_map.240), calls=%async_computation.1 | async-start | bytes 5767168 | tf_op jit(solution)/shard_map/all_to_all | solution.py:339
  18.7 3.5 %copy-start.6 = (bf16[1024,1]{0,1:T(2,128)(2,1)S(1)}, bf16[1024,1]{0,1:T(2,128)(2,1)}, u32[]{:S(2)}) copy-start(bf16[1024,1]{0,1:T(2,128)(2,1)} %param.42) | copy-start | bytes 6148
  18.7 3.5 %copy-start.3 = (bf16[479,1024]{1,0:T(8,128)(2,1)S(1)}, bf16[479,1024]{1,0:T(8,128)(2,1)}, u32[]{:S(2)}) copy-start(bf16[479,1024]{1,0:T(8,128)(2,1)} %param.40) | copy-start | bytes 2942980
  19.4 2.8 %copy-start.5 = (s32[896]{0:T(1024)S(1)}, s32[896]{0:T(1024)}, u32[]{:S(2)}) copy-start(s32[896]{0:T(1024)} %constant.50) | copy-start | bytes 10756
  22.3 4.3 %copy-start.8 = (bf16[512,13]{0,1:T(8,128)(2,1)S(1)}, bf16[512,13]{0,1:T(8,128)(2,1)}, u32[]{:S(2)}) copy-start(bf16[512,13]{0,1:T(8,128)(2,1)} %param.32) | copy-start | bytes 39940
  22.3 4.3 %copy-start.9 = (bf16[13,512]{1,0:T(8,128)(2,1)S(1)}, bf16[13,512]{1,0:T(8,128)(2,1)}, u32[]{:S(2)}) copy-start(bf16[13,512]{1,0:T(8,128)(2,1)} %param.34) | copy-start | bytes 39940
  22.3 4.3 %copy-start.10 = (f32[512]{0:T(512)S(1)}, f32[512]{0:T(512)}, u32[]{:S(2)}) copy-start(f32[512]{0:T(512)} %param.35) | copy-start | bytes 6148
  22.3 4.3 %copy-start.11 = (f32[256]{0:T(256)S(1)}, f32[256]{0:T(256)}, u32[]{:S(2)}) copy-start(f32[256]{0:T(256)} %param.37) | copy-start | bytes 3076
  22.3 4.7 %copy-start.4 = (bf16[256,128]{1,0:T(8,128)(2,1)S(1)}, bf16[256,128]{1,0:T(8,128)(2,1)}, u32[]{:S(2)}) copy-start(bf16[256,128]{1,0:T(8,128)(2,1)} %param.38) | copy-start | bytes 196612
  22.3 4.7 %copy-start.7 = (f32[128]{0:T(128)S(1)}, f32[128]{0:T(128)}, u32[]{:S(2)}) copy-start(f32[128]{0:T(128)} %param.39) | copy-start | bytes 1540
  57.2 32.9 %all-to-all-start = ((bf16[64,128,128]{2,1,0:T(8,128)(2,1)}), bf16[64,128,128]{2,1,0:T(8,128)(2,1)S(1)}, u32[]{:S(2)}, u32[]{:S(2)}) async-start(bf16[64,128,128]{2,1,0:T(8,128)(2,1)} %shard_map.238), calls=%async_computation | async-start | bytes 4194304 | tf_op jit(solution)/shard_map/all_to_all | solution.py:339
  73.6 3.7 %collective-permute-start.2 = (f32[1,128]{1,0:T(1,128)}, f32[1,128]{1,0:T(1,128)S(1)}, u32[]{:S(2)}, u32[]{:S(2)}) collective-permute-start(f32[1,128]{1,0:T(1,128)} %get-tuple-element.17), channel_id=1, source_target_pairs={{0,96},{32,0},{64,32},{96,64},{1,97},{33,1},{65,33},{97,65},{2,98}... | collective-permute-start | bytes 1544 | tf_op jit(solution)/shard_map/ppermute | solution.py:343
  74.7 4.9 %collective-permute-start.1 = (f32[1,128]{1,0:T(1,128)}, f32[1,128]{1,0:T(1,128)S(1)}, u32[]{:S(2)}, u32[]{:S(2)}) collective-permute-start(f32[1,128]{1,0:T(1,128)} %get-tuple-element.17), channel_id=1, source_target_pairs={{0,32},{32,64},{64,96},{96,0},{1,33},{33,65},{65,97},{97,1},{2,34}... | collective-permute-start | bytes 1544 | tf_op jit(solution)/shard_map/ppermute | solution.py:343
  75.7 5.2 %collective-permute-start = (f32[1,128]{1,0:T(1,128)}, f32[1,128]{1,0:T(1,128)S(1)}, u32[]{:S(2)}, u32[]{:S(2)}) collective-permute-start(f32[1,128]{1,0:T(1,128)} %get-tuple-element.17), channel_id=1, source_target_pairs={{0,64},{32,96},{64,0},{96,32},{1,65},{33,97},{65,1},{97,33},{2,66}... | collective-permute-start | bytes 1544 | tf_op jit(solution)/shard_map/ppermute | solution.py:343
  81.5 1.1 %collective-permute-start.3 = (f32[1,128]{1,0:T(1,128)S(1)}, f32[1,128]{1,0:T(1,128)S(1)}, u32[]{:S(2)}, u32[]{:S(2)}) collective-permute-start(f32[1,128]{1,0:T(1,128)S(1)} %add_add_fusion.2), channel_id=1, source_target_pairs={{0,1},{1,0},{2,3},{3,2},{4,5},{5,4},{6,7},{7,6},{8,9},{9,8},{10,11... | collective-permute-start | bytes 1544 | tf_op jit(solution)/shard_map/ppermute | solution.py:440
  82.7 8.8 %collective-permute-start.6 = (f32[1,128]{1,0:T(1,128)S(1)}, f32[1,128]{1,0:T(1,128)S(1)}, u32[]{:S(2)}, u32[]{:S(2)}) collective-permute-start(f32[1,128]{1,0:T(1,128)S(1)} %add.75), channel_id=1, source_target_pairs={{0,6},{1,7},{2,0},{3,1},{4,2},{5,3},{6,4},{7,5},{8,14},{9,15},{10,... | collective-permute-start | bytes 1544 | tf_op jit(solution)/shard_map/ppermute | solution.py:349
  85.6 5.9 %collective-permute-start.5 = (f32[1,128]{1,0:T(1,128)S(1)}, f32[1,128]{1,0:T(1,128)S(1)}, u32[]{:S(2)}, u32[]{:S(2)}) collective-permute-start(f32[1,128]{1,0:T(1,128)S(1)} %add.75), channel_id=1, source_target_pairs={{0,2},{1,3},{2,4},{3,5},{4,6},{5,7},{6,0},{7,1},{8,10},{9,11},{10,... | collective-permute-start | bytes 1544 | tf_op jit(solution)/shard_map/ppermute | solution.py:349
  85.6 5.9 %collective-permute-start.4 = (f32[1,128]{1,0:T(1,128)S(1)}, f32[1,128]{1,0:T(1,128)S(1)}, u32[]{:S(2)}, u32[]{:S(2)}) collective-permute-start(f32[1,128]{1,0:T(1,128)S(1)} %add.75), channel_id=1, source_target_pairs={{0,4},{1,5},{2,6},{3,7},{4,0},{5,1},{6,2},{7,3},{8,12},{9,13},{10,... | collective-permute-start | bytes 1544 | tf_op jit(solution)/shard_map/ppermute | solution.py:349
  91.5 4.2 %collective-permute-start.9 = (f32[1,128]{1,0:T(1,128)S(1)}, f32[1,128]{1,0:T(1,128)S(1)}, u32[]{:S(2)}, u32[]{:S(2)}) collective-permute-start(f32[1,128]{1,0:T(1,128)S(1)} %add_add_fusion.1), channel_id=1, source_target_pairs={{0,24},{1,25},{2,26},{3,27},{4,28},{5,29},{6,30},{7,31},{8,0},{9,1... | collective-permute-start | bytes 1544 | tf_op jit(solution)/shard_map/ppermute | solution.py:349
  93.5 4.8 %collective-permute-start.8 = (f32[1,128]{1,0:T(1,128)S(1)}, f32[1,128]{1,0:T(1,128)S(1)}, u32[]{:S(2)}, u32[]{:S(2)}) collective-permute-start(f32[1,128]{1,0:T(1,128)S(1)} %add_add_fusion.1), channel_id=1, source_target_pairs={{0,8},{1,9},{2,10},{3,11},{4,12},{5,13},{6,14},{7,15},{8,16},{9,17... | collective-permute-start | bytes 1544 | tf_op jit(solution)/shard_map/ppermute | solution.py:349
  93.6 5.0 %collective-permute-start.7 = (f32[1,128]{1,0:T(1,128)S(1)}, f32[1,128]{1,0:T(1,128)S(1)}, u32[]{:S(2)}, u32[]{:S(2)}) collective-permute-start(f32[1,128]{1,0:T(1,128)S(1)} %add_add_fusion.1), channel_id=1, source_target_pairs={{0,16},{1,17},{2,18},{3,19},{4,20},{5,21},{6,22},{7,23},{8,24},{9,... | collective-permute-start | bytes 1544 | tf_op jit(solution)/shard_map/ppermute | solution.py:349
